TPU v7x, 256 devices: a whole 4x4x8 slice. The times are simulated.
256 devices in a mesh: seg: 32 (over y, x, core), fft: 8 (over z).
Axes of the slice: x: 4, y: 4, z: 8, core: 2. Of those that a mesh axis runs over, the one named last changes fastest.
Arguments:
- voltage: float32 [32, 2, 256, 4096], P('seg', None, None, 'fft'), may hold values from -6 to 6
- chirp_phase: float32 [2, 512, 4096], P(None, 'fft'), may hold values from -3.140625 to 3.140625
Outputs:
- dedispersed: float32 [32, 2, 256, 4096], P('seg', None, None, 'fft')
All inputs are finite; a program needn't handle non-finite values.
Results may differ from a plain program's by a relative error of at most 0.0001.
Values sent between devices are 32-bit elements; how exact they have to be, the bound alone decides.
A program may use at most 128 MiB of HBM per device.

v0:
```python
import math

import jax
import jax.numpy as jnp
from jax import lax
from jax.experimental import pallas as pl
from jax.sharding import PartitionSpec as P

B1 = 64
TILE_ROWS = 8


HIGHEST = lax.Precision.HIGHEST
HIGH = lax.Precision.HIGH


def passed_along(shard, axis, by):
    length = lax.axis_size(axis)
    pairs = [(i, i + by) for i in range(length) if 0 <= i + by < length]
    return lax.ppermute(shard, axis, pairs)


def rotation(products, period):
    reduced = jnp.mod(products, period).astype(jnp.float32)
    angles = reduced * jnp.float32(-2.0 * math.pi / period)
    return jnp.stack([jnp.cos(angles), jnp.sin(angles)])


def conjugate(pair):
    return jnp.stack([pair[0], -pair[1]])


def real_table(pair):
    return jnp.stack([jnp.stack([pair[0], pair[1]]), jnp.stack([-pair[1], pair[0]])])


def complex_mul(left_pair, right_pair):
    first = left_pair[0] * right_pair[0] - left_pair[1] * right_pair[1]
    second = left_pair[0] * right_pair[1] + left_pair[1] * right_pair[0]
    return jnp.stack([first, second])


def fold_order(row_count, groups):
    half_count = row_count // (2 * groups)
    places = jnp.arange(row_count, dtype=jnp.int32)
    within = places % (2 * half_count)
    base_row = places // (2 * half_count) * half_count + within % half_count
    mirror_row = jnp.where(base_row > 0, row_count - base_row, row_count // 2)
    return jnp.where(within >= half_count, mirror_row, base_row)


def both_halves(outer, inner, period, reverse_outer, reverse_inner):
    last_outer = outer.shape[0] - 1
    last_inner = inner.shape[0] - 1
    natural = outer[:, None] * inner[None, :]
    outer_turned = (last_outer - outer) if reverse_outer else outer
    inner_turned = (last_inner - inner) if reverse_inner else inner
    turned = outer_turned[:, None] * inner_turned[None, :]
    return jnp.stack([rotation(natural, period), rotation(turned, period)], axis=1)


def reverse_lanes(values):
    width = values.shape[-1]
    tiles = values.reshape(values.shape[:-1] + (width // 128, 128))
    tiles = jnp.flip(tiles, axis=-2)
    lane = jnp.arange(128, dtype=jnp.int32)
    anti = (lane[:, None] + lane[None, :] == 127).astype(jnp.float32)
    flipped = jnp.einsum("...l,lm->...m", tiles, anti, precision=HIGHEST)
    return flipped.reshape(values.shape)


def partners(base, mirror, is_first):
    first_base = jnp.roll(reverse_lanes(base[:, 0]), 1, axis=-1)
    first_mirror = reverse_lanes(mirror[:, 0])
    of_base = mirror.at[:, 0].set(jnp.where(is_first, first_base, mirror[:, 0]))
    of_mirror = base.at[:, 0].set(jnp.where(is_first, first_mirror, base[:, 0]))
    return of_base, of_mirror


def post_process(spec, partner, turn):
    even = 0.5 * (spec + partner)
    odd = jnp.stack([0.5 * (spec[1] - partner[1]), -0.5 * (spec[0] - partner[0])])
    return even + complex_mul(odd, turn)


def pre_process(filtered, partner, turn):
    even_back = 0.5 * (filtered + partner)
    odd_back = complex_mul(0.5 * (filtered - partner), conjugate(turn))
    return jnp.stack([even_back[0] - odd_back[1], even_back[1] + odd_back[0]])


def middle_kernel(spec_ref, phase_ref, row_ref, column_ref, out_ref):
    turn_re = row_ref[0] * column_ref[0] - row_ref[1] * column_ref[1]
    turn_im = row_ref[0] * column_ref[1] + row_ref[1] * column_ref[0]
    filtered = []
    for half in (0, 1):
        other = 1 - half
        spec = jnp.stack([spec_ref[0, half], spec_ref[1, half]])
        partner = jnp.stack([spec_ref[0, other], -spec_ref[1, other]])
        turn = jnp.stack([turn_re[half], turn_im[half]])
        transformed = post_process(spec, partner, turn)
        phase = phase_ref[half]
        filtered.append(complex_mul(transformed, jnp.stack([jnp.cos(phase), jnp.sin(phase)])))
    for half in (0, 1):
        other = filtered[1 - half]
        turn = jnp.stack([turn_re[half], turn_im[half]])
        packed = pre_process(filtered[half], conjugate(other), turn)
        out_ref[0, half] = packed[0]
        out_ref[1, half] = packed[1]


def middle(spectrum, phase_rows, row_turn, column_turn):
    rows = spectrum.shape[2]
    columns = spectrum.shape[3]
    spec_block = pl.BlockSpec((2, 2, TILE_ROWS, columns), lambda i: (0, 0, i, 0))
    return pl.pallas_call(
        middle_kernel,
        out_shape=jax.ShapeDtypeStruct(spectrum.shape, jnp.float32),
        grid=(rows // TILE_ROWS,),
        in_specs=[
            spec_block,
            pl.BlockSpec((2, TILE_ROWS, columns), lambda i: (0, i, 0)),
            pl.BlockSpec((2, 2, TILE_ROWS, 1), lambda i: (0, 0, i, 0)),
            pl.BlockSpec((2, 2, 1, columns), lambda i: (0, 0, 0, 0)),
        ],
        out_specs=spec_block,
    )(spectrum, phase_rows, row_turn, column_turn)


def per_device(voltage, chirp_phase):
    groups = lax.axis_size("fft")
    device = lax.axis_index("fft")
    quarter = voltage.shape[2]
    row_count = 4 * quarter
    local_width = voltage.shape[3]
    columns = local_width * groups
    second_len = columns // B1
    total_bins = row_count * columns
    half_count = row_count // (2 * groups)
    local_rows = 2 * half_count
    is_first = device == 0
    row_order = fold_order(row_count, groups)
    local_order = lax.dynamic_slice_in_dim(row_order, device * local_rows, local_rows)
    first_range = jnp.arange(B1, dtype=jnp.int32)
    second_range = jnp.arange(second_len, dtype=jnp.int32)
    column_range = jnp.arange(columns, dtype=jnp.int32)
    sample_rows = jnp.arange(quarter, dtype=jnp.int32)
    entry_table = real_table(rotation(sample_rows[:, None] * row_order[None, :], row_count))
    spread = jnp.einsum("pmb,pqmr->qrb", voltage[0], entry_table, precision=HIGH)
    spread = spread.reshape(2, row_count, B1 // groups, second_len)
    device_turn = rotation(row_order * (device * local_width), total_bins)
    block_range = jnp.arange(B1 // groups, dtype=jnp.int32)
    within_turn = rotation(row_order[:, None] * (second_len * block_range)[None, :], total_bins)
    inner_turn = rotation(row_order[:, None] * second_range[None, :], total_bins)
    outer_turn = complex_mul(device_turn[:, :, None], within_turn)
    spread = complex_mul(complex_mul(spread, outer_turn[..., None]), inner_turn[:, :, None, :])
    gathered = lax.all_to_all(spread, "fft", split_axis=1, concat_axis=2, tiled=True)
    gathered = gathered.reshape(2, 2, half_count, B1, second_len)
    section_one = both_halves(first_range, first_range, B1, False, True)
    block_turn = both_halves(first_range, second_range, columns, True, False)
    section_two = both_halves(second_range, second_range, second_len, False, True)
    gathered = jnp.einsum("phrun,pqhuk->qhrkn", gathered, real_table(section_one), precision=HIGH)
    gathered = complex_mul(gathered, block_turn[:, :, None])
    spectrum = jnp.einsum("phrkn,pqhnj->qhrjk", gathered, real_table(section_two), precision=HIGH)
    spectrum = spectrum.reshape(2, 2, half_count, columns)
    half_rows = jnp.stack([local_order[:half_count], local_order[half_count:]])
    row_turn = rotation(half_rows, 2 * total_bins)[..., None]
    stored_columns = jnp.stack([column_range, columns - 1 - column_range])
    column_turn = rotation(stored_columns, 2 * columns)[:, :, None, :]
    phase_rows = jnp.stack([chirp_phase[0], reverse_lanes(chirp_phase[1])])
    packed = middle(spectrum, phase_rows, row_turn, column_turn)
    first_spec = spectrum[:, :, 0]
    first_turn = complex_mul(row_turn[:, :, 0], column_turn[:, :, 0])
    live = jnp.stack([column_range > 0, column_range >= 0])
    first_partner = jnp.stack(
        [jnp.roll(reverse_lanes(first_spec[:, 0]), 1, axis=-1), reverse_lanes(first_spec[:, 1])], axis=1
    )
    first_filtered = complex_mul(
        post_process(first_spec, conjugate(first_partner), first_turn),
        jnp.stack([jnp.cos(phase_rows[:, 0]), jnp.sin(phase_rows[:, 0])]),
    )
    first_filtered = jnp.where(live[None], first_filtered, 0.0)
    first_partner = jnp.stack(
        [jnp.roll(reverse_lanes(first_filtered[:, 0]), 1, axis=-1), reverse_lanes(first_filtered[:, 1])],
        axis=1,
    )
    first_packed = pre_process(first_filtered, conjugate(first_partner), first_turn)
    packed = packed.at[:, :, 0].set(jnp.where(is_first, first_packed, packed[:, :, 0]))
    packed = packed.reshape(2, 2, half_count, second_len, B1)
    back_two = both_halves(second_range, second_range, second_len, True, False)
    back_turn = both_halves(first_range, second_range, columns, True, False)
    back_one = both_halves(first_range, first_range, B1, True, False)
    packed = jnp.einsum(
        "phrjk,pqhjv->qhrkv", packed, real_table(conjugate(back_two)), precision=HIGH
    )
    packed = complex_mul(packed, conjugate(back_turn)[:, :, None])
    packed = jnp.einsum(
        "phrkv,pqhku->qhruv", packed, real_table(conjugate(back_one)), precision=HIGH
    )
    packed = packed.reshape(2, local_rows, B1, second_len)
    upper_turn = rotation(local_order[:, None] * (second_len * first_range)[None, :], total_bins)
    lower_turn = rotation(local_order[:, None] * second_range[None, :], total_bins)
    packed = complex_mul(
        complex_mul(packed, conjugate(upper_turn)[..., None]), conjugate(lower_turn)[:, :, None, :]
    )
    packed = packed.reshape(2, local_rows, groups, local_width)
    arrived = lax.all_to_all(packed, "fft", split_axis=2, concat_axis=1, tiled=True)
    arrived = arrived.reshape(2, row_count, local_width)
    exit_turn = rotation(
        row_order[:, None] * jnp.arange(row_count, dtype=jnp.int32)[None, :], row_count
    )
    exit_table = real_table(jnp.stack([exit_turn[0] / total_bins, -exit_turn[1] / total_bins]))

    def sample_block(block_id):
        lower = block_id * quarter
        table = exit_table[:, :, :, lower : lower + quarter]
        return jnp.einsum("prn,pqrm->qmn", arrived, table, precision=HIGH)

    running = sample_block(3)
    for block_id in (2, 1, 0):
        running = sample_block(block_id) + passed_along(running, "seg", 1)
    return running[None]


def solution(mesh):
    in_specs = (P("seg", None, None, "fft"), P(None, "fft", None))
    out_specs = P("seg", None, None, "fft")
    return jax.shard_map(
        per_device, mesh=mesh, in_specs=in_specs, out_specs=out_specs, check_vma=False
    )
```

profile of v0, /device:TPU:16, one launch (start us, length us, event | category | flops | bytes accessed | tf_op | source)
XLA Modules:
  0.0 444.3 jit_solution(6310554099111862635)
XLA Ops:
  0.0 1.8 fusion.74
  1.8 5.3 %fusion.61 = (f32[1,256,1024]{2,1,0:T(8,128)S(1)}, f32[1,256,1024]{2,1,0:T(8,128)S(1)}, f32[1,256,1024]{2,1,0:T(8,128)}) fusion(s32[1024]{0:T(1024)S(1)} %select_select_fusion), kind=kLoop, calls=%fused_computation.86 | loop fusion | flops 3932160 | bytes 3149824 | tf_op jit(solution)/shard_map/sin | solution.py:26
  7.1 2.1 maximum_bitcast_fusion.4
  9.2 3.7 fusion.36
  13.0 0.6 fusion.209
  13.9 0.9 multiply_subtract_fusion.4
  14.8 2.5 pad_maximum_fusion.2
  17.3 8.1 %copy.91 = f32[2,1024,8,64]{3,2,0,1:T(8,128)} copy(f32[2,1024,8,64]{1,3,2,0:T(8,128)} %pad_maximum_fusion.2) | data formatting | bytes 8388608 | tf_op jit(solution)/shard_map/stack | solution.py:40
  25.4 9.8 %reshape.2085 = f32[8,1,131072]{2,1,0:T(1,128)} reshape(f32[1024,2,8,64]{3,2,1,0:T(8,128)} %bitcast.240) | data formatting | bytes 8388608
  35.3 9.1 %all-to-all-start = ((f32[8,1,131072]{2,1,0:T(1,128)}), f32[8,1,131072]{2,1,0:T(1,128)}, u32[]{:S(2)}, u32[]{:S(2)}) async-start(f32[8,1,131072]{2,1,0:T(1,128)} %reshape.2085), calls=%async_computation | async-start | bytes 8388608 | tf_op jit(solution)/shard_map/all_to_all | solution.py:157
  44.7 0.5 fusion.203
  45.7 0.7 broadcast_in_dim.20.column_ref
  46.4 0.8 copy.102.row_ref
  48.2 1.1 copy.99
  49.5 1.2 convolution_bitcast_fusion.1
  50.7 0.6 copy.98
  51.3 2.1 pad_maximum_fusion.4
  53.4 2.5 copy.101.phase_ref
  56.7 0.5 fusion.201
  57.2 83.6 %all-to-all-done = f32[8,1,131072]{2,1,0:T(1,128)} async-done(((f32[8,1,131072]{2,1,0:T(1,128)}), f32[8,1,131072]{2,1,0:T(1,128)}, u32[]{:S(2)}, u32[]{:S(2)}) %all-to-all-start) | async-done | bytes 4194336 | tf_op jit(solution)/shard_map/all_to_all | solution.py:157
  140.7 0.5 broadcast.2179
  141.3 13.9 %reduce.6 = f32[8,131072]{1,0:T(8,128)} reduce(f32[8,1,131072]{2,1,0:T(1,128)} %all-to-all-done, f32[]{:T(128)} %broadcast.2179), dimensions={1}, to_apply=%all_to_all.22.reduce_sub_computation | reduce | bytes 8388612 | tf_op jit(solution)/shard_map/all_to_all | solution.py:157
  155.2 8.7 %reshape.2086 = f32[1024,2,8,64]{3,2,1,0:T(8,128)} reshape(f32[8,131072]{1,0:T(8,128)} %reduce.6) | data formatting | bytes 8388608
  163.9 4.6 %copy.92 = f32[2,8,128,8,64]{4,3,1,0,2:T(8,128)S(1)} copy(f32[2,8,128,8,64]{4,3,0,2,1:T(8,128)} %bitcast.241) | data formatting | bytes 8388608 | tf_op jit(solution)/shard_map/all_to_all | solution.py:157
  168.5 4.5 %convolution_bitcast_fusion = f32[2,2,64,64,64]{4,3,2,0,1:T(8,128)S(1)} fusion(f32[2,2,64,64,64,1]{4,3,0,2,5,1:T(8,128)S(1)} %bitcast.242, f32[1,2,2,64,64]{3,4,0,1,2:T(8,128)S(1)} %maximum_bitcast_fusion.12, f32[1,2,2,64,64]{3,4,0,1,2:T(8,128)S(1)} %fusion.72), kind=kOutput, calls=%fused_computation.49 | convolution fusion | flops 805339136 | bytes 8519680 | tf_op jit(solution)/shard_map/phrun,pqhuk->qhrkn/dot_general | solution.py:162
  173.0 2.0 multiply_subtract_fusion.1
  175.0 8.2 %fusion.27 = f32[2,2,64,64,64]{4,3,2,0,1:T(8,128)} fusion(f32[1,2,2,64,64]{3,4,0,1,2:T(8,128)S(1)} %maximum_bitcast_fusion.12, f32[1,2,2,64,64]{3,4,0,1,2:T(8,128)S(1)} %fusion.72, f32[1,2,64,64,64]{4,3,2,0,1:T(8,128)S(1)} %get-tuple-element.36, f32[1,2,64,64,64]{4,3,2,0,1:T(8,128)S(1)} %get-tuple-element.35), kind=kOutput, calls=%fused_computation.46 | convolution fusion | flops 806387712 | bytes 8519680 | tf_op jit(solution)/shard_map/phrkn,pqhnj->qhrjk/dot_general | solution.py:164
  183.3 8.1 %reshape.2082 = f32[2,2,64,4096]{3,2,0,1:T(8,128)} reshape(f32[2,2,64,64,64]{4,3,2,0,1:T(8,128)} %fusion.27) | data formatting | bytes 8388608 | tf_op jit(solution)/shard_map/reshape | solution.py:165
  191.4 1.1 slice.308
  192.5 1.1 fusion.208
  193.6 4.6 %copy.100.spec_ref = f32[2,2,64,4096]{3,2,1,0:T(8,128)} copy(f32[2,2,64,4096]{3,2,0,1:T(8,128)} %reshape.2082) | data formatting | bytes 8388608 | tf_op jit(solution)/shard_map/reshape | solution.py:165
  199.3 0.5 fusion.125
  200.5 15.5 %shard_map.28 = f32[2,2,64,4096]{3,2,1,0:T(8,128)} custom-call(f32[2,2,64,4096]{3,2,1,0:T(8,128)} %copy.100.spec_ref, f32[2,64,4096]{2,1,0:T(8,128)} %copy.101.phase_ref, f32[2,2,64,1]{3,2,1,0:T(8,128)} %copy.102.row_ref, f32[2,2,1,4096]{3,2,1,0:T(1,128)} %broadcast_in_dim.20.column_ref), custom_call_target="tpu_custom_call" | custom-call | tf_op jit(solution)/shard_map/pallas_call | solution.py:116
  216.0 1.1 slice.333
  217.6 1.9 scatter.4
  219.5 7.9 %reshape.2061 = f32[2,2,64,64,64]{4,3,2,1,0:T(8,128)} reshape(f32[2,2,64,4096]{3,2,1,0:T(8,128)} %scatter.4) | data formatting | bytes 8388608 | tf_op jit(solution)/shard_map/reshape | solution.py:189
  227.4 9.9 %fusion.30 = f32[2,2,64,64,64]{4,3,2,0,1:T(8,128)S(1)} fusion(f32[2,2,64,64,64]{4,3,2,1,0:T(8,128)} %reshape.2061, f32[1,2,2,64,64]{3,4,1,2,0:T(8,128)S(1)} %get-tuple-element.64, f32[1,2,2,64,64]{3,4,1,2,0:T(8,128)S(1)} %get-tuple-element.63), kind=kOutput, calls=%fused_computation.47 | convolution fusion | flops 805339136 | bytes 8519680 | tf_op jit(solution)/shard_map/phrjk,pqhjv->qhrkv/dot_general | solution.py:193
  237.3 2.0 multiply_subtract_fusion
  239.3 4.1 fusion.33
  243.4 4.2 fusion.207
  247.6 4.8 %squeeze.22 = f32[1,128,8,512]{3,2,1,0:T(8,128)} reshape(f32[1,2,64,64,64]{4,3,2,0,1:T(8,128)} %get-tuple-element.37) | data formatting | bytes 4194304 | tf_op jit(solution)/shard_map/squeeze | solution.py:38
  252.3 2.0 copy.111
  254.3 4.8 %squeeze.23 = f32[1,128,8,512]{3,2,1,0:T(8,128)} reshape(f32[1,2,64,64,64]{4,3,2,0,1:T(8,128)} %get-tuple-element.38) | data formatting | bytes 4194304 | tf_op jit(solution)/shard_map/squeeze | solution.py:38
  259.1 3.0 copy.112
  262.9 0.8 copy-done.4
  263.7 2.3 multiply_subtract_fusion.2
  266.3 1.2 copy-done.5
  267.8 2.3 copy.115
  270.1 4.7 %all-to-all-start.1 = ((f32[2,128,8,512]{1,3,0,2:T(8,128)}), f32[2,128,8,512]{1,3,0,2:T(8,128)}, u32[]{:S(2)}, u32[]{:S(2)}) async-start(f32[2,128,8,512]{1,3,0,2:T(8,128)} %copy.115), calls=%async_computation.1 | async-start | bytes 8388608 | tf_op jit(solution)/shard_map/all_to_all | solution.py:207
  274.9 16.8 %fusion.39 = (f32[1,1024,1024]{1,2,0:T(8,128)S(1)}, f32[1,1024,1024]{1,2,0:T(8,128)S(1)}, f32[1,1024,1024]{1,2,0:T(8,128)S(1)}) fusion(s32[1024]{0:T(1024)S(1)} %select_select_fusion), kind=kLoop, calls=%fused_computation.64 | loop fusion | flops 18874368 | bytes 12587008 | tf_op jit(solution)/shard_map/neg | solution.py:34
  291.6 6.7 %maximum_bitcast_fusion.1 = (f32[1,2,1024,1024]{2,3,0,1:T(8,128)}, f32[1,2,1024,1024]{2,3,0,1:T(8,128)}) fusion(f32[1,1024,1024]{1,2,0:T(8,128)S(1)} %get-tuple-element.77, f32[1,1024,1024]{1,2,0:T(8,128)S(1)} %get-tuple-element.75, f32[1,1024,1024]{1,2,0:T(8,128)S(1)} %get-tuple-element.76), kind=kLoop, calls=%fused_computation.7 | loop fusion | flops 4194304 | bytes 29360128 | tf_op jit(solution)/shard_map/stack | solution.py:34
  298.4 73.2 %all-to-all-done.1 = f32[2,128,8,512]{1,3,0,2:T(8,128)} async-done(((f32[2,128,8,512]{1,3,0,2:T(8,128)}), f32[2,128,8,512]{1,3,0,2:T(8,128)}, u32[]{:S(2)}, u32[]{:S(2)}) %all-to-all-start.1) | async-done | bytes 4194336 | tf_op jit(solution)/shard_map/all_to_all | solution.py:207
  371.6 5.4 %copy.116 = f32[2,8,128,1,512]{4,2,1,0,3:T(8,128)} copy(f32[2,8,128,1,512]{2,4,0,1,3:T(8,128)} %bitcast.78) | data formatting | bytes 8388608 | tf_op jit(solution)/shard_map/all_to_all | solution.py:207
  377.0 7.2 %fusion.40 = f32[2,256,512]{2,1,0:T(8,128)S(1)} fusion(f32[2,1024,512,1]{2,1,0,3:T(8,128)} %bitcast.236, f32[1,2,1024,1024]{2,3,0,1:T(8,128)} %get-tuple-element.41, f32[1,2,1024,1024]{2,3,0,1:T(8,128)} %get-tuple-element.42), kind=kOutput, calls=%fused_computation.68 | convolution fusion | flops 3222274048 | bytes 22020096 | tf_op jit(solution)/shard_map/prn,pqrm->qmn/dot_general | solution.py:217
  384.2 2.4 collective-permute-start
  386.6 16.1 %collective-permute-done = f32[2,256,512]{2,1,0:T(8,128)S(1)} collective-permute-done((f32[2,256,512]{2,1,0:T(8,128)S(1)}, f32[2,256,512]{2,1,0:T(8,128)S(1)}, u32[]{:S(2)}, u32[]{:S(2)}) %collective-permute-start) | collective-permute-done | bytes 1048608 | tf_op jit(solution)/shard_map/ppermute | solution.py:20
  402.7 3.5 fusion.50
  406.2 1.9 collective-permute-start.1
  408.2 3.5 fusion.41
  411.7 12.7 %collective-permute-done.1 = f32[2,256,512]{2,1,0:T(8,128)S(1)} collective-permute-done((f32[2,256,512]{2,1,0:T(8,128)S(1)}, f32[2,256,512]{2,1,0:T(8,128)S(1)}, u32[]{:S(2)}, u32[]{:S(2)}) %collective-permute-start.1) | collective-permute-done | bytes 1048608 | tf_op jit(solution)/shard_map/ppermute | solution.py:20
  424.7 1.9 collective-permute-start.2
  426.6 3.5 fusion.44
  430.2 12.7 %collective-permute-done.2 = f32[2,256,512]{2,1,0:T(8,128)S(1)} collective-permute-done((f32[2,256,512]{2,1,0:T(8,128)S(1)}, f32[2,256,512]{2,1,0:T(8,128)S(1)}, u32[]{:S(2)}, u32[]{:S(2)}) %collective-permute-start.2) | collective-permute-done | bytes 1048608 | tf_op jit(solution)/shard_map/ppermute | solution.py:20
  442.9 1.2 add_bitcast_fusion
  (90 shorter events, 6.9 us)
Async XLA Ops:
  0.0 9.2 %copy-start = (f32[1,2,256,512]{3,2,1,0:T(8,128)S(1)}, f32[1,2,256,512]{3,2,1,0:T(8,128)}, u32[]{:S(2)}) copy-start(f32[1,2,256,512]{3,2,1,0:T(8,128)} %param.4) | copy-start | bytes 3145732
  12.9 1.0 copy-start.7
  35.3 12.7 %copy-start.6 = (f32[2,64,4096]{2,1,0:T(8,128)S(1)}, f32[2,64,4096]{2,1,0:T(8,128)}, u32[]{:S(2)}) copy-start(f32[2,64,4096]{2,1,0:T(8,128)} %param.5) | copy-start | bytes 6291460
  35.3 105.4 %all-to-all-start = ((f32[8,1,131072]{2,1,0:T(1,128)}), f32[8,1,131072]{2,1,0:T(1,128)}, u32[]{:S(2)}, u32[]{:S(2)}) async-start(f32[8,1,131072]{2,1,0:T(1,128)} %reshape.2085), calls=%async_computation | async-start | bytes 8388608 | tf_op jit(solution)/shard_map/all_to_all | solution.py:157
  262.1 1.6 copy-start.4
  265.9 1.6 copy-start.5
  270.1 101.5 %all-to-all-start.1 = ((f32[2,128,8,512]{1,3,0,2:T(8,128)}), f32[2,128,8,512]{1,3,0,2:T(8,128)}, u32[]{:S(2)}, u32[]{:S(2)}) async-start(f32[2,128,8,512]{1,3,0,2:T(8,128)} %copy.115), calls=%async_computation.1 | async-start | bytes 8388608 | tf_op jit(solution)/shard_map/all_to_all | solution.py:207
  377.0 25.7 %slice-start = ((s8[8388608]{0:T(1024)(128)(4,1)}), s8[4194304]{0:T(1024)(128)(4,1)S(1)}, s32[]{:S(2)}) async-start(s8[8388608]{0:T(1024)(128)(4,1)} %bitcast.234), calls=%async_computation.2 | async-start | bytes 8388608
  377.0 25.7 %slice-start.1 = ((s8[8388608]{0:T(1024)(128)(4,1)}), s8[4194304]{0:T(1024)(128)(4,1)S(1)}, s32[]{:S(2)}) async-start(s8[8388608]{0:T(1024)(128)(4,1)} %bitcast.234), calls=%async_computation.3 | async-start | bytes 8388608
  377.0 25.7 %copy-start.2 = (f32[1,2,1024,1024]{2,3,0,1:T(8,128)S(1)}, f32[1,2,1024,1024]{2,3,0,1:T(8,128)}, u32[]{:S(2)}) copy-start(f32[1,2,1024,1024]{2,3,0,1:T(8,128)} %get-tuple-element.42) | copy-start | bytes 25165828
  377.0 25.7 %copy-start.3 = (f32[2,8,128,1,512]{4,2,1,0,3:T(8,128)S(1)}, f32[2,8,128,1,512]{4,2,1,0,3:T(8,128)}, u32[]{:S(2)}) copy-start(f32[2,8,128,1,512]{4,2,1,0,3:T(8,128)} %copy.116) | copy-start | bytes 12582916
  384.2 18.5 %collective-permute-start = (f32[2,256,512]{2,1,0:T(8,128)S(1)}, f32[2,256,512]{2,1,0:T(8,128)S(1)}, u32[]{:S(2)}, u32[]{:S(2)}) collective-permute-start(f32[2,256,512]{2,1,0:T(8,128)S(1)} %fusion.40), channel_id=1, source_target_pairs={{0,8},{8,16},{16,24},{24,32},{32,40},{40,48},{48,56},{56,64},{64,7... | collective-permute-start | bytes 3145736 | tf_op jit(solution)/shard_map/ppermute | solution.py:20
  406.2 18.2 %collective-permute-start.1 = (f32[2,256,512]{2,1,0:T(8,128)S(1)}, f32[2,256,512]{2,1,0:T(8,128)S(1)}, u32[]{:S(2)}, u32[]{:S(2)}) collective-permute-start(f32[2,256,512]{2,1,0:T(8,128)S(1)} %fusion.50), channel_id=1, source_target_pairs={{0,8},{8,16},{16,24},{24,32},{32,40},{40,48},{48,56},{56,64},{64,7... | collective-permute-start | bytes 3145736 | tf_op jit(solution)/shard_map/ppermute | solution.py:20
  424.7 18.2 %collective-permute-start.2 = (f32[2,256,512]{2,1,0:T(8,128)S(1)}, f32[2,256,512]{2,1,0:T(8,128)S(1)}, u32[]{:S(2)}, u32[]{:S(2)}) collective-permute-start(f32[2,256,512]{2,1,0:T(8,128)S(1)} %add.670), channel_id=1, source_target_pairs={{0,8},{8,16},{16,24},{24,32},{32,40},{40,48},{48,56},{56,64},{64,7... | collective-permute-start | bytes 3145736 | tf_op jit(solution)/shard_map/ppermute | solution.py:20
  426.6 17.5 %copy-start.1 = (f32[1,2,256,512]{3,2,1,0:T(8,128)S(1)}, f32[1,2,256,512]{3,2,1,0:T(8,128)}, u32[]{:S(2)}) copy-start(f32[1,2,256,512]{3,2,1,0:T(8,128)} %param.4) | copy-start | bytes 3145732
where the time goes:
time: 452 us; the launch traced here: 444 us
  waiting for transfers between devices  198 us (44%)
  local copies, waits for them, and re-layouts  95 us (21%)
  other arithmetic  64.4 us (14%)
  matrix products  50.1 us (11%)
  starting transfers between devices  20.1 us (4%)
  Pallas kernels  15.5 us (3%)
    all_to_all x1, waiting for transfers between devices, per_device(): lax.all_to_all(spread, 'fft', split_axis=1, concat_axis=2, tiled=True)  83.6 us
    all_to_all x1, waiting for transfers between devices, per_device(): lax.all_to_all(packed, 'fft', split_axis=2, concat_axis=1, tiled=True)  73.2 us
    ppermute x3, waiting for transfers between devices, passed_along(): return lax.ppermute(shard, axis, pairs)  41.6 us
    unnamed x26, local copies, waits for them, and re-layouts  21 us
    dot_general x4, matrix products, sample_block(): return jnp.einsum('prn,pqrm->qmn', arrived, table, precision=HIGH)  17.8 us
    neg x1, other arithmetic, real_table(): -pair[1]  16.8 us
    pallas_call x1, Pallas kernels, middle(): pl.pallas_call(middle_kernel, out_shape=jax.ShapeDtypeStruct(spectrum.sha...  15.5 us
    squeeze x4, local copies, waits for them, and re-layouts, complex_mul(): first = left_pair[0] * right_pair[0] - left_pair[1] * right_pair[1]  14.5 us
  transfers between devices with their start and end apart: 5, of which 5 were waited for; matrix products, arithmetic and copies ran while one was open for 10% of the time, Pallas kernels for 0%

commit v1 on v0

--- a/solution.py
+++ b/solution.py
@@ -146,20 +146,27 @@
     column_range = jnp.arange(columns, dtype=jnp.int32)
     sample_rows = jnp.arange(quarter, dtype=jnp.int32)
     entry_table = real_table(rotation(sample_rows[:, None] * row_order[None, :], row_count))
-    spread = jnp.einsum("pmb,pqmr->qrb", voltage[0], entry_table, precision=HIGH)
-    spread = spread.reshape(2, row_count, B1 // groups, second_len)
+    samples_in = voltage[0].reshape(2, quarter, B1 // groups, second_len)
+    entry_blocks = entry_table.reshape(2, 2, quarter, groups, local_rows)
     device_turn = rotation(row_order * (device * local_width), total_bins)
     block_range = jnp.arange(B1 // groups, dtype=jnp.int32)
     within_turn = rotation(row_order[:, None] * (second_len * block_range)[None, :], total_bins)
     inner_turn = rotation(row_order[:, None] * second_range[None, :], total_bins)
     outer_turn = complex_mul(device_turn[:, :, None], within_turn)
-    spread = complex_mul(complex_mul(spread, outer_turn[..., None]), inner_turn[:, :, None, :])
-    gathered = lax.all_to_all(spread, "fft", split_axis=1, concat_axis=2, tiled=True)
-    gathered = gathered.reshape(2, 2, half_count, B1, second_len)
+    turn = complex_mul(outer_turn[..., None], inner_turn[:, :, None, :])
+    turn = turn.reshape(2, groups, local_rows, B1 // groups, second_len)
+    spread = jnp.einsum("pmun,pqmdr->dqrun", samples_in, entry_blocks, precision=HIGH)
+    spread = jnp.stack([
+        spread[:, 0] * turn[0] - spread[:, 1] * turn[1],
+        spread[:, 0] * turn[1] + spread[:, 1] * turn[0],
+    ], axis=1)
+    gathered = lax.all_to_all(spread, "fft", split_axis=0, concat_axis=0, tiled=True)
+    gathered = gathered.reshape(groups, 2, 2, half_count, B1 // groups, second_len)
     section_one = both_halves(first_range, first_range, B1, False, True)
     block_turn = both_halves(first_range, second_range, columns, True, False)
     section_two = both_halves(second_range, second_range, second_len, False, True)
-    gathered = jnp.einsum("phrun,pqhuk->qhrkn", gathered, real_table(section_one), precision=HIGH)
+    first_blocks = real_table(section_one).reshape(2, 2, 2, groups, B1 // groups, B1)
+    gathered = jnp.einsum("sphrun,pqhsuk->qhrkn", gathered, first_blocks, precision=HIGH)
     gathered = complex_mul(gathered, block_turn[:, :, None])
     spectrum = jnp.einsum("phrkn,pqhnj->qhrjk", gathered, real_table(section_two), precision=HIGH)
     spectrum = spectrum.reshape(2, 2, half_count, columns)
@@ -204,8 +211,8 @@
         complex_mul(packed, conjugate(upper_turn)[..., None]), conjugate(lower_turn)[:, :, None, :]
     )
     packed = packed.reshape(2, local_rows, groups, local_width)
-    arrived = lax.all_to_all(packed, "fft", split_axis=2, concat_axis=1, tiled=True)
-    arrived = arrived.reshape(2, row_count, local_width)
+    packed = jnp.transpose(packed, (2, 0, 1, 3))
+    arrived = lax.all_to_all(packed, "fft", split_axis=0, concat_axis=0, tiled=True)
     exit_turn = rotation(
         row_order[:, None] * jnp.arange(row_count, dtype=jnp.int32)[None, :], row_count
     )
@@ -214,7 +221,8 @@
     def sample_block(block_id):
         lower = block_id * quarter
         table = exit_table[:, :, :, lower : lower + quarter]
-        return jnp.einsum("prn,pqrm->qmn", arrived, table, precision=HIGH)
+        table = table.reshape(2, 2, groups, local_rows, quarter)
+        return jnp.einsum("sprn,pqsrm->qmn", arrived, table, precision=HIGH)
 
     running = sample_block(3)
     for block_id in (2, 1, 0):

time: 452 us -> 425 us (0.940)
  matrix products: 50.1 us -> 73 us
  local copies, waits for them, and re-layouts: 95 us -> 73.2 us
  waiting for transfers between devices: 198 us -> 179 us
  other arithmetic: 64.4 us -> 56.4 us
    dot_general x6, matrix products: 26 us -> 49.2 us  [the longest x4 36.7 us: sample_block(): return jnp.einsum('sprn,pqsrm->qmn', arrived, table, precision=HIGH)]
    unnamed x26 -> x19, local copies, waits for them, and re-layouts: 21 us -> 3.62 us
    all_to_all x1 -> x0, other arithmetic: 13.9 us -> none  [per_device(): lax.all_to_all(spread, 'fft', split_axis=1, concat_axis=2, tiled=True)]
    ppermute x3, waiting for transfers between devices: 41.6 us -> 31.3 us  [passed_along(): return lax.ppermute(shard, axis, pairs)]
    all_to_all x2, waiting for transfers between devices: 157 us -> 148 us  [the longest x1 83.1 us: per_device(): lax.all_to_all(spread, 'fft', split_axis=0, concat_axis=0, tiled=True)]
    another operation x2, local copies, waits for them, and re-layouts: 10.5 us -> 2.38 us  [the longest x1 2.28 us: per_device(): jnp.stack([spread[:, 0] * turn[0] - spread[:, 1] * turn[1], spread[:, 0]...]
    transpose x0 -> x1, local copies, waits for them, and re-layouts: none -> 5.43 us  [per_device(): packed = jnp.transpose(packed, (2, 0, 1, 3))]
    all_to_all x3 -> x1, local copies, waits for them, and re-layouts: 10.5 us -> 9.22 us  [per_device(): lax.all_to_all(spread, 'fft', split_axis=0, concat_axis=0, tiled=True)]
  transfers between devices with their start and end apart: 5 -> 5, of which waited for: 5 -> 5; matrix products, arithmetic and copies ran while one was open for 10% -> 15% of each run, Pallas kernels for 0% -> 0%
where the time goes in v1:
time: 425 us; the launch traced here: 418 us
  waiting for transfers between devices  179 us (42%)
  local copies, waits for them, and re-layouts  73.2 us (17%)
  matrix products  73 us (17%)
  other arithmetic  56.4 us (13%)
  starting transfers between devices  19.2 us (5%)
  Pallas kernels  15.5 us (4%)
    all_to_all x1, waiting for transfers between devices, per_device(): lax.all_to_all(spread, 'fft', split_axis=0, concat_axis=0, tiled=True)  83.1 us
    all_to_all x1, waiting for transfers between devices, per_device(): lax.all_to_all(packed, 'fft', split_axis=0, concat_axis=0, tiled=True)  64.9 us
    dot_general x4, matrix products, sample_block(): return jnp.einsum('sprn,pqsrm->qmn', arrived, table, precision=HIGH)  36.7 us
    ppermute x3, waiting for transfers between devices, passed_along(): return lax.ppermute(shard, axis, pairs)  31.3 us
    neg x1, other arithmetic, real_table(): -pair[1]  19.2 us
    pallas_call x1, Pallas kernels, middle(): pl.pallas_call(middle_kernel, out_shape=jax.ShapeDtypeStruct(spectrum.sha...  15.5 us
    squeeze x4, local copies, waits for them, and re-layouts, complex_mul(): first = left_pair[0] * right_pair[0] - left_pair[1] * right_pair[1]  14.7 us
    another operation x5, other arithmetic, real_table(): jnp.stack([jnp.stack([pair[0], pair[1]]), jnp.stack([-pair[1], pair[0]])])  12.6 us
  transfers between devices with their start and end apart: 5, of which 5 were waited for; matrix products, arithmetic and copies ran while one was open for 15% of the time, Pallas kernels for 0%

profile of v1, /device:TPU:16, one launch (start us, length us, event | category | flops | bytes accessed | tf_op | source)
XLA Modules:
  0.0 417.8 jit_solution(5178224550777639411)
XLA Ops:
  0.0 1.0 fusion.90
  1.1 5.0 %fusion.67 = (f32[1,1,256,8,128]{4,2,0,3,1:T(8,128)S(1)}, f32[1,1,256,8,128]{4,2,0,3,1:T(8,128)}, f32[1,1,256,8,128]{4,2,0,3,1:T(8,128)}) fusion(s32[8,128]{1,0:T(8,128)S(1)} %select_select_fusion), kind=kLoop, calls=%fused_computation.91 | loop fusion | flops 3932160 | bytes 3149824 | tf_op jit(solution)/shard_map/sin | solution.py:26
  6.2 1.3 copy.69
  7.7 5.7 %fusion.41 = f32[8,2,128,8,64]{2,4,3,0,1:T(8,128)S(1)} fusion(f32[2,256,8,64,1,1]{1,3,2,0,5,4:T(8,128)} %bitcast.271, f32[1,1,256,8,128]{4,2,0,3,1:T(8,128)} %get-tuple-element.87, f32[1,1,256,8,128]{4,2,0,3,1:T(8,128)} %get-tuple-element.86, f32[1,1,256,8,128]{4,2,0,3,1:T(8,128)S(1)} %get-tuple-element.85), kind=kOutput, calls=%fused_computation.58 | convolution fusion | flops 3224371200 | bytes 8388608 | tf_op jit(solution)/shard_map/pmun,pqmdr->dqrun/dot_general | solution.py:158
  13.4 1.1 multiply_subtract_fusion.4
  14.6 0.6 pad_maximum_fusion.1
  15.2 2.3 copy.71
  17.5 8.9 %all-to-all-start = ((f32[8,2,128,8,64]{2,4,3,1,0:T(8,128)}), f32[8,2,128,8,64]{2,4,3,1,0:T(8,128)}, u32[]{:S(2)}, u32[]{:S(2)}) async-start(f32[8,2,128,8,64]{2,4,3,1,0:T(8,128)} %copy.71), calls=%async_computation | async-start | bytes 8388608 | tf_op jit(solution)/shard_map/all_to_all | solution.py:163
  26.7 0.5 fusion.238
  27.2 0.4 sin.204
  27.6 0.7 broadcast_in_dim.23.column_ref
  28.3 0.8 copy.82.row_ref
  29.3 0.4 fusion.195
  30.5 1.1 copy.79
  31.8 1.2 convolution_bitcast_fusion.1
  33.0 0.6 copy.78
  33.6 2.1 pad_maximum_fusion.2
  35.7 2.5 copy.81.phase_ref
  38.8 0.3 fusion.183
  39.1 0.5 fusion.236
  39.6 83.1 %all-to-all-done = f32[8,2,128,8,64]{2,4,3,1,0:T(8,128)} async-done(((f32[8,2,128,8,64]{2,4,3,1,0:T(8,128)}), f32[8,2,128,8,64]{2,4,3,1,0:T(8,128)}, u32[]{:S(2)}, u32[]{:S(2)}) %all-to-all-start) | async-done | bytes 4194336 | tf_op jit(solution)/shard_map/all_to_all | solution.py:163
  122.7 9.2 %copy.72 = f32[8,2,128,8,64]{4,3,0,1,2:T(8,128)} copy(f32[8,2,128,8,64]{2,4,3,1,0:T(8,128)} %all-to-all-done) | data formatting | bytes 8388608 | tf_op jit(solution)/shard_map/all_to_all | solution.py:163
  131.9 6.8 %convolution_bitcast_fusion = f32[2,2,64,64,64]{4,3,2,0,1:T(8,128)S(1)} fusion(f32[8,2,2,64,8,64,1]{5,4,0,1,3,6,2:T(8,128)} %bitcast.257, f32[1,2,2,8,8,64]{5,4,3,0,1,2:T(8,128)S(1)} %bitcast.272, f32[1,1,1,8,8,64]{5,4,3,0,1,2:T(8,128)S(1)} %get-tuple-element.81, f32[1,1,1,8,8,64]{5,4,3,0,1,2:T(8,128)S(1)} %get-tuple-element.82, ...), kind=kOutput, calls=%fused_computation.57 | convolution fusion | flops 805437440 | bytes 8519680 | tf_op jit(solution)/shard_map/sphrun,pqhsuk->qhrkn/dot_general | solution.py:169
  138.7 2.0 multiply_subtract_fusion.1
  140.7 8.3 %fusion.32 = f32[2,2,64,64,64]{4,3,2,0,1:T(8,128)} fusion(f32[1,2,2,64,64]{3,4,0,1,2:T(8,128)S(1)} %get-tuple-element.61, f32[1,2,2,64,64]{3,4,0,1,2:T(8,128)S(1)} %fusion.88, f32[1,2,64,64,64]{4,3,2,0,1:T(8,128)S(1)} %get-tuple-element.40, f32[1,2,64,64,64]{4,3,2,0,1:T(8,128)S(1)} %get-tuple-element.39), kind=kOutput, calls=%fused_computation.54 | convolution fusion | flops 806387712 | bytes 8519680 | tf_op jit(solution)/shard_map/phrkn,pqhnj->qhrjk/dot_general | solution.py:171
  149.0 7.9 %reshape.2131 = f32[2,2,64,4096]{3,2,0,1:T(8,128)} reshape(f32[2,2,64,64,64]{4,3,2,0,1:T(8,128)} %fusion.32) | data formatting | bytes 8388608 | tf_op jit(solution)/shard_map/reshape | solution.py:172
  157.0 1.1 slice.312
  158.0 1.1 fusion.243
  159.1 4.6 %copy.80.spec_ref = f32[2,2,64,4096]{3,2,1,0:T(8,128)} copy(f32[2,2,64,4096]{3,2,0,1:T(8,128)} %reshape.2131) | data formatting | bytes 8388608 | tf_op jit(solution)/shard_map/reshape | solution.py:172
  164.8 0.5 fusion.147
  166.0 15.5 %shard_map.28 = f32[2,2,64,4096]{3,2,1,0:T(8,128)} custom-call(f32[2,2,64,4096]{3,2,1,0:T(8,128)} %copy.80.spec_ref, f32[2,64,4096]{2,1,0:T(8,128)} %copy.81.phase_ref, f32[2,2,64,1]{3,2,1,0:T(8,128)} %copy.82.row_ref, f32[2,2,1,4096]{3,2,1,0:T(1,128)} %broadcast_in_dim.23.column_ref), custom_call_target="tpu_custom_call" | custom-call | tf_op jit(solution)/shard_map/pallas_call | solution.py:116
  181.6 1.1 slice.337
  183.1 1.9 scatter.4
  185.0 7.9 %reshape.2103 = f32[2,2,64,64,64]{4,3,2,1,0:T(8,128)} reshape(f32[2,2,64,4096]{3,2,1,0:T(8,128)} %scatter.4) | data formatting | bytes 8388608 | tf_op jit(solution)/shard_map/reshape | solution.py:196
  192.9 9.6 %fusion.35 = f32[2,2,64,64,64]{4,3,2,0,1:T(8,128)S(1)} fusion(f32[2,2,64,64,64]{4,3,2,1,0:T(8,128)} %reshape.2103, f32[1,2,2,64,64]{3,4,1,2,0:T(8,128)S(1)} %get-tuple-element.66, f32[1,2,2,64,64]{3,4,1,2,0:T(8,128)S(1)} %get-tuple-element.65), kind=kOutput, calls=%fused_computation.55 | convolution fusion | flops 805339136 | bytes 8519680 | tf_op jit(solution)/shard_map/phrjk,pqhjv->qhrkv/dot_general | solution.py:200
  202.6 2.0 multiply_subtract_fusion
  204.6 4.1 fusion.38
  208.7 4.2 %fusion.242 = (f32[1,2,64,64,64]{4,3,2,0,1:T(8,128)}, f32[1,2,64,64,64]{4,3,2,0,1:T(8,128)}) fusion(f32[2,2,64,64,64]{4,3,2,0,1:T(8,128)S(1)} %fusion.38), kind=kLoop, calls=%fused_computation.388 | loop fusion | bytes 8388608 | tf_op jit(solution)/shard_map/slice | solution.py:38
  212.9 4.8 %squeeze.13 = f32[1,128,8,512]{3,2,1,0:T(8,128)} reshape(f32[1,2,64,64,64]{4,3,2,0,1:T(8,128)} %get-tuple-element.41) | data formatting | bytes 4194304 | tf_op jit(solution)/shard_map/squeeze | solution.py:38
  217.6 2.0 copy.91
  219.6 4.8 %squeeze.14 = f32[1,128,8,512]{3,2,1,0:T(8,128)} reshape(f32[1,2,64,64,64]{4,3,2,0,1:T(8,128)} %get-tuple-element.42) | data formatting | bytes 4194304 | tf_op jit(solution)/shard_map/squeeze | solution.py:38
  224.4 3.2 copy.92
  228.4 0.8 copy-done.3
  229.2 2.3 multiply_subtract_fusion.2
  231.5 0.4 multiply_add_fusion.2
  231.8 1.2 copy-done.4
  233.0 2.3 maximum_bitcast_fusion.4
  235.4 5.4 %copy.95 = f32[8,2,128,512]{3,2,1,0:T(8,128)} copy(f32[8,2,128,512]{2,3,0,1:T(8,128)} %maximum_bitcast_fusion.4) | data formatting | bytes 8388608 | tf_op jit(solution)/shard_map/transpose | solution.py:214
  240.8 4.6 %all-to-all-start.1 = ((f32[8,2,128,512]{3,2,1,0:T(8,128)}), f32[8,2,128,512]{3,2,1,0:T(8,128)}, u32[]{:S(2)}, u32[]{:S(2)}) async-start(f32[8,2,128,512]{3,2,1,0:T(8,128)} %copy.95), calls=%async_computation.1 | async-start | bytes 8388608 | tf_op jit(solution)/shard_map/all_to_all | solution.py:215
  245.4 19.2 %fusion.44 = (f32[1,1024,1024]{2,1,0:T(8,128)S(1)}, f32[1,1024,1024]{2,1,0:T(8,128)}, f32[1,1024,1024]{2,1,0:T(8,128)}) fusion(s32[1024]{0:T(1024)S(1)} %select_select_fusion.1), kind=kLoop, calls=%fused_computation.70 | loop fusion | flops 18874368 | bytes 12587008 | tf_op jit(solution)/shard_map/neg | solution.py:34
  264.6 5.7 %maximum_bitcast_fusion.1 = (f32[1,2,1024,1024]{3,2,1,0:T(8,128)S(1)}, f32[1,2,1024,1024]{3,2,1,0:T(8,128)S(1)}) fusion(f32[1,1024,1024]{2,1,0:T(8,128)} %get-tuple-element.90, f32[1,1024,1024]{2,1,0:T(8,128)S(1)} %get-tuple-element.88, f32[1,1024,1024]{2,1,0:T(8,128)} %get-tuple-element.89), kind=kLoop, calls=%fused_computation.7 | loop fusion | flops 4194304 | bytes 29360128 | tf_op jit(solution)/shard_map/stack | solution.py:34
  270.3 6.9 %fusion.9 = (f32[2,2,1024,256]{3,2,1,0:T(8,128)}, f32[2,2,1024,256]{3,2,1,0:T(8,128)}, f32[2,2,1024,256]{3,2,1,0:T(8,128)}, f32[2,2,1024,256]{3,2,1,0:T(8,128)}) fusion(f32[1,2,1024,1024]{3,2,1,0:T(8,128)S(1)} %get-tuple-element.48, f32[1,2,1024,1024]{3,2,1,0:T(8,128)S(1)} %get-tuple-element.47), kind=kLoop, calls=%fused_computation.22 | loop fusion | flops 4194304 | bytes 33554432 | tf_op jit(solution)/shard_map/stack | solution.py:34
  277.2 64.9 %all-to-all-done.1 = f32[8,2,128,512]{3,2,1,0:T(8,128)} async-done(((f32[8,2,128,512]{3,2,1,0:T(8,128)}), f32[8,2,128,512]{3,2,1,0:T(8,128)}, u32[]{:S(2)}, u32[]{:S(2)}) %all-to-all-start.1) | async-done | bytes 4194336 | tf_op jit(solution)/shard_map/all_to_all | solution.py:215
  342.1 10.1 %fusion.54 = f32[2,256,512]{2,1,0:T(8,128)S(1)} fusion(f32[2,2,8,128,256]{4,3,2,1,0:T(8,128)} %bitcast.265, f32[8,2,128,512]{3,2,1,0:T(8,128)} %all-to-all-done.1), kind=kOutput, calls=%fused_computation.77 | convolution fusion | flops 3221225472 | bytes 9437184 | tf_op jit(solution)/shard_map/sprn,pqsrm->qmn/dot_general | solution.py:225
  352.2 1.9 collective-permute-start
  354.1 16.3 %collective-permute-done = f32[2,256,512]{2,1,0:T(8,128)S(1)} collective-permute-done((f32[2,256,512]{2,1,0:T(8,128)S(1)}, f32[2,256,512]{2,1,0:T(8,128)S(1)}, u32[]{:S(2)}, u32[]{:S(2)}) %collective-permute-start) | collective-permute-done | bytes 1048608 | tf_op jit(solution)/shard_map/ppermute | solution.py:20
  370.4 9.1 %fusion.57 = f32[2,256,512]{2,1,0:T(8,128)S(1)} fusion(f32[2,256,512]{2,1,0:T(8,128)S(1)} %collective-permute-done, f32[2,2,8,128,256]{4,3,2,1,0:T(8,128)S(1)} %bitcast.264, f32[8,2,128,512]{3,2,1,0:T(8,128)} %all-to-all-done.1), kind=kOutput, calls=%fused_computation.79 | convolution fusion | flops 3221487616 | bytes 10485760 | tf_op jit(solution)/shard_map/sprn,pqsrm->qmn/dot_general | solution.py:225
  379.5 1.9 collective-permute-start.1
  381.5 8.8 %fusion.48 = f32[2,256,512]{2,1,0:T(8,128)S(1)} fusion(f32[2,2,8,128,256]{4,3,2,1,0:T(8,128)S(1)} %bitcast.263, f32[8,2,128,512]{3,2,1,0:T(8,128)} %all-to-all-done.1), kind=kOutput, calls=%fused_computation.75 | convolution fusion | flops 3221225472 | bytes 9437184 | tf_op jit(solution)/shard_map/sprn,pqsrm->qmn/dot_general | solution.py:225
  390.3 7.4 %collective-permute-done.1 = f32[2,256,512]{2,1,0:T(8,128)S(1)} collective-permute-done((f32[2,256,512]{2,1,0:T(8,128)S(1)}, f32[2,256,512]{2,1,0:T(8,128)S(1)}, u32[]{:S(2)}, u32[]{:S(2)}) %collective-permute-start.1) | collective-permute-done | bytes 1048608 | tf_op jit(solution)/shard_map/ppermute | solution.py:20
  397.9 1.9 collective-permute-start.2
  399.9 8.7 %fusion.45 = f32[2,256,512]{2,1,0:T(8,128)S(1)} fusion(f32[2,2,8,128,256]{4,3,2,1,0:T(8,128)S(1)} %bitcast.262, f32[8,2,128,512]{3,2,1,0:T(8,128)} %all-to-all-done.1), kind=kOutput, calls=%fused_computation.74 | convolution fusion | flops 3221225472 | bytes 9437184 | tf_op jit(solution)/shard_map/sprn,pqsrm->qmn/dot_general | solution.py:225
  408.6 7.6 %collective-permute-done.2 = f32[2,256,512]{2,1,0:T(8,128)S(1)} collective-permute-done((f32[2,256,512]{2,1,0:T(8,128)S(1)}, f32[2,256,512]{2,1,0:T(8,128)S(1)}, u32[]{:S(2)}, u32[]{:S(2)}) %collective-permute-start.2) | collective-permute-done | bytes 1048608 | tf_op jit(solution)/shard_map/ppermute | solution.py:20
  416.2 1.2 add_bitcast_fusion
  (82 shorter events, 5.4 us)
Async XLA Ops:
  0.0 6.2 %copy-start.6 = (f32[1,2,256,512]{3,2,1,0:T(8,128)S(1)}, f32[1,2,256,512]{3,2,1,0:T(8,128)}, u32[]{:S(2)}) copy-start(f32[1,2,256,512]{3,2,1,0:T(8,128)} %param.4) | copy-start | bytes 3145732
  17.5 12.9 %copy-start.5 = (f32[2,64,4096]{2,1,0:T(8,128)S(1)}, f32[2,64,4096]{2,1,0:T(8,128)}, u32[]{:S(2)}) copy-start(f32[2,64,4096]{2,1,0:T(8,128)} %param.5) | copy-start | bytes 6291460
  17.5 105.2 %all-to-all-start = ((f32[8,2,128,8,64]{2,4,3,1,0:T(8,128)}), f32[8,2,128,8,64]{2,4,3,1,0:T(8,128)}, u32[]{:S(2)}, u32[]{:S(2)}) async-start(f32[8,2,128,8,64]{2,4,3,1,0:T(8,128)} %copy.71), calls=%async_computation | async-start | bytes 8388608 | tf_op jit(solution)/shard_map/all_to_all | solution.py:163
  227.6 1.6 copy-start.3
  231.5 1.6 copy-start.4
  240.8 101.3 %all-to-all-start.1 = ((f32[8,2,128,512]{3,2,1,0:T(8,128)}), f32[8,2,128,512]{3,2,1,0:T(8,128)}, u32[]{:S(2)}, u32[]{:S(2)}) async-start(f32[8,2,128,512]{3,2,1,0:T(8,128)} %copy.95), calls=%async_computation.1 | async-start | bytes 8388608 | tf_op jit(solution)/shard_map/all_to_all | solution.py:215
  342.1 28.3 %copy-start.2 = (f32[2,2,1024,256]{3,2,1,0:T(8,128)S(1)}, f32[2,2,1024,256]{3,2,1,0:T(8,128)}, u32[]{:S(2)}) copy-start(f32[2,2,1024,256]{3,2,1,0:T(8,128)} %get-tuple-element.33) | copy-start | bytes 12582916
  352.2 18.2 %collective-permute-start = (f32[2,256,512]{2,1,0:T(8,128)S(1)}, f32[2,256,512]{2,1,0:T(8,128)S(1)}, u32[]{:S(2)}, u32[]{:S(2)}) collective-permute-start(f32[2,256,512]{2,1,0:T(8,128)S(1)} %fusion.54), channel_id=1, source_target_pairs={{0,8},{8,16},{16,24},{24,32},{32,40},{40,48},{48,56},{56,64},{64,7... | collective-permute-start | bytes 3145736 | tf_op jit(solution)/shard_map/ppermute | solution.py:20
  370.4 11.0 %copy-start.1 = (f32[2,2,1024,256]{3,2,1,0:T(8,128)S(1)}, f32[2,2,1024,256]{3,2,1,0:T(8,128)}, u32[]{:S(2)}) copy-start(f32[2,2,1024,256]{3,2,1,0:T(8,128)} %get-tuple-element.35) | copy-start | bytes 12582916
  379.5 18.2 %collective-permute-start.1 = (f32[2,256,512]{2,1,0:T(8,128)S(1)}, f32[2,256,512]{2,1,0:T(8,128)S(1)}, u32[]{:S(2)}, u32[]{:S(2)}) collective-permute-start(f32[2,256,512]{2,1,0:T(8,128)S(1)} %fusion.57), channel_id=1, source_target_pairs={{0,8},{8,16},{16,24},{24,32},{32,40},{40,48},{48,56},{56,64},{64,7... | collective-permute-start | bytes 3145736 | tf_op jit(solution)/shard_map/ppermute | solution.py:20
  381.4 18.4 %copy-start = (f32[2,2,1024,256]{3,2,1,0:T(8,128)S(1)}, f32[2,2,1024,256]{3,2,1,0:T(8,128)}, u32[]{:S(2)}) copy-start(f32[2,2,1024,256]{3,2,1,0:T(8,128)} %get-tuple-element.34) | copy-start | bytes 12582916
  397.9 18.2 %collective-permute-start.2 = (f32[2,256,512]{2,1,0:T(8,128)S(1)}, f32[2,256,512]{2,1,0:T(8,128)S(1)}, u32[]{:S(2)}, u32[]{:S(2)}) collective-permute-start(f32[2,256,512]{2,1,0:T(8,128)S(1)} %add.716), channel_id=1, source_target_pairs={{0,8},{8,16},{16,24},{24,32},{32,40},{40,48},{48,56},{56,64},{64,7... | collective-permute-start | bytes 3145736 | tf_op jit(solution)/shard_map/ppermute | solution.py:20

commit v2 on v1

--- a/solution.py
+++ b/solution.py
@@ -201,18 +201,23 @@
         "phrjk,pqhjv->qhrkv", packed, real_table(conjugate(back_two)), precision=HIGH
     )
     packed = complex_mul(packed, conjugate(back_turn)[:, :, None])
-    packed = jnp.einsum(
-        "phrkv,pqhku->qhruv", packed, real_table(conjugate(back_one)), precision=HIGH
-    )
-    packed = packed.reshape(2, local_rows, B1, second_len)
+    last_table = real_table(conjugate(back_one))
+    packed = [
+        jnp.einsum("phrkv,phku->hruv", packed, last_table[:, part], precision=HIGH).reshape(
+            local_rows, B1, second_len
+        )
+        for part in (0, 1)
+    ]
     upper_turn = rotation(local_order[:, None] * (second_len * first_range)[None, :], total_bins)
     lower_turn = rotation(local_order[:, None] * second_range[None, :], total_bins)
-    packed = complex_mul(
-        complex_mul(packed, conjugate(upper_turn)[..., None]), conjugate(lower_turn)[:, :, None, :]
-    )
-    packed = packed.reshape(2, local_rows, groups, local_width)
-    packed = jnp.transpose(packed, (2, 0, 1, 3))
+    back_row = complex_mul(upper_turn[..., None], lower_turn[:, :, None, :])
+    signal_re = packed[0] * back_row[0] + packed[1] * back_row[1]
+    signal_im = packed[1] * back_row[0] - packed[0] * back_row[1]
+    signal_re = jnp.transpose(signal_re.reshape(local_rows, groups, local_width), (1, 0, 2))
+    signal_im = jnp.transpose(signal_im.reshape(local_rows, groups, local_width), (1, 0, 2))
+    packed = jnp.stack([signal_re, signal_im], axis=1)
     arrived = lax.all_to_all(packed, "fft", split_axis=0, concat_axis=0, tiled=True)
+    arrived = jnp.transpose(arrived, (1, 0, 2, 3)).reshape(2, row_count, local_width)
     exit_turn = rotation(
         row_order[:, None] * jnp.arange(row_count, dtype=jnp.int32)[None, :], row_count
     )
@@ -221,8 +226,7 @@
     def sample_block(block_id):
         lower = block_id * quarter
         table = exit_table[:, :, :, lower : lower + quarter]
-        table = table.reshape(2, 2, groups, local_rows, quarter)
-        return jnp.einsum("sprn,pqsrm->qmn", arrived, table, precision=HIGH)
+        return jnp.einsum("prn,pqrm->qmn", arrived, table, precision=HIGH)
 
     running = sample_block(3)
     for block_id in (2, 1, 0):

time: 425 us -> 414 us (0.974)
  waiting for transfers between devices: 179 us -> 195 us
  matrix products: 73 us -> 57.5 us
  other arithmetic: 56.4 us -> 49.9 us
  local copies, waits for them, and re-layouts: 73.2 us -> 67.4 us
    dot_general x5 -> x6, matrix products: 40.7 us -> 25.7 us  [the longest x4 17.8 us: sample_block(): return jnp.einsum('prn,pqrm->qmn', arrived, table, precision=HIGH)]
    squeeze x4 -> x0, local copies, waits for them, and re-layouts: 14.7 us -> none  [complex_mul(): first = left_pair[0] * right_pair[0] - left_pair[1] * right_pair[1]]
    reshape x0 -> x4, local copies, waits for them, and re-layouts: none -> 13.1 us  [per_device(): jnp.einsum('phrkv,phku->hruv', packed, last_table[:, part], precision=HIGH)]
    ppermute x3, waiting for transfers between devices: 31.3 us -> 41.5 us  [passed_along(): return lax.ppermute(shard, axis, pairs)]
    all_to_all x1, waiting for transfers between devices: 64.9 us -> 73.2 us  [per_device(): lax.all_to_all(packed, 'fft', split_axis=0, concat_axis=0, tiled=True)]
    another operation x5 -> x4, other arithmetic: 12.6 us -> 6.81 us  [real_table(): jnp.stack([jnp.stack([pair[0], pair[1]]), jnp.stack([-pair[1], pair[0]])])]
  transfers between devices with their start and end apart: 5 -> 5, of which waited for: 5 -> 5; matrix products, arithmetic and copies ran while one was open for 15% -> 11% of each run, Pallas kernels for 0% -> 0%
where the time goes in v2:
time: 414 us; the launch traced here: 407 us
  waiting for transfers between devices  195 us (47%)
  local copies, waits for them, and re-layouts  67.4 us (16%)
  matrix products  57.5 us (14%)
  other arithmetic  49.9 us (12%)
  starting transfers between devices  19.9 us (5%)
  Pallas kernels  15.5 us (4%)
    all_to_all x1, waiting for transfers between devices, per_device(): lax.all_to_all(spread, 'fft', split_axis=0, concat_axis=0, tiled=True)  80.5 us
    all_to_all x1, waiting for transfers between devices, per_device(): lax.all_to_all(packed, 'fft', split_axis=0, concat_axis=0, tiled=True)  73.2 us
    ppermute x3, waiting for transfers between devices, passed_along(): return lax.ppermute(shard, axis, pairs)  41.5 us
    dot_general x4, matrix products, sample_block(): return jnp.einsum('prn,pqrm->qmn', arrived, table, precision=HIGH)  17.8 us
    neg x1, other arithmetic, real_table(): -pair[1]  16.8 us
    pallas_call x1, Pallas kernels, middle(): pl.pallas_call(middle_kernel, out_shape=jax.ShapeDtypeStruct(spectrum.sha...  15.5 us
    reshape x4, local copies, waits for them, and re-layouts, per_device(): jnp.einsum('phrkv,phku->hruv', packed, last_table[:, part], precision=HIGH)  13.1 us
    reshape x2, local copies, waits for them, and re-layouts, per_device(): spectrum = spectrum.reshape(2, 2, half_count, columns)  12.5 us
  transfers between devices with their start and end apart: 5, of which 5 were waited for; matrix products, arithmetic and copies ran while one was open for 11% of the time, Pallas kernels for 0%

profile of v2, /device:TPU:16, one launch (start us, length us, event | category | flops | bytes accessed | tf_op | source)
XLA Modules:
  0.0 406.5 jit_solution(15046792496287071838)
XLA Ops:
  0.0 1.0 fusion.103
  1.1 5.0 %fusion.74 = (f32[1,1,256,8,128]{4,2,0,3,1:T(8,128)S(1)}, f32[1,1,256,8,128]{4,2,0,3,1:T(8,128)}, f32[1,1,256,8,128]{4,2,0,3,1:T(8,128)}) fusion(s32[8,128]{1,0:T(8,128)S(1)} %select_select_fusion), kind=kLoop, calls=%fused_computation.97 | loop fusion | flops 3932160 | bytes 3149824 | tf_op jit(solution)/shard_map/sin | solution.py:26
  6.2 1.3 copy.62
  7.5 0.2 multiply_subtract_fusion.7
  7.7 5.7 %fusion.46 = f32[8,2,128,8,64]{2,4,3,0,1:T(8,128)S(1)} fusion(f32[2,256,8,64,1,1]{1,3,2,0,5,4:T(8,128)} %bitcast.275, f32[1,1,256,8,128]{4,2,0,3,1:T(8,128)} %get-tuple-element.87, f32[1,1,256,8,128]{4,2,0,3,1:T(8,128)} %get-tuple-element.86, f32[1,1,256,8,128]{4,2,0,3,1:T(8,128)S(1)} %get-tuple-element.85), kind=kOutput, calls=%fused_computation.58 | convolution fusion | flops 3224371200 | bytes 8388608 | tf_op jit(solution)/shard_map/pmun,pqmdr->dqrun/dot_general | solution.py:158
  13.4 1.1 multiply_subtract_fusion.3
  14.6 0.6 pad_maximum_fusion.3
  15.2 2.3 copy.64
  17.4 8.9 %all-to-all-start = ((f32[8,2,128,8,64]{2,4,3,1,0:T(8,128)}), f32[8,2,128,8,64]{2,4,3,1,0:T(8,128)}, u32[]{:S(2)}, u32[]{:S(2)}) async-start(f32[8,2,128,8,64]{2,4,3,1,0:T(8,128)} %copy.64), calls=%async_computation | async-start | bytes 8388608 | tf_op jit(solution)/shard_map/all_to_all | solution.py:163
  26.6 0.5 fusion.257
  27.1 0.4 sin.204
  27.6 0.7 broadcast_in_dim.23.column_ref
  28.3 0.8 copy.75.row_ref
  29.2 0.4 fusion.210
  30.5 1.1 copy.72
  31.7 1.2 convolution_bitcast_fusion.1
  33.0 0.6 copy.71
  33.6 2.1 pad_maximum_fusion.5
  35.7 2.6 copy.74.phase_ref
  38.5 0.3 fusion.194
  38.8 0.3 fusion.198
  39.2 2.5 multiply_subtract_fusion.2
  41.7 0.5 fusion.255
  42.2 80.5 %all-to-all-done = f32[8,2,128,8,64]{2,4,3,1,0:T(8,128)} async-done(((f32[8,2,128,8,64]{2,4,3,1,0:T(8,128)}), f32[8,2,128,8,64]{2,4,3,1,0:T(8,128)}, u32[]{:S(2)}, u32[]{:S(2)}) %all-to-all-start) | async-done | bytes 4194336 | tf_op jit(solution)/shard_map/all_to_all | solution.py:163
  122.6 9.6 %copy.65 = f32[8,2,128,8,64]{4,3,0,1,2:T(8,128)} copy(f32[8,2,128,8,64]{2,4,3,1,0:T(8,128)} %all-to-all-done) | data formatting | bytes 8388608 | tf_op jit(solution)/shard_map/all_to_all | solution.py:163
  132.2 6.4 %convolution_bitcast_fusion = f32[2,2,64,64,64]{4,3,2,0,1:T(8,128)S(1)} fusion(f32[8,2,2,64,8,64,1]{5,4,0,1,3,6,2:T(8,128)} %bitcast.269, f32[1,2,2,8,8,64]{5,4,3,0,1,2:T(8,128)S(1)} %bitcast.276, f32[1,1,1,8,8,64]{5,4,3,0,1,2:T(8,128)S(1)} %get-tuple-element.81, f32[1,1,1,8,8,64]{5,4,3,0,1,2:T(8,128)S(1)} %get-tuple-element.82, ...), kind=kOutput, calls=%fused_computation.55 | convolution fusion | flops 805437440 | bytes 8519680 | tf_op jit(solution)/shard_map/sphrun,pqhsuk->qhrkn/dot_general | solution.py:169
  138.7 2.0 multiply_subtract_fusion.1
  140.7 8.3 %fusion.34 = f32[2,2,64,64,64]{4,3,2,0,1:T(8,128)} fusion(f32[1,2,2,64,64]{3,4,0,1,2:T(8,128)S(1)} %get-tuple-element.58, f32[1,2,2,64,64]{3,4,0,1,2:T(8,128)S(1)} %fusion.95, f32[1,2,64,64,64]{4,3,2,0,1:T(8,128)S(1)} %get-tuple-element.33, f32[1,2,64,64,64]{4,3,2,0,1:T(8,128)S(1)} %get-tuple-element.32), kind=kOutput, calls=%fused_computation.53 | convolution fusion | flops 806387712 | bytes 8519680 | tf_op jit(solution)/shard_map/phrkn,pqhnj->qhrjk/dot_general | solution.py:171
  149.0 7.9 %reshape.1967 = f32[2,2,64,4096]{3,2,0,1:T(8,128)} reshape(f32[2,2,64,64,64]{4,3,2,0,1:T(8,128)} %fusion.34) | data formatting | bytes 8388608 | tf_op jit(solution)/shard_map/reshape | solution.py:172
  156.9 1.1 slice.310
  158.0 1.1 fusion.261
  159.1 4.6 %copy.73.spec_ref = f32[2,2,64,4096]{3,2,1,0:T(8,128)} copy(f32[2,2,64,4096]{3,2,0,1:T(8,128)} %reshape.1967) | data formatting | bytes 8388608 | tf_op jit(solution)/shard_map/reshape | solution.py:172
  164.8 0.5 fusion.160
  166.0 15.5 %shard_map.28 = f32[2,2,64,4096]{3,2,1,0:T(8,128)} custom-call(f32[2,2,64,4096]{3,2,1,0:T(8,128)} %copy.73.spec_ref, f32[2,64,4096]{2,1,0:T(8,128)} %copy.74.phase_ref, f32[2,2,64,1]{3,2,1,0:T(8,128)} %copy.75.row_ref, f32[2,2,1,4096]{3,2,1,0:T(1,128)} %broadcast_in_dim.23.column_ref), custom_call_target="tpu_custom_call" | custom-call | tf_op jit(solution)/shard_map/pallas_call | solution.py:116
  181.5 1.1 slice.335
  183.1 2.1 scatter.4
  185.1 7.9 %reshape.1941 = f32[2,2,64,64,64]{4,3,2,1,0:T(8,128)} reshape(f32[2,2,64,4096]{3,2,1,0:T(8,128)} %scatter.4) | data formatting | bytes 8388608 | tf_op jit(solution)/shard_map/reshape | solution.py:196
  193.1 9.5 %fusion.37 = f32[2,2,64,64,64]{4,3,2,0,1:T(8,128)S(1)} fusion(f32[2,2,64,64,64]{4,3,2,1,0:T(8,128)} %reshape.1941, f32[1,2,2,64,64]{3,4,1,2,0:T(8,128)S(1)} %get-tuple-element.63, f32[1,2,2,64,64]{3,4,1,2,0:T(8,128)S(1)} %get-tuple-element.62), kind=kOutput, calls=%fused_computation.54 | convolution fusion | flops 805339136 | bytes 8519680 | tf_op jit(solution)/shard_map/phrjk,pqhjv->qhrkv/dot_general | solution.py:200
  202.5 2.0 multiply_subtract_fusion
  204.6 3.9 fusion.43
  208.5 4.0 fusion.40
  212.5 3.4 reshape.1942
  215.9 4.8 %reshape.1943 = f32[128,8,512]{2,1,0:T(8,128)} reshape(f32[2,64,64,64]{3,2,1,0:T(8,128)} %fusion.43) | data formatting | bytes 4194304 | tf_op jit(solution)/shard_map/reshape | solution.py:206
  220.7 3.0 copy.87
  223.7 1.9 copy.84
  225.6 3.9 fusion.50
  229.5 0.3 pad_maximum_fusion.4
  229.8 2.3 copy.90
  232.1 4.8 %all-to-all-start.1 = ((f32[8,2,128,512]{2,3,1,0:T(8,128)}), f32[8,2,128,512]{2,3,1,0:T(8,128)}, u32[]{:S(2)}, u32[]{:S(2)}) async-start(f32[8,2,128,512]{2,3,1,0:T(8,128)} %copy.90), calls=%async_computation.1 | async-start | bytes 8388608 | tf_op jit(solution)/shard_map/all_to_all | solution.py:219
  236.9 16.8 %fusion.53 = (f32[1,1024,1024]{1,2,0:T(8,128)S(1)}, f32[1,1024,1024]{1,2,0:T(8,128)S(1)}, f32[1,1024,1024]{1,2,0:T(8,128)S(1)}) fusion(s32[1024]{0:T(1024)S(1)} %select_select_fusion.1), kind=kLoop, calls=%fused_computation.76 | loop fusion | flops 18874368 | bytes 12587008 | tf_op jit(solution)/shard_map/neg | solution.py:34
  253.7 6.7 %maximum_bitcast_fusion.1 = (f32[1,2,1024,1024]{2,3,0,1:T(8,128)}, f32[1,2,1024,1024]{2,3,0,1:T(8,128)}) fusion(f32[1,1024,1024]{1,2,0:T(8,128)S(1)} %get-tuple-element.78, f32[1,1024,1024]{1,2,0:T(8,128)S(1)} %get-tuple-element.76, f32[1,1024,1024]{1,2,0:T(8,128)S(1)} %get-tuple-element.77), kind=kLoop, calls=%fused_computation.7 | loop fusion | flops 4194304 | bytes 29360128 | tf_op jit(solution)/shard_map/stack | solution.py:34
  260.4 73.2 %all-to-all-done.1 = f32[8,2,128,512]{2,3,1,0:T(8,128)} async-done(((f32[8,2,128,512]{2,3,1,0:T(8,128)}), f32[8,2,128,512]{2,3,1,0:T(8,128)}, u32[]{:S(2)}, u32[]{:S(2)}) %all-to-all-start.1) | async-done | bytes 4194336 | tf_op jit(solution)/shard_map/all_to_all | solution.py:219
  333.6 5.4 %copy.91 = f32[2,8,128,512]{3,2,1,0:T(8,128)} copy(f32[2,8,128,512]{2,3,0,1:T(8,128)} %bitcast.83) | data formatting | bytes 8388608 | tf_op jit(solution)/shard_map/transpose | solution.py:220
  339.0 7.2 %fusion.54 = f32[2,256,512]{2,1,0:T(8,128)S(1)} fusion(f32[2,1024,512,1]{2,1,0,3:T(8,128)} %bitcast.265, f32[1,2,1024,1024]{2,3,0,1:T(8,128)} %get-tuple-element.38, f32[1,2,1024,1024]{2,3,0,1:T(8,128)} %get-tuple-element.39), kind=kOutput, calls=%fused_computation.80 | convolution fusion | flops 3222274048 | bytes 22020096 | tf_op jit(solution)/shard_map/prn,pqrm->qmn/dot_general | solution.py:229
  346.1 2.4 collective-permute-start
  348.6 16.0 %collective-permute-done = f32[2,256,512]{2,1,0:T(8,128)S(1)} collective-permute-done((f32[2,256,512]{2,1,0:T(8,128)S(1)}, f32[2,256,512]{2,1,0:T(8,128)S(1)}, u32[]{:S(2)}, u32[]{:S(2)}) %collective-permute-start) | collective-permute-done | bytes 1048608 | tf_op jit(solution)/shard_map/ppermute | solution.py:20
  364.7 3.5 fusion.64
  368.2 1.9 collective-permute-start.1
  370.1 3.5 fusion.55
  373.7 12.7 %collective-permute-done.1 = f32[2,256,512]{2,1,0:T(8,128)S(1)} collective-permute-done((f32[2,256,512]{2,1,0:T(8,128)S(1)}, f32[2,256,512]{2,1,0:T(8,128)S(1)}, u32[]{:S(2)}, u32[]{:S(2)}) %collective-permute-start.1) | collective-permute-done | bytes 1048608 | tf_op jit(solution)/shard_map/ppermute | solution.py:20
  386.7 1.9 collective-permute-start.2
  388.6 3.5 fusion.58
  392.1 12.7 %collective-permute-done.2 = f32[2,256,512]{2,1,0:T(8,128)S(1)} collective-permute-done((f32[2,256,512]{2,1,0:T(8,128)S(1)}, f32[2,256,512]{2,1,0:T(8,128)S(1)}, u32[]{:S(2)}, u32[]{:S(2)}) %collective-permute-start.2) | collective-permute-done | bytes 1048608 | tf_op jit(solution)/shard_map/ppermute | solution.py:20
  404.9 1.2 add_bitcast_fusion
  (78 shorter events, 4.1 us)
Async XLA Ops:
  0.0 6.2 %copy-start.3 = (f32[1,2,256,512]{3,2,1,0:T(8,128)S(1)}, f32[1,2,256,512]{3,2,1,0:T(8,128)}, u32[]{:S(2)}) copy-start(f32[1,2,256,512]{3,2,1,0:T(8,128)} %param.4) | copy-start | bytes 3145732
  17.4 12.9 %copy-start.2 = (f32[2,64,4096]{2,1,0:T(8,128)S(1)}, f32[2,64,4096]{2,1,0:T(8,128)}, u32[]{:S(2)}) copy-start(f32[2,64,4096]{2,1,0:T(8,128)} %param.5) | copy-start | bytes 6291460
  17.4 105.2 %all-to-all-start = ((f32[8,2,128,8,64]{2,4,3,1,0:T(8,128)}), f32[8,2,128,8,64]{2,4,3,1,0:T(8,128)}, u32[]{:S(2)}, u32[]{:S(2)}) async-start(f32[8,2,128,8,64]{2,4,3,1,0:T(8,128)} %copy.64), calls=%async_computation | async-start | bytes 8388608 | tf_op jit(solution)/shard_map/all_to_all | solution.py:163
  232.1 101.5 %all-to-all-start.1 = ((f32[8,2,128,512]{2,3,1,0:T(8,128)}), f32[8,2,128,512]{2,3,1,0:T(8,128)}, u32[]{:S(2)}, u32[]{:S(2)}) async-start(f32[8,2,128,512]{2,3,1,0:T(8,128)} %copy.90), calls=%async_computation.1 | async-start | bytes 8388608 | tf_op jit(solution)/shard_map/all_to_all | solution.py:219
  339.0 25.7 %slice-start = ((s8[8388608]{0:T(1024)(128)(4,1)}), s8[4194304]{0:T(1024)(128)(4,1)S(1)}, s32[]{:S(2)}) async-start(s8[8388608]{0:T(1024)(128)(4,1)} %bitcast.263), calls=%async_computation.2 | async-start | bytes 8388608
  339.0 25.7 %slice-start.1 = ((s8[8388608]{0:T(1024)(128)(4,1)}), s8[4194304]{0:T(1024)(128)(4,1)S(1)}, s32[]{:S(2)}) async-start(s8[8388608]{0:T(1024)(128)(4,1)} %bitcast.263), calls=%async_computation.3 | async-start | bytes 8388608
  339.0 25.7 %copy-start = (f32[1,2,1024,1024]{2,3,0,1:T(8,128)S(1)}, f32[1,2,1024,1024]{2,3,0,1:T(8,128)}, u32[]{:S(2)}) copy-start(f32[1,2,1024,1024]{2,3,0,1:T(8,128)} %get-tuple-element.39) | copy-start | bytes 25165828
  339.0 25.7 %copy-start.1 = (f32[2,8,128,512]{3,2,1,0:T(8,128)S(1)}, f32[2,8,128,512]{3,2,1,0:T(8,128)}, u32[]{:S(2)}) copy-start(f32[2,8,128,512]{3,2,1,0:T(8,128)} %copy.91) | copy-start | bytes 12582916
  346.1 18.5 %collective-permute-start = (f32[2,256,512]{2,1,0:T(8,128)S(1)}, f32[2,256,512]{2,1,0:T(8,128)S(1)}, u32[]{:S(2)}, u32[]{:S(2)}) collective-permute-start(f32[2,256,512]{2,1,0:T(8,128)S(1)} %fusion.54), channel_id=1, source_target_pairs={{0,8},{8,16},{16,24},{24,32},{32,40},{40,48},{48,56},{56,64},{64,7... | collective-permute-start | bytes 3145736 | tf_op jit(solution)/shard_map/ppermute | solution.py:20
  368.2 18.2 %collective-permute-start.1 = (f32[2,256,512]{2,1,0:T(8,128)S(1)}, f32[2,256,512]{2,1,0:T(8,128)S(1)}, u32[]{:S(2)}, u32[]{:S(2)}) collective-permute-start(f32[2,256,512]{2,1,0:T(8,128)S(1)} %fusion.64), channel_id=1, source_target_pairs={{0,8},{8,16},{16,24},{24,32},{32,40},{40,48},{48,56},{56,64},{64,7... | collective-permute-start | bytes 3145736 | tf_op jit(solution)/shard_map/ppermute | solution.py:20
  386.7 18.2 %collective-permute-start.2 = (f32[2,256,512]{2,1,0:T(8,128)S(1)}, f32[2,256,512]{2,1,0:T(8,128)S(1)}, u32[]{:S(2)}, u32[]{:S(2)}) collective-permute-start(f32[2,256,512]{2,1,0:T(8,128)S(1)} %add.702), channel_id=1, source_target_pairs={{0,8},{8,16},{16,24},{24,32},{32,40},{40,48},{48,56},{56,64},{64,7... | collective-permute-start | bytes 3145736 | tf_op jit(solution)/shard_map/ppermute | solution.py:20

commit v3 on v2

--- a/solution.py
+++ b/solution.py
@@ -4,10 +4,12 @@
 import jax.numpy as jnp
 from jax import lax
 from jax.experimental import pallas as pl
+from jax.experimental.pallas import tpu as pltpu
 from jax.sharding import PartitionSpec as P
 
 B1 = 64
 TILE_ROWS = 8
+TAIL_CHUNKS = 4
 
 
 HIGHEST = lax.Precision.HIGHEST
@@ -125,6 +127,69 @@
         ],
         out_specs=spec_block,
     )(spectrum, phase_rows, row_turn, column_turn)
+
+
+def tail_kernel(b1_ref, b2_ref, b3_ref, out_ref, land, sums, send_sem, recv_sem):
+    me = lax.axis_index("seg")
+    count = lax.axis_size("seg")
+    lane = lax.axis_index("fft")
+    right = lax.rem(me + 1, count)
+    left = lax.rem(me + count - 1, count)
+    rows = b1_ref.shape[1] // TAIL_CHUNKS
+    barrier = pltpu.get_barrier_semaphore()
+    for neighbour in (left, right):
+        pl.semaphore_signal(
+            barrier, inc=1, device_id=(neighbour, lane), device_id_type=pl.DeviceIdType.MESH
+        )
+    pl.semaphore_wait(barrier, 2)
+    keep = jnp.where(me > 0, 1.0, 0.0).astype(jnp.float32)
+
+    def hop(step, chunk, source):
+        part = pl.ds(chunk * rows, rows)
+        return pltpu.make_async_remote_copy(
+            src_ref=source.at[:, part],
+            dst_ref=land.at[step, :, part],
+            send_sem=send_sem.at[step, chunk],
+            recv_sem=recv_sem.at[step, chunk],
+            device_id=(right, lane),
+            device_id_type=pl.DeviceIdType.MESH,
+        )
+
+    copies = []
+    for chunk in range(TAIL_CHUNKS):
+        copy = hop(0, chunk, b3_ref)
+        copy.start()
+        copies.append(copy)
+    for step, block_ref in ((1, b2_ref), (2, b1_ref)):
+        for chunk in range(TAIL_CHUNKS):
+            part = pl.ds(chunk * rows, rows)
+            copies[(step - 1) * TAIL_CHUNKS + chunk].wait_recv()
+            sums[step - 1, :, part] = block_ref[:, part] + keep * land[step - 1, :, part]
+            copy = hop(step, chunk, sums.at[step - 1])
+            copy.start()
+            copies.append(copy)
+    for chunk in range(TAIL_CHUNKS):
+        part = pl.ds(chunk * rows, rows)
+        copies[2 * TAIL_CHUNKS + chunk].wait_recv()
+        out_ref[:, part] = keep * land[2, :, part]
+    for copy in copies:
+        copy.wait_send()
+
+
+def tail_sum(b1, b2, b3):
+    return pl.pallas_call(
+        tail_kernel,
+        out_shape=jax.ShapeDtypeStruct(b1.shape, jnp.float32),
+        in_specs=[pl.BlockSpec(memory_space=pltpu.VMEM)] * 3,
+        out_specs=pl.BlockSpec(memory_space=pltpu.VMEM),
+        scratch_shapes=[
+            pltpu.VMEM((3,) + b1.shape, jnp.float32),
+            pltpu.VMEM((2,) + b1.shape, jnp.float32),
+            pltpu.SemaphoreType.DMA((3, TAIL_CHUNKS)),
+            pltpu.SemaphoreType.DMA((3, TAIL_CHUNKS)),
+        ],
+        compiler_params=pltpu.CompilerParams(collective_id=0, has_side_effects=True),
+    )(b1, b2, b3)
 
 
 def per_device(voltage, chirp_phase):
@@ -228,10 +293,8 @@
         table = exit_table[:, :, :, lower : lower + quarter]
         return jnp.einsum("prn,pqrm->qmn", arrived, table, precision=HIGH)
 
-    running = sample_block(3)
-    for block_id in (2, 1, 0):
-        running = sample_block(block_id) + passed_along(running, "seg", 1)
-    return running[None]
+    tail = tail_sum(sample_block(1), sample_block(2), sample_block(3))
+    return (sample_block(0) + tail)[None]
 
 
 def solution(mesh):

time: 414 us -> 416 us (level)
  Pallas kernels: 15.5 us -> 57.5 us
  waiting for transfers between devices: 195 us -> 154 us
  matrix products: 57.5 us -> 65 us
  starting transfers between devices: 19.9 us -> 13.6 us
    pallas_call x0 -> x1, Pallas kernels: none -> 41.9 us  [tail_sum(): pl.pallas_call(tail_kernel, out_shape=jax.ShapeDtypeStruct(b1.shape, jnp....]
    ppermute x3 -> x0, waiting for transfers between devices: 41.5 us -> none  [passed_along(): return lax.ppermute(shard, axis, pairs)]
    dot_general x4, matrix products: 17.8 us -> 25.3 us  [sample_block(): return jnp.einsum('prn,pqrm->qmn', arrived, table, precision=HIGH)]
    ppermute x3 -> x0, starting transfers between devices: 6.28 us -> none  [passed_along(): return lax.ppermute(shard, axis, pairs)]
  transfers between devices with their start and end apart: 5 -> 2, of which waited for: 5 -> 2; matrix products, arithmetic and copies ran while one was open for 11% -> 10% of each run, Pallas kernels for 0% -> 0%
where the time goes in v3:
time: 416 us; the launch traced here: 409 us
  waiting for transfers between devices  154 us (37%)
  local copies, waits for them, and re-layouts  69.3 us (17%)
  matrix products  65 us (16%)
  Pallas kernels  57.5 us (14%)
  other arithmetic  48.6 us (12%)
  starting transfers between devices  13.6 us (3%)
    all_to_all x1, waiting for transfers between devices, per_device(): lax.all_to_all(spread, 'fft', split_axis=0, concat_axis=0, tiled=True)  80.5 us
    all_to_all x1, waiting for transfers between devices, per_device(): lax.all_to_all(packed, 'fft', split_axis=0, concat_axis=0, tiled=True)  73.2 us
    pallas_call x1, Pallas kernels, tail_sum(): pl.pallas_call(tail_kernel, out_shape=jax.ShapeDtypeStruct(b1.shape, jnp....  41.9 us
    dot_general x4, matrix products, sample_block(): return jnp.einsum('prn,pqrm->qmn', arrived, table, precision=HIGH)  25.3 us
    neg x1, other arithmetic, real_table(): -pair[1]  16.8 us
    pallas_call x1, Pallas kernels, middle(): pl.pallas_call(middle_kernel, out_shape=jax.ShapeDtypeStruct(spectrum.sha...  15.5 us
    reshape x4, local copies, waits for them, and re-layouts, per_device(): jnp.einsum('phrkv,phku->hruv', packed, last_table[:, part], precision=HIGH)  13 us
    reshape x2, local copies, waits for them, and re-layouts, per_device(): spectrum = spectrum.reshape(2, 2, half_count, columns)  12.6 us
  transfers between devices with their start and end apart: 2, of which 2 were waited for; matrix products, arithmetic and copies ran while one was open for 10% of the time, Pallas kernels for 0%

profile of v3, /device:TPU:16, one launch (start us, length us, event | category | flops | bytes accessed | tf_op | source)
XLA Modules:
  0.0 408.6 jit_solution(10429459262037008983)
XLA Ops:
  0.0 1.0 fusion.106
  1.1 5.1 %fusion.77 = (f32[1,1,256,8,128]{4,2,0,3,1:T(8,128)S(1)}, f32[1,1,256,8,128]{4,2,0,3,1:T(8,128)}, f32[1,1,256,8,128]{4,2,0,3,1:T(8,128)}) fusion(s32[8,128]{1,0:T(8,128)S(1)} %select_select_fusion), kind=kLoop, calls=%fused_computation.97 | loop fusion | flops 3932160 | bytes 3149824 | tf_op jit(solution)/shard_map/sin | solution.py:28
  6.2 1.3 copy.62
  7.5 0.2 multiply_subtract_fusion.7
  7.7 5.7 %fusion.46 = f32[8,2,128,8,64]{2,4,3,0,1:T(8,128)S(1)} fusion(f32[2,256,8,64,1,1]{1,3,2,0,5,4:T(8,128)} %bitcast.275, f32[1,1,256,8,128]{4,2,0,3,1:T(8,128)} %get-tuple-element.87, f32[1,1,256,8,128]{4,2,0,3,1:T(8,128)} %get-tuple-element.86, f32[1,1,256,8,128]{4,2,0,3,1:T(8,128)S(1)} %get-tuple-element.85), kind=kOutput, calls=%fused_computation.58 | convolution fusion | flops 3224371200 | bytes 8388608 | tf_op jit(solution)/shard_map/pmun,pqmdr->dqrun/dot_general | solution.py:223
  13.5 1.1 multiply_subtract_fusion.3
  14.6 0.6 pad_maximum_fusion.3
  15.2 2.3 copy.64
  17.5 8.9 %all-to-all-start = ((f32[8,2,128,8,64]{2,4,3,1,0:T(8,128)}), f32[8,2,128,8,64]{2,4,3,1,0:T(8,128)}, u32[]{:S(2)}, u32[]{:S(2)}) async-start(f32[8,2,128,8,64]{2,4,3,1,0:T(8,128)} %copy.64), calls=%async_computation | async-start | bytes 8388608 | tf_op jit(solution)/shard_map/all_to_all | solution.py:228
  26.7 0.5 fusion.260
  27.2 0.4 sin.204
  27.7 0.7 broadcast_in_dim.23.column_ref
  28.3 0.8 copy.75.row_ref
  29.3 0.4 fusion.213
  30.5 1.1 copy.72
  31.6 0.2 copy.131
  31.8 1.2 convolution_bitcast_fusion.1
  33.0 0.6 copy.71
  33.6 2.1 pad_maximum_fusion.5
  35.7 2.6 copy.74.phase_ref
  38.6 0.3 fusion.197
  38.9 0.3 fusion.201
  39.2 2.5 multiply_subtract_fusion.2
  41.8 0.5 fusion.258
  42.2 80.5 %all-to-all-done = f32[8,2,128,8,64]{2,4,3,1,0:T(8,128)} async-done(((f32[8,2,128,8,64]{2,4,3,1,0:T(8,128)}), f32[8,2,128,8,64]{2,4,3,1,0:T(8,128)}, u32[]{:S(2)}, u32[]{:S(2)}) %all-to-all-start) | async-done | bytes 4194336 | tf_op jit(solution)/shard_map/all_to_all | solution.py:228
  122.7 9.6 %copy.65 = f32[8,2,128,8,64]{4,3,0,1,2:T(8,128)} copy(f32[8,2,128,8,64]{2,4,3,1,0:T(8,128)} %all-to-all-done) | data formatting | bytes 8388608 | tf_op jit(solution)/shard_map/all_to_all | solution.py:228
  132.3 6.4 %convolution_bitcast_fusion = f32[2,2,64,64,64]{4,3,2,0,1:T(8,128)S(1)} fusion(f32[8,2,2,64,8,64,1]{5,4,0,1,3,6,2:T(8,128)} %bitcast.269, f32[1,2,2,8,8,64]{5,4,3,0,1,2:T(8,128)S(1)} %bitcast.276, f32[1,1,1,8,8,64]{5,4,3,0,1,2:T(8,128)S(1)} %get-tuple-element.81, f32[1,1,1,8,8,64]{5,4,3,0,1,2:T(8,128)S(1)} %get-tuple-element.82, ...), kind=kOutput, calls=%fused_computation.55 | convolution fusion | flops 805437440 | bytes 8519680 | tf_op jit(solution)/shard_map/sphrun,pqhsuk->qhrkn/dot_general | solution.py:234
  138.7 2.0 multiply_subtract_fusion.1
  140.8 8.3 %fusion.34 = f32[2,2,64,64,64]{4,3,2,0,1:T(8,128)} fusion(f32[1,2,2,64,64]{3,4,0,1,2:T(8,128)S(1)} %get-tuple-element.58, f32[1,2,2,64,64]{3,4,0,1,2:T(8,128)S(1)} %fusion.98, f32[1,2,64,64,64]{4,3,2,0,1:T(8,128)S(1)} %get-tuple-element.33, f32[1,2,64,64,64]{4,3,2,0,1:T(8,128)S(1)} %get-tuple-element.32), kind=kOutput, calls=%fused_computation.53 | convolution fusion | flops 806387712 | bytes 8519680 | tf_op jit(solution)/shard_map/phrkn,pqhnj->qhrjk/dot_general | solution.py:236
  149.1 7.9 %reshape.1967 = f32[2,2,64,4096]{3,2,0,1:T(8,128)} reshape(f32[2,2,64,64,64]{4,3,2,0,1:T(8,128)} %fusion.34) | data formatting | bytes 8388608 | tf_op jit(solution)/shard_map/reshape | solution.py:237
  157.0 1.1 slice.310
  158.1 1.1 fusion.264
  159.1 4.6 %copy.73.spec_ref = f32[2,2,64,4096]{3,2,1,0:T(8,128)} copy(f32[2,2,64,4096]{3,2,0,1:T(8,128)} %reshape.1967) | data formatting | bytes 8388608 | tf_op jit(solution)/shard_map/reshape | solution.py:237
  163.9 0.2 convolution_bitcast_fusion.3
  164.1 0.2 fusion.119
  164.9 0.5 fusion.163
  165.5 0.2 convolution_bitcast_fusion.2
  166.1 15.5 %shard_map.28 = f32[2,2,64,4096]{3,2,1,0:T(8,128)} custom-call(f32[2,2,64,4096]{3,2,1,0:T(8,128)} %copy.73.spec_ref, f32[2,64,4096]{2,1,0:T(8,128)} %copy.74.phase_ref, f32[2,2,64,1]{3,2,1,0:T(8,128)} %copy.75.row_ref, f32[2,2,1,4096]{3,2,1,0:T(1,128)} %broadcast_in_dim.23.column_ref), custom_call_target="tpu_custom_call" | custom-call | tf_op jit(solution)/shard_map/pallas_call | solution.py:118
  181.6 1.1 slice.335
  183.2 2.1 scatter.4
  185.2 7.9 %reshape.1941 = f32[2,2,64,64,64]{4,3,2,1,0:T(8,128)} reshape(f32[2,2,64,4096]{3,2,1,0:T(8,128)} %scatter.4) | data formatting | bytes 8388608 | tf_op jit(solution)/shard_map/reshape | solution.py:261
  193.2 9.5 %fusion.37 = f32[2,2,64,64,64]{4,3,2,0,1:T(8,128)S(1)} fusion(f32[2,2,64,64,64]{4,3,2,1,0:T(8,128)} %reshape.1941, f32[1,2,2,64,64]{3,4,1,2,0:T(8,128)S(1)} %get-tuple-element.63, f32[1,2,2,64,64]{3,4,1,2,0:T(8,128)S(1)} %get-tuple-element.62), kind=kOutput, calls=%fused_computation.54 | convolution fusion | flops 805339136 | bytes 8519680 | tf_op jit(solution)/shard_map/phrjk,pqhjv->qhrkv/dot_general | solution.py:265
  202.6 2.0 multiply_subtract_fusion
  204.7 3.9 fusion.43
  208.6 4.0 fusion.40
  212.6 3.4 reshape.1942
  216.0 4.8 %reshape.1943 = f32[128,8,512]{2,1,0:T(8,128)} reshape(f32[2,64,64,64]{3,2,1,0:T(8,128)} %fusion.43) | data formatting | bytes 4194304 | tf_op jit(solution)/shard_map/reshape | solution.py:271
  220.8 2.9 copy.87
  223.8 1.8 copy.84
  225.6 3.9 fusion.50
  229.5 0.3 pad_maximum_fusion.4
  229.8 2.3 copy.90
  232.1 4.8 %all-to-all-start.1 = ((f32[8,2,128,512]{2,3,1,0:T(8,128)}), f32[8,2,128,512]{2,3,1,0:T(8,128)}, u32[]{:S(2)}, u32[]{:S(2)}) async-start(f32[8,2,128,512]{2,3,1,0:T(8,128)} %copy.90), calls=%async_computation.1 | async-start | bytes 8388608 | tf_op jit(solution)/shard_map/all_to_all | solution.py:284
  236.9 16.8 %fusion.53 = (f32[1,1024,1024]{1,2,0:T(8,128)S(1)}, f32[1,1024,1024]{1,2,0:T(8,128)S(1)}, f32[1,1024,1024]{1,2,0:T(8,128)S(1)}) fusion(s32[1024]{0:T(1024)S(1)} %select_select_fusion.1), kind=kLoop, calls=%fused_computation.76 | loop fusion | flops 18874368 | bytes 12587008 | tf_op jit(solution)/shard_map/neg | solution.py:36
  253.7 6.8 %maximum_bitcast_fusion.1 = (f32[1,2,1024,1024]{2,3,0,1:T(8,128)}, f32[1,2,1024,1024]{2,3,0,1:T(8,128)}) fusion(f32[1,1024,1024]{1,2,0:T(8,128)S(1)} %get-tuple-element.78, f32[1,1024,1024]{1,2,0:T(8,128)S(1)} %get-tuple-element.76, f32[1,1024,1024]{1,2,0:T(8,128)S(1)} %get-tuple-element.77), kind=kLoop, calls=%fused_computation.7 | loop fusion | flops 4194304 | bytes 29360128 | tf_op jit(solution)/shard_map/stack | solution.py:36
  260.5 73.2 %all-to-all-done.1 = f32[8,2,128,512]{2,3,1,0:T(8,128)} async-done(((f32[8,2,128,512]{2,3,1,0:T(8,128)}), f32[8,2,128,512]{2,3,1,0:T(8,128)}, u32[]{:S(2)}, u32[]{:S(2)}) %all-to-all-start.1) | async-done | bytes 4194336 | tf_op jit(solution)/shard_map/all_to_all | solution.py:284
  333.6 5.6 %copy.91 = f32[2,8,128,512]{3,2,1,0:T(8,128)} copy(f32[2,8,128,512]{2,3,0,1:T(8,128)} %bitcast.83) | data formatting | bytes 8388608 | tf_op jit(solution)/shard_map/transpose | solution.py:285
  339.3 8.1 %fusion.55.b1_ref = f32[2,256,512]{2,1,0:T(8,128)} fusion(f32[2,1024,512,1]{2,1,0,3:T(8,128)} %bitcast.265, f32[1,2,1024,1024]{2,3,0,1:T(8,128)} %get-tuple-element.39, f32[1,2,1024,1024]{2,3,0,1:T(8,128)} %get-tuple-element.38), kind=kOutput, calls=%fused_computation.81 | convolution fusion | flops 3222274048 | bytes 22020096 | tf_op jit(solution)/shard_map/prn,pqrm->qmn/dot_general | solution.py:294
  347.3 0.3 copy-done.1
  347.7 1.4 copy-done.2
  349.0 4.5 %fusion.54.b3_ref = f32[2,256,512]{2,1,0:T(8,128)} fusion(f32[2,1024,512,1]{2,1,0,3:T(8,128)S(1)} %bitcast.267, f32[1,2,1024,1024]{2,3,0,1:T(8,128)S(1)} %copy-done, f32[1,2,1024,1024]{2,3,0,1:T(8,128)S(1)} %copy-done.1), kind=kOutput, calls=%fused_computation.80 | convolution fusion | flops 3222274048 | bytes 22020096 | tf_op jit(solution)/shard_map/prn,pqrm->qmn/dot_general | solution.py:294
  353.5 4.5 %fusion.61.b2_ref = f32[2,256,512]{2,1,0:T(8,128)} fusion(f32[2,1024,512,1]{2,1,0,3:T(8,128)S(1)} %bitcast.268, f32[1,2,1024,1024]{2,3,0,1:T(8,128)S(1)} %copy-done.1, f32[1,2,1024,1024]{2,3,0,1:T(8,128)S(1)} %copy-done), kind=kOutput, calls=%fused_computation.83 | convolution fusion | flops 3222274048 | bytes 22020096 | tf_op jit(solution)/shard_map/prn,pqrm->qmn/dot_general | solution.py:294
  358.1 41.9 %shard_map.29 = f32[2,256,512]{2,1,0:T(8,128)} custom-call(f32[2,256,512]{2,1,0:T(8,128)} %fusion.55.b1_ref, f32[2,256,512]{2,1,0:T(8,128)} %fusion.61.b2_ref, f32[2,256,512]{2,1,0:T(8,128)} %fusion.54.b3_ref), custom_call_target="tpu_custom_call" | custom-call | tf_op jit(solution)/shard_map/pallas_call | solution.py:180
  400.0 8.1 %fusion.67 = f32[1,2,256,512]{3,2,1,0:T(8,128)} fusion(f32[2,256,512]{2,1,0:T(8,128)} %shard_map.29, f32[2,1024,512,1]{2,1,0,3:T(8,128)} %bitcast.266, f32[1,2,1024,1024]{2,3,0,1:T(8,128)} %get-tuple-element.39, f32[1,2,1024,1024]{2,3,0,1:T(8,128)} %get-tuple-element.38), kind=kOutput, calls=%fused_computation.86 | convolution fusion | flops 3222536192 | bytes 23068672 | tf_op jit(solution)/shard_map/prn,pqrm->qmn/dot_general | solution.py:294
  (68 shorter events, 3.2 us)
Async XLA Ops:
  0.0 6.2 %copy-start.4 = (f32[1,2,256,512]{3,2,1,0:T(8,128)S(1)}, f32[1,2,256,512]{3,2,1,0:T(8,128)}, u32[]{:S(2)}) copy-start(f32[1,2,256,512]{3,2,1,0:T(8,128)} %param.4) | copy-start | bytes 3145732
  17.5 12.9 %copy-start.3 = (f32[2,64,4096]{2,1,0:T(8,128)S(1)}, f32[2,64,4096]{2,1,0:T(8,128)}, u32[]{:S(2)}) copy-start(f32[2,64,4096]{2,1,0:T(8,128)} %param.5) | copy-start | bytes 6291460
  17.5 105.2 %all-to-all-start = ((f32[8,2,128,8,64]{2,4,3,1,0:T(8,128)}), f32[8,2,128,8,64]{2,4,3,1,0:T(8,128)}, u32[]{:S(2)}, u32[]{:S(2)}) async-start(f32[8,2,128,8,64]{2,4,3,1,0:T(8,128)} %copy.64), calls=%async_computation | async-start | bytes 8388608 | tf_op jit(solution)/shard_map/all_to_all | solution.py:228
  232.1 101.5 %all-to-all-start.1 = ((f32[8,2,128,512]{2,3,1,0:T(8,128)}), f32[8,2,128,512]{2,3,1,0:T(8,128)}, u32[]{:S(2)}, u32[]{:S(2)}) async-start(f32[8,2,128,512]{2,3,1,0:T(8,128)} %copy.90), calls=%async_computation.1 | async-start | bytes 8388608 | tf_op jit(solution)/shard_map/all_to_all | solution.py:284
  339.2 8.1 %copy-start = (f32[1,2,1024,1024]{2,3,0,1:T(8,128)S(1)}, f32[1,2,1024,1024]{2,3,0,1:T(8,128)}, u32[]{:S(2)}) copy-start(f32[1,2,1024,1024]{2,3,0,1:T(8,128)} %get-tuple-element.38) | copy-start | bytes 25165828
  339.2 8.4 %copy-start.1 = (f32[1,2,1024,1024]{2,3,0,1:T(8,128)S(1)}, f32[1,2,1024,1024]{2,3,0,1:T(8,128)}, u32[]{:S(2)}) copy-start(f32[1,2,1024,1024]{2,3,0,1:T(8,128)} %get-tuple-element.39) | copy-start | bytes 25165828
  339.2 9.8 %copy-start.2 = (f32[2,8,128,512]{3,2,1,0:T(8,128)S(1)}, f32[2,8,128,512]{3,2,1,0:T(8,128)}, u32[]{:S(2)}) copy-start(f32[2,8,128,512]{3,2,1,0:T(8,128)} %copy.91) | copy-start | bytes 12582916

commit v4 on v2

--- a/solution.py
+++ b/solution.py
@@ -216,22 +216,28 @@
     signal_re = jnp.transpose(signal_re.reshape(local_rows, groups, local_width), (1, 0, 2))
     signal_im = jnp.transpose(signal_im.reshape(local_rows, groups, local_width), (1, 0, 2))
     packed = jnp.stack([signal_re, signal_im], axis=1)
-    arrived = lax.all_to_all(packed, "fft", split_axis=0, concat_axis=0, tiled=True)
-    arrived = jnp.transpose(arrived, (1, 0, 2, 3)).reshape(2, row_count, local_width)
     exit_turn = rotation(
         row_order[:, None] * jnp.arange(row_count, dtype=jnp.int32)[None, :], row_count
     )
     exit_table = real_table(jnp.stack([exit_turn[0] / total_bins, -exit_turn[1] / total_bins]))
-
-    def sample_block(block_id):
-        lower = block_id * quarter
-        table = exit_table[:, :, :, lower : lower + quarter]
-        return jnp.einsum("prn,pqrm->qmn", arrived, table, precision=HIGH)
-
-    running = sample_block(3)
-    for block_id in (2, 1, 0):
-        running = sample_block(block_id) + passed_along(running, "seg", 1)
-    return running[None]
+    piece = local_width // 2
+    outputs = []
+    for chunk in range(2):
+        arrived = lax.all_to_all(
+            packed[..., chunk * piece : (chunk + 1) * piece], "fft", split_axis=0, concat_axis=0, tiled=True
+        )
+        arrived = jnp.transpose(arrived, (1, 0, 2, 3)).reshape(2, row_count, piece)
+
+        def sample_block(block_id):
+            lower = block_id * quarter
+            table = exit_table[:, :, :, lower : lower + quarter]
+            return jnp.einsum("prn,pqrm->qmn", arrived, table, precision=HIGH)
+
+        running = sample_block(3)
+        for block_id in (2, 1, 0):
+            running = sample_block(block_id) + passed_along(running, "seg", 1)
+        outputs.append(running)
+    return jnp.concatenate(outputs, axis=-1)[None]
 
 
 def solution(mesh):

time: 414 us -> 417 us (level)
  waiting for transfers between devices: 195 us -> 148 us
  local copies, waits for them, and re-layouts: 67.4 us -> 83.2 us
  matrix products: 57.5 us -> 72.7 us
  starting transfers between devices: 19.9 us -> 32.3 us
  other arithmetic: 49.9 us -> 56.3 us
    ppermute x3 -> x6, waiting for transfers between devices: 41.5 us -> 8.14 us  [passed_along(): return lax.ppermute(shard, axis, pairs)]
    all_to_all x1 -> x2, waiting for transfers between devices: 73.2 us -> 59.9 us  [per_device(): lax.all_to_all(packed[..., chunk * piece:(chunk + 1) * piece], 'fft', spl...]
    dot_general x4 -> x8, matrix products: 17.8 us -> 28.5 us  [sample_block(): return jnp.einsum('prn,pqrm->qmn', arrived, table, precision=HIGH)]
    unnamed x17 -> x37, local copies, waits for them, and re-layouts: 1.63 us -> 10.3 us
    ppermute x3 -> x6, starting transfers between devices: 6.28 us -> 14.3 us  [passed_along(): return lax.ppermute(shard, axis, pairs)]
    slice x0 -> x2, local copies, waits for them, and re-layouts: none -> 4.67 us  [per_device(): packed[..., chunk * piece:(chunk + 1) * piece]]
    dot_general x2, matrix products: 7.9 us -> 12.4 us  [per_device(): jnp.einsum('phrkv,phku->hruv', packed, last_table[:, part], precision=HIGH)]
    reshape x0 -> x2, local copies, waits for them, and re-layouts: none -> 4.43 us  [per_device(): arrived = jnp.transpose(arrived, (1, 0, 2, 3)).reshape(2, row_count, piece)]
  transfers between devices with their start and end apart: 5 -> 9, of which waited for: 5 -> 6; matrix products, arithmetic and copies ran while one was open for 11% -> 22% of each run, Pallas kernels for 0% -> 0%
where the time goes in v4:
time: 417 us; the launch traced here: 410 us
  waiting for transfers between devices  148 us (35%)
  local copies, waits for them, and re-layouts  83.2 us (20%)
  matrix products  72.7 us (17%)
  other arithmetic  56.3 us (14%)
  starting transfers between devices  32.3 us (8%)
  Pallas kernels  15.5 us (4%)
    all_to_all x1, waiting for transfers between devices, per_device(): lax.all_to_all(spread, 'fft', split_axis=0, concat_axis=0, tiled=True)  80.5 us
    all_to_all x2, waiting for transfers between devices, per_device(): lax.all_to_all(packed[..., chunk * piece:(chunk + 1) * piece], 'fft', spl...  59.9 us
    dot_general x8, matrix products, sample_block(): return jnp.einsum('prn,pqrm->qmn', arrived, table, precision=HIGH)  28.5 us
    neg x1, other arithmetic, real_table(): -pair[1]  19.7 us
    pallas_call x1, Pallas kernels, middle(): pl.pallas_call(middle_kernel, out_shape=jax.ShapeDtypeStruct(spectrum.sha...  15.5 us
    ppermute x6, starting transfers between devices, passed_along(): return lax.ppermute(shard, axis, pairs)  14.3 us
    reshape x2, local copies, waits for them, and re-layouts, per_device(): spectrum = spectrum.reshape(2, 2, half_count, columns)  12.6 us
    dot_general x2, matrix products, per_device(): jnp.einsum('phrkv,phku->hruv', packed, last_table[:, part], precision=HIGH)  12.4 us
  transfers between devices with their start and end apart: 9, of which 6 were waited for; matrix products, arithmetic and copies ran while one was open for 22% of the time, Pallas kernels for 0%

profile of v4, /device:TPU:16, one launch (start us, length us, event | category | flops | bytes accessed | tf_op | source)
XLA Modules:
  0.0 409.9 jit_solution(968139176741844870)
XLA Ops:
  0.0 5.1 %fusion.74 = (f32[1,1,256,8,128]{4,2,0,3,1:T(8,128)S(1)}, f32[1,1,256,8,128]{4,2,0,3,1:T(8,128)}, f32[1,1,256,8,128]{4,2,0,3,1:T(8,128)}) fusion(s32[8,128]{1,0:T(8,128)S(1)} %select_select_fusion), kind=kLoop, calls=%fused_computation.114 | loop fusion | flops 3932160 | bytes 3149824 | tf_op jit(solution)/shard_map/sin | solution.py:26
  6.2 1.3 copy.102
  7.8 5.7 %fusion.38 = f32[8,2,128,8,64]{2,4,3,0,1:T(8,128)S(1)} fusion(f32[2,256,8,64,1,1]{1,3,2,0,5,4:T(8,128)} %bitcast.368, f32[1,1,256,8,128]{4,2,0,3,1:T(8,128)} %get-tuple-element.89, f32[1,1,256,8,128]{4,2,0,3,1:T(8,128)} %get-tuple-element.88, f32[1,1,256,8,128]{4,2,0,3,1:T(8,128)S(1)} %get-tuple-element.87), kind=kOutput, calls=%fused_computation.54 | convolution fusion | flops 3224371200 | bytes 8388608 | tf_op jit(solution)/shard_map/pmun,pqmdr->dqrun/dot_general | solution.py:158
  15.2 2.3 copy.104
  17.5 8.9 %all-to-all-start = ((f32[8,2,128,8,64]{2,4,3,1,0:T(8,128)}), f32[8,2,128,8,64]{2,4,3,1,0:T(8,128)}, u32[]{:S(2)}, u32[]{:S(2)}) async-start(f32[8,2,128,8,64]{2,4,3,1,0:T(8,128)} %copy.104), calls=%async_computation | async-start | bytes 8388608 | tf_op jit(solution)/shard_map/all_to_all | solution.py:163
  29.2 1.2 convolution_bitcast_fusion.1
  33.6 2.1 pad_maximum_fusion.3
  35.7 2.5 copy.114.phase_ref
  39.3 2.5 multiply_subtract_fusion.2
  42.3 80.5 %all-to-all-done = f32[8,2,128,8,64]{2,4,3,1,0:T(8,128)} async-done(((f32[8,2,128,8,64]{2,4,3,1,0:T(8,128)}), f32[8,2,128,8,64]{2,4,3,1,0:T(8,128)}, u32[]{:S(2)}, u32[]{:S(2)}) %all-to-all-start) | async-done | bytes 4194336 | tf_op jit(solution)/shard_map/all_to_all | solution.py:163
  122.7 9.6 %copy.105 = f32[8,2,128,8,64]{4,3,0,1,2:T(8,128)} copy(f32[8,2,128,8,64]{2,4,3,1,0:T(8,128)} %all-to-all-done) | data formatting | bytes 8388608 | tf_op jit(solution)/shard_map/all_to_all | solution.py:163
  132.3 6.4 %convolution_bitcast_fusion = f32[2,2,64,64,64]{4,3,2,0,1:T(8,128)S(1)} fusion(f32[8,2,2,64,8,64,1]{5,4,0,1,3,6,2:T(8,128)} %bitcast.362, f32[1,2,2,8,8,64]{5,4,3,0,1,2:T(8,128)S(1)} %bitcast.369, f32[1,1,1,8,8,64]{5,4,3,0,1,2:T(8,128)S(1)} %get-tuple-element.83, f32[1,1,1,8,8,64]{5,4,3,0,1,2:T(8,128)S(1)} %get-tuple-element.84, ...), kind=kOutput, calls=%fused_computation.51 | convolution fusion | flops 805437440 | bytes 8519680 | tf_op jit(solution)/shard_map/sphrun,pqhsuk->qhrkn/dot_general | solution.py:169
  138.7 2.0 multiply_subtract_fusion.1
  140.8 8.3 %fusion.26 = f32[2,2,64,64,64]{4,3,2,0,1:T(8,128)} fusion(f32[1,2,2,64,64]{3,4,0,1,2:T(8,128)S(1)} %get-tuple-element.60, f32[1,2,2,64,64]{3,4,0,1,2:T(8,128)S(1)} %fusion.95, f32[1,2,64,64,64]{4,3,2,0,1:T(8,128)S(1)} %get-tuple-element.33, f32[1,2,64,64,64]{4,3,2,0,1:T(8,128)S(1)} %get-tuple-element.32), kind=kOutput, calls=%fused_computation.49 | convolution fusion | flops 806387712 | bytes 8519680 | tf_op jit(solution)/shard_map/phrkn,pqhnj->qhrjk/dot_general | solution.py:171
  149.1 8.0 %reshape.1982 = f32[2,2,64,4096]{3,2,0,1:T(8,128)} reshape(f32[2,2,64,64,64]{4,3,2,0,1:T(8,128)} %fusion.26) | data formatting | bytes 8388608 | tf_op jit(solution)/shard_map/reshape | solution.py:172
  159.2 4.6 %copy.113.spec_ref = f32[2,2,64,4096]{3,2,1,0:T(8,128)} copy(f32[2,2,64,4096]{3,2,0,1:T(8,128)} %reshape.1982) | data formatting | bytes 8388608 | tf_op jit(solution)/shard_map/reshape | solution.py:172
  166.1 15.5 %shard_map.28 = f32[2,2,64,4096]{3,2,1,0:T(8,128)} custom-call(f32[2,2,64,4096]{3,2,1,0:T(8,128)} %copy.113.spec_ref, f32[2,64,4096]{2,1,0:T(8,128)} %copy.114.phase_ref, f32[2,2,64,1]{3,2,1,0:T(8,128)} %copy.115.row_ref, f32[2,2,1,4096]{3,2,1,0:T(1,128)} %broadcast_in_dim.23.column_ref), custom_call_target="tpu_custom_call" | custom-call | tf_op jit(solution)/shard_map/pallas_call | solution.py:116
  183.2 2.1 scatter.4
  185.2 7.9 %reshape.1944 = f32[2,2,64,64,64]{4,3,2,1,0:T(8,128)} reshape(f32[2,2,64,4096]{3,2,1,0:T(8,128)} %scatter.4) | data formatting | bytes 8388608 | tf_op jit(solution)/shard_map/reshape | solution.py:196
  193.1 9.5 %fusion.29 = f32[2,2,64,64,64]{4,3,2,0,1:T(8,128)S(1)} fusion(f32[2,2,64,64,64]{4,3,2,1,0:T(8,128)} %reshape.1944, f32[1,2,2,64,64]{3,4,1,2,0:T(8,128)S(1)} %get-tuple-element.65, f32[1,2,2,64,64]{3,4,1,2,0:T(8,128)S(1)} %get-tuple-element.64), kind=kOutput, calls=%fused_computation.50 | convolution fusion | flops 805339136 | bytes 8519680 | tf_op jit(solution)/shard_map/phrjk,pqhjv->qhrkv/dot_general | solution.py:200
  202.6 2.0 multiply_subtract_fusion
  204.7 2.0 copy-done.2
  206.7 1.3 copy-done.3
  208.0 4.0 fusion.32
  212.0 3.4 reshape.1945
  215.5 1.9 copy.124
  217.3 8.4 %fusion.35 = f32[2,64,64,64]{3,2,1,0:T(8,128)} fusion(f32[2,2,64,64,1]{2,3,1,0,4:T(8,128)S(1)} %get-tuple-element.46, f32[1,2,64,64,64]{4,3,2,0,1:T(8,128)} %copy-done.3, f32[1,2,64,64,64]{4,3,2,0,1:T(8,128)} %copy-done.2), kind=kOutput, calls=%fused_computation.53 | convolution fusion | flops 403701760 | bytes 6356992 | tf_op jit(solution)/shard_map/phrkv,phku->hruv/dot_general | solution.py:206
  225.8 3.4 reshape.1946
  229.2 2.1 copy.127
  231.3 3.9 fusion.49
  235.2 1.6 fusion.41
  236.8 1.5 copy.130
  238.3 3.6 all-to-all-start.1
  241.9 3.2 copy.141
  245.1 44.8 %all-to-all-done.1 = f32[8,2,128,256]{2,3,1,0:T(8,128)S(1)} async-done(((f32[8,2,128,256]{2,3,1,0:T(8,128)}), f32[8,2,128,256]{2,3,1,0:T(8,128)S(1)}, u32[]{:S(2)}, u32[]{:S(2)}) %all-to-all-start.1) | async-done | bytes 2097184 | tf_op jit(solution)/shard_map/all_to_all | solution.py:226
  290.0 5.5 %all-to-all-start.2 = ((f32[8,2,128,256]{2,3,1,0:T(8,128)}), f32[8,2,128,256]{2,3,1,0:T(8,128)}, u32[]{:S(2)}, u32[]{:S(2)}) async-start(f32[8,2,128,256]{2,3,1,0:T(8,128)} %copy.141), calls=%async_computation.2 | async-start | bytes 4194304 | tf_op jit(solution)/shard_map/all_to_all | solution.py:226
  295.5 19.7 %fusion.58 = (f32[1,1024,1024]{2,1,0:T(8,128)}, f32[1,1024,1024]{2,1,0:T(8,128)}, f32[1,1024,1024]{2,1,0:T(8,128)}) fusion(s32[1024]{0:T(1024)S(1)} %select_select_fusion.1), kind=kLoop, calls=%fused_computation.88 | loop fusion | flops 18874368 | bytes 12587008 | tf_op jit(solution)/shard_map/neg | solution.py:34
  315.2 6.8 %maximum_bitcast_fusion.1 = (f32[1,2,1024,1024]{3,2,0,1:T(8,128)S(1)}, f32[1,2,1024,1024]{3,2,0,1:T(8,128)S(1)}) fusion(f32[1,1024,1024]{2,1,0:T(8,128)} %get-tuple-element.80, f32[1,1024,1024]{2,1,0:T(8,128)} %get-tuple-element.78, f32[1,1024,1024]{2,1,0:T(8,128)} %get-tuple-element.79), kind=kLoop, calls=%fused_computation.7 | loop fusion | flops 4194304 | bytes 29360128 | tf_op jit(solution)/shard_map/stack | solution.py:34
  322.6 2.7 copy-done
  325.4 2.5 copy-done.1
  327.9 1.9 fusion.61
  329.8 1.9 collective-permute-start
  331.7 15.0 %all-to-all-done.2 = f32[8,2,128,256]{2,3,1,0:T(8,128)} async-done(((f32[8,2,128,256]{2,3,1,0:T(8,128)}), f32[8,2,128,256]{2,3,1,0:T(8,128)}, u32[]{:S(2)}, u32[]{:S(2)}) %all-to-all-start.2) | async-done | bytes 2097184 | tf_op jit(solution)/shard_map/all_to_all | solution.py:226
  346.8 4.9 %fusion.64 = f32[2,256,256]{1,2,0:T(8,128)S(1)} fusion(f32[2,2,1024,256]{3,2,0,1:T(8,128)} %copy-done.4, f32[8,2,128,256]{2,3,1,0:T(8,128)} %all-to-all-done.2), kind=kOutput, calls=%fused_computation.98 | convolution fusion | flops 1610612736 | bytes 6815744 | tf_op jit(solution)/shard_map/prn,pqrm->qmn/dot_general | solution.py:234
  351.7 2.3 collective-permute-start.3
  354.0 5.0 %fusion.66 = f32[2,256,256]{1,2,0:T(8,128)} fusion(f32[2,256,256]{1,2,0:T(8,128)S(1)} %collective-permute-done, f32[1,2,1024,1024]{3,2,0,1:T(8,128)} %copy-done.1, f32[1,2,1024,1024]{3,2,0,1:T(8,128)} %copy-done, f32[8,2,128,256]{2,3,1,0:T(8,128)S(1)} %all-to-all-done.1), kind=kOutput, calls=%fused_computation.102 | convolution fusion | flops 1611792384 | bytes 19922944 | tf_op jit(solution)/shard_map/prn,pqrm->qmn/dot_general | solution.py:234
  359.0 3.5 collective-permute-start.1
  362.5 2.0 collective-permute-done.3
  364.6 3.6 fusion.65
  368.2 1.9 collective-permute-start.4
  370.1 2.0 fusion.59
  372.1 2.6 copy.131
  374.6 2.7 reshape.1966
  377.4 4.2 %copy.142 = f32[2,8,128,256]{2,1,3,0:T(8,128)} copy(f32[2,8,128,256]{2,3,0,1:T(8,128)} %bitcast.92) | data formatting | bytes 4194304 | tf_op jit(solution)/shard_map/transpose | solution.py:229
  381.5 1.7 reshape.1974
  383.3 4.9 %fusion.62 = f32[2,256,256]{1,2,0:T(8,128)S(1)} fusion(f32[1,2,1024,1024]{3,2,0,1:T(8,128)} %copy-done.1, f32[1,2,1024,1024]{3,2,0,1:T(8,128)} %copy-done, f32[8,2,128,256]{2,3,1,0:T(8,128)} %all-to-all-done.2), kind=kOutput, calls=%fused_computation.96 | convolution fusion | flops 1611661312 | bytes 19398656 | tf_op jit(solution)/shard_map/prn,pqrm->qmn/dot_general | solution.py:234
  388.2 1.3 add.711
  389.5 2.2 collective-permute-start.2
  391.7 1.3 add.714
  393.0 2.5 collective-permute-start.5
  395.5 4.3 %convolution_bitcast_fusion.3 = f32[2,256,256]{1,2,0:T(8,128)S(1)} fusion(f32[2,1024,256,1]{1,2,0,3:T(8,128)S(1)} %copy-done.5, f32[1,2,1024,1024]{3,2,0,1:T(8,128)} %copy-done.1, f32[1,2,1024,1024]{3,2,0,1:T(8,128)} %copy-done), kind=kOutput, calls=%fused_computation.100 | convolution fusion | flops 1611661312 | bytes 19398656 | tf_op jit(solution)/shard_map/prn,pqrm->qmn/dot_general | solution.py:234
  399.8 2.0 convolution_bitcast_fusion.2
  402.4 5.5 %collective-permute-done.5 = f32[2,256,256]{1,2,0:T(8,128)S(1)} collective-permute-done((f32[2,256,256]{1,2,0:T(8,128)S(1)}, f32[2,256,256]{1,2,0:T(8,128)S(1)}, u32[]{:S(2)}, u32[]{:S(2)}) %collective-permute-start.5) | collective-permute-done | bytes 524320 | tf_op jit(solution)/shard_map/ppermute | solution.py:20
  408.1 1.3 copy.152
  (122 shorter events, 17.5 us)
Async XLA Ops:
  0.0 6.2 %copy-start.7 = (f32[1,2,256,512]{3,2,1,0:T(8,128)S(1)}, f32[1,2,256,512]{3,2,1,0:T(8,128)}, u32[]{:S(2)}) copy-start(f32[1,2,256,512]{3,2,1,0:T(8,128)} %param.4) | copy-start | bytes 3145732
  17.5 11.3 %copy-start.6 = (f32[2,64,4096]{2,1,0:T(8,128)S(1)}, f32[2,64,4096]{2,1,0:T(8,128)}, u32[]{:S(2)}) copy-start(f32[2,64,4096]{2,1,0:T(8,128)} %param.5) | copy-start | bytes 6291460
  17.5 105.2 %all-to-all-start = ((f32[8,2,128,8,64]{2,4,3,1,0:T(8,128)}), f32[8,2,128,8,64]{2,4,3,1,0:T(8,128)}, u32[]{:S(2)}, u32[]{:S(2)}) async-start(f32[8,2,128,8,64]{2,4,3,1,0:T(8,128)} %copy.104), calls=%async_computation | async-start | bytes 8388608 | tf_op jit(solution)/shard_map/all_to_all | solution.py:163
  204.7 2.0 copy-start.2
  204.7 3.4 copy-start.3
  238.3 51.6 %all-to-all-start.1 = ((f32[8,2,128,256]{2,3,1,0:T(8,128)}), f32[8,2,128,256]{2,3,1,0:T(8,128)S(1)}, u32[]{:S(2)}, u32[]{:S(2)}) async-start(f32[8,2,128,256]{2,3,1,0:T(8,128)} %copy.130), calls=%async_computation.1 | async-start | bytes 4194304 | tf_op jit(solution)/shard_map/all_to_all | solution.py:226
  290.0 56.8 %all-to-all-start.2 = ((f32[8,2,128,256]{2,3,1,0:T(8,128)}), f32[8,2,128,256]{2,3,1,0:T(8,128)}, u32[]{:S(2)}, u32[]{:S(2)}) async-start(f32[8,2,128,256]{2,3,1,0:T(8,128)} %copy.141), calls=%async_computation.2 | async-start | bytes 4194304 | tf_op jit(solution)/shard_map/all_to_all | solution.py:226
  322.1 3.3 copy-start
  322.1 5.8 %copy-start.1 = (f32[1,2,1024,1024]{3,2,0,1:T(8,128)}, f32[1,2,1024,1024]{3,2,0,1:T(8,128)S(1)}, u32[]{:S(2)}) copy-start(f32[1,2,1024,1024]{3,2,0,1:T(8,128)S(1)} %get-tuple-element.41) | copy-start | bytes 25165828
  327.9 2.0 copy-start.4
  329.8 24.2 %collective-permute-start = (f32[2,256,256]{1,2,0:T(8,128)S(1)}, f32[2,256,256]{1,2,0:T(8,128)S(1)}, u32[]{:S(2)}, u32[]{:S(2)}) collective-permute-start(f32[2,256,256]{1,2,0:T(8,128)S(1)} %fusion.61), channel_id=1, source_target_pairs={{0,8},{8,16},{16,24},{24,32},{32,40},{40,48},{48,56},{56,64},{64,7... | collective-permute-start | bytes 1572872 | tf_op jit(solution)/shard_map/ppermute | solution.py:20
  346.8 17.8 %slice-start = ((s8[8388608]{0:T(1024)(128)(4,1)}), s8[4194304]{0:T(1024)(128)(4,1)S(1)}, s32[]{:S(2)}) async-start(s8[8388608]{0:T(1024)(128)(4,1)} %bitcast.353), calls=%async_computation.3 | async-start | bytes 8388608
  346.8 17.8 %slice-start.4 = ((s8[8388608]{0:T(1024)(128)(4,1)}), s8[4194304]{0:T(1024)(128)(4,1)S(1)}, s32[]{:S(2)}) async-start(s8[8388608]{0:T(1024)(128)(4,1)} %bitcast.357), calls=%async_computation.7 | async-start | bytes 8388608
  351.6 12.9 %slice-start.1 = ((s8[8388608]{0:T(1024)(128)(4,1)}), s8[4194304]{0:T(1024)(128)(4,1)S(1)}, s32[]{:S(2)}) async-start(s8[8388608]{0:T(1024)(128)(4,1)} %bitcast.353), calls=%async_computation.4 | async-start | bytes 8388608
  351.7 12.9 %slice-start.5 = ((s8[8388608]{0:T(1024)(128)(4,1)}), s8[4194304]{0:T(1024)(128)(4,1)S(1)}, s32[]{:S(2)}) async-start(s8[8388608]{0:T(1024)(128)(4,1)} %bitcast.357), calls=%async_computation.8 | async-start | bytes 8388608
  351.7 12.9 %collective-permute-start.3 = (f32[2,256,256]{1,2,0:T(8,128)S(1)}, f32[2,256,256]{1,2,0:T(8,128)S(1)}, u32[]{:S(2)}, u32[]{:S(2)}) collective-permute-start(f32[2,256,256]{1,2,0:T(8,128)S(1)} %fusion.64), channel_id=1, source_target_pairs={{0,8},{8,16},{16,24},{24,32},{32,40},{40,48},{48,56},{56,64},{64,7... | collective-permute-start | bytes 1572872 | tf_op jit(solution)/shard_map/ppermute | solution.py:20
  359.0 29.2 %collective-permute-start.1 = (f32[2,256,256]{1,2,0:T(8,128)}, f32[2,256,256]{1,2,0:T(8,128)}, u32[]{:S(2)}, u32[]{:S(2)}) collective-permute-start(f32[2,256,256]{1,2,0:T(8,128)} %fusion.66), channel_id=1, source_target_pairs={{0,8},{8,16},{16,24},{24,32},{32,40},{40,48},{48,56},{56,64},{64,7... | collective-permute-start | bytes 1572872 | tf_op jit(solution)/shard_map/ppermute | solution.py:20
  368.2 23.5 %collective-permute-start.4 = (f32[2,256,256]{1,2,0:T(8,128)S(1)}, f32[2,256,256]{1,2,0:T(8,128)}, u32[]{:S(2)}, u32[]{:S(2)}) collective-permute-start(f32[2,256,256]{1,2,0:T(8,128)S(1)} %fusion.65), channel_id=1, source_target_pairs={{0,8},{8,16},{16,24},{24,32},{32,40},{40,48},{48,56},{56,64},{64,7... | collective-permute-start | bytes 1572872 | tf_op jit(solution)/shard_map/ppermute | solution.py:20
  383.2 16.5 %slice-start.6 = ((s8[8388608]{0:T(1024)(128)(4,1)}), s8[4194304]{0:T(1024)(128)(4,1)S(1)}, s32[]{:S(2)}) async-start(s8[8388608]{0:T(1024)(128)(4,1)} %bitcast.359), calls=%async_computation.9 | async-start | bytes 8388608
  388.2 7.3 %copy-start.5 = (f32[2,1024,256,1]{1,2,0,3:T(8,128)S(1)}, f32[2,1024,256,1]{1,2,0,3:T(8,128)}, u32[]{:S(2)}) copy-start(f32[2,1024,256,1]{1,2,0,3:T(8,128)} %reshape.1966) | copy-start | bytes 6291460
  389.5 10.3 %slice-start.7 = ((s8[8388608]{0:T(1024)(128)(4,1)}), s8[4194304]{0:T(1024)(128)(4,1)S(1)}, s32[]{:S(2)}) async-start(s8[8388608]{0:T(1024)(128)(4,1)} %bitcast.359), calls=%async_computation.10 | async-start | bytes 8388608
  389.5 12.9 %collective-permute-start.2 = (f32[2,256,256]{1,2,0:T(8,128)S(1)}, f32[2,256,256]{1,2,0:T(8,128)S(1)}, u32[]{:S(2)}, u32[]{:S(2)}) collective-permute-start(f32[2,256,256]{1,2,0:T(8,128)S(1)} %add.711), channel_id=1, source_target_pairs={{0,8},{8,16},{16,24},{24,32},{32,40},{40,48},{48,56},{56,64},{64,7... | collective-permute-start | bytes 1572872 | tf_op jit(solution)/shard_map/ppermute | solution.py:20
  391.7 8.1 %slice-start.2 = ((s8[8388608]{0:T(1024)(128)(4,1)}), s8[4194304]{0:T(1024)(128)(4,1)S(1)}, s32[]{:S(2)}) async-start(s8[8388608]{0:T(1024)(128)(4,1)} %bitcast.355), calls=%async_computation.5 | async-start | bytes 8388608
  392.9 6.8 %slice-start.3 = ((s8[8388608]{0:T(1024)(128)(4,1)}), s8[4194304]{0:T(1024)(128)(4,1)S(1)}, s32[]{:S(2)}) async-start(s8[8388608]{0:T(1024)(128)(4,1)} %bitcast.355), calls=%async_computation.6 | async-start | bytes 8388608
  393.0 15.0 %collective-permute-start.5 = (f32[2,256,256]{1,2,0:T(8,128)S(1)}, f32[2,256,256]{1,2,0:T(8,128)S(1)}, u32[]{:S(2)}, u32[]{:S(2)}) collective-permute-start(f32[2,256,256]{1,2,0:T(8,128)S(1)} %add.714), channel_id=1, source_target_pairs={{0,8},{8,16},{16,24},{24,32},{32,40},{40,48},{48,56},{56,64},{64,7... | collective-permute-start | bytes 1572872 | tf_op jit(solution)/shard_map/ppermute | solution.py:20

commit v5 on v2

--- a/solution.py
+++ b/solution.py
@@ -89,7 +89,7 @@
     return jnp.stack([even_back[0] - odd_back[1], even_back[1] + odd_back[0]])
 
 
-def middle_kernel(spec_ref, phase_ref, row_ref, column_ref, out_ref):
+def middle_kernel(spec_ref, cos_ref, sin_ref, row_ref, column_ref, out_ref):
     turn_re = row_ref[0] * column_ref[0] - row_ref[1] * column_ref[1]
     turn_im = row_ref[0] * column_ref[1] + row_ref[1] * column_ref[0]
     filtered = []
@@ -99,8 +99,7 @@
         partner = jnp.stack([spec_ref[0, other], -spec_ref[1, other]])
         turn = jnp.stack([turn_re[half], turn_im[half]])
         transformed = post_process(spec, partner, turn)
-        phase = phase_ref[half]
-        filtered.append(complex_mul(transformed, jnp.stack([jnp.cos(phase), jnp.sin(phase)])))
+        filtered.append(complex_mul(transformed, jnp.stack([cos_ref[half], sin_ref[half]])))
     for half in (0, 1):
         other = filtered[1 - half]
         turn = jnp.stack([turn_re[half], turn_im[half]])
@@ -110,6 +109,7 @@
 
 
 def middle(spectrum, phase_rows, row_turn, column_turn):
+    phase_block = pl.BlockSpec((2, TILE_ROWS, spectrum.shape[3]), lambda i: (0, i, 0))
     rows = spectrum.shape[2]
     columns = spectrum.shape[3]
     spec_block = pl.BlockSpec((2, 2, TILE_ROWS, columns), lambda i: (0, 0, i, 0))
@@ -119,12 +119,13 @@
         grid=(rows // TILE_ROWS,),
         in_specs=[
             spec_block,
-            pl.BlockSpec((2, TILE_ROWS, columns), lambda i: (0, i, 0)),
+            phase_block,
+            phase_block,
             pl.BlockSpec((2, 2, TILE_ROWS, 1), lambda i: (0, 0, i, 0)),
             pl.BlockSpec((2, 2, 1, columns), lambda i: (0, 0, 0, 0)),
         ],
         out_specs=spec_block,
-    )(spectrum, phase_rows, row_turn, column_turn)
+    )(spectrum, jnp.cos(phase_rows), jnp.sin(phase_rows), row_turn, column_turn)
 
 
 def per_device(voltage, chirp_phase):

time: 414 us -> 408 us (0.986)
  waiting for transfers between devices: 195 us -> 164 us
  other arithmetic: 49.9 us -> 78.9 us
  Pallas kernels: 15.5 us -> 10.4 us
    all_to_all x1, waiting for transfers between devices: 80.5 us -> 48.9 us  [per_device(): lax.all_to_all(spread, 'fft', split_axis=0, concat_axis=0, tiled=True)]
    sin x0 -> x1, other arithmetic: none -> 31.1 us  [middle(): jnp.sin(phase_rows)]
    pallas_call x1, Pallas kernels: 15.5 us -> 10.4 us  [middle(): pl.pallas_call(middle_kernel, out_shape=jax.ShapeDtypeStruct(spectrum.sha...]
  transfers between devices with their start and end apart: 5 -> 5, of which waited for: 5 -> 5; matrix products, arithmetic and copies ran while one was open for 11% -> 19% of each run, Pallas kernels for 0% -> 0%
where the time goes in v5:
time: 408 us; the launch traced here: 401 us
  waiting for transfers between devices  164 us (40%)
  other arithmetic  78.9 us (19%)
  local copies, waits for them, and re-layouts  69.7 us (17%)
  matrix products  57.4 us (14%)
  starting transfers between devices  20.1 us (5%)
  Pallas kernels  10.4 us (3%)
    all_to_all x1, waiting for transfers between devices, per_device(): lax.all_to_all(packed, 'fft', split_axis=0, concat_axis=0, tiled=True)  73.2 us
    all_to_all x1, waiting for transfers between devices, per_device(): lax.all_to_all(spread, 'fft', split_axis=0, concat_axis=0, tiled=True)  48.9 us
    ppermute x3, waiting for transfers between devices, passed_along(): return lax.ppermute(shard, axis, pairs)  41.6 us
    sin x1, other arithmetic, middle(): jnp.sin(phase_rows)  31.1 us
    dot_general x4, matrix products, sample_block(): return jnp.einsum('prn,pqrm->qmn', arrived, table, precision=HIGH)  17.8 us
    neg x1, other arithmetic, real_table(): -pair[1]  16.8 us
    reshape x4, local copies, waits for them, and re-layouts, per_device(): jnp.einsum('phrkv,phku->hruv', packed, last_table[:, part], precision=HIGH)  13.1 us
    reshape x2, local copies, waits for them, and re-layouts, per_device(): spectrum = spectrum.reshape(2, 2, half_count, columns)  12.9 us
  transfers between devices with their start and end apart: 5, of which 5 were waited for; matrix products, arithmetic and copies ran while one was open for 19% of the time, Pallas kernels for 0%

profile of v5, /device:TPU:16, one launch (start us, length us, event | category | flops | bytes accessed | tf_op | source)
XLA Modules:
  0.0 401.1 jit_solution(10342987912639601532)
XLA Ops:
  0.0 1.0 fusion.105
  1.1 5.0 %fusion.76 = (f32[1,1,256,8,128]{4,2,0,3,1:T(8,128)S(1)}, f32[1,1,256,8,128]{4,2,0,3,1:T(8,128)}, f32[1,1,256,8,128]{4,2,0,3,1:T(8,128)}) fusion(s32[8,128]{1,0:T(8,128)S(1)} %select_select_fusion), kind=kLoop, calls=%fused_computation.99 | loop fusion | flops 3932160 | bytes 3149824 | tf_op jit(solution)/shard_map/sin | solution.py:26
  6.2 1.3 copy.98
  7.7 5.7 %fusion.46 = f32[8,2,128,8,64]{2,4,3,0,1:T(8,128)S(1)} fusion(f32[2,256,8,64,1,1]{1,3,2,0,5,4:T(8,128)} %bitcast.275, f32[1,1,256,8,128]{4,2,0,3,1:T(8,128)} %get-tuple-element.89, f32[1,1,256,8,128]{4,2,0,3,1:T(8,128)} %get-tuple-element.88, f32[1,1,256,8,128]{4,2,0,3,1:T(8,128)S(1)} %get-tuple-element.87), kind=kOutput, calls=%fused_computation.58 | convolution fusion | flops 3224371200 | bytes 8388608 | tf_op jit(solution)/shard_map/pmun,pqmdr->dqrun/dot_general | solution.py:159
  13.4 1.1 multiply_subtract_fusion.3
  14.6 0.6 pad_maximum_fusion.3
  15.2 2.3 copy.100
  17.4 9.1 %all-to-all-start = ((f32[8,2,128,8,64]{2,4,3,1,0:T(8,128)}), f32[8,2,128,8,64]{2,4,3,1,0:T(8,128)}, u32[]{:S(2)}, u32[]{:S(2)}) async-start(f32[8,2,128,8,64]{2,4,3,1,0:T(8,128)} %copy.100), calls=%async_computation | async-start | bytes 8388608 | tf_op jit(solution)/shard_map/all_to_all | solution.py:164
  26.9 0.5 fusion.259
  27.4 0.4 sin.208
  27.9 0.7 broadcast_in_dim.23.column_ref
  28.6 0.8 copy.112.row_ref
  29.5 0.4 fusion.212
  30.7 1.1 copy.108
  32.0 1.2 convolution_bitcast_fusion.1
  33.2 0.6 copy.107
  33.9 31.1 %fusion.74 = (f32[2,64,4096]{2,0,1:T(2,128)S(1)}, f32[2,64,4096]{2,0,1:T(2,128)S(1)}) fusion(f32[1,64,4096]{2,0,1:T(1,128)S(1)} %bitcast.270, f32[1,64,4096]{2,0,1:T(1,128)S(1)} %copy.108), kind=kLoop, calls=%fused_computation.97 | loop fusion | flops 524288 | bytes 6291456 | tf_op jit(solution)/shard_map/sin | solution.py:128
  64.9 2.5 copy.111.sin_ref
  67.5 2.6 copy.110.cos_ref
  70.3 0.3 fusion.196
  70.6 0.3 fusion.200
  71.0 2.5 multiply_subtract_fusion.2
  73.5 0.5 fusion.257
  74.0 48.9 %all-to-all-done = f32[8,2,128,8,64]{2,4,3,1,0:T(8,128)} async-done(((f32[8,2,128,8,64]{2,4,3,1,0:T(8,128)}), f32[8,2,128,8,64]{2,4,3,1,0:T(8,128)}, u32[]{:S(2)}, u32[]{:S(2)}) %all-to-all-start) | async-done | bytes 4194336 | tf_op jit(solution)/shard_map/all_to_all | solution.py:164
  122.9 9.2 %copy.101 = f32[8,2,128,8,64]{4,3,0,1,2:T(8,128)} copy(f32[8,2,128,8,64]{2,4,3,1,0:T(8,128)} %all-to-all-done) | data formatting | bytes 8388608 | tf_op jit(solution)/shard_map/all_to_all | solution.py:164
  132.1 6.4 %convolution_bitcast_fusion = f32[2,2,64,64,64]{4,3,2,0,1:T(8,128)S(1)} fusion(f32[8,2,2,64,8,64,1]{5,4,0,1,3,6,2:T(8,128)} %bitcast.269, f32[1,2,2,8,8,64]{5,4,3,0,1,2:T(8,128)S(1)} %bitcast.276, f32[1,1,1,8,8,64]{5,4,3,0,1,2:T(8,128)S(1)} %get-tuple-element.83, f32[1,1,1,8,8,64]{5,4,3,0,1,2:T(8,128)S(1)} %get-tuple-element.84, ...), kind=kOutput, calls=%fused_computation.55 | convolution fusion | flops 805437440 | bytes 8519680 | tf_op jit(solution)/shard_map/sphrun,pqhsuk->qhrkn/dot_general | solution.py:170
  138.5 2.0 multiply_subtract_fusion.1
  140.5 8.3 %fusion.34 = f32[2,2,64,64,64]{4,3,2,0,1:T(8,128)} fusion(f32[1,2,2,64,64]{3,4,0,1,2:T(8,128)S(1)} %get-tuple-element.60, f32[1,2,2,64,64]{3,4,0,1,2:T(8,128)S(1)} %fusion.97, f32[1,2,64,64,64]{4,3,2,0,1:T(8,128)S(1)} %get-tuple-element.33, f32[1,2,64,64,64]{4,3,2,0,1:T(8,128)S(1)} %get-tuple-element.32), kind=kOutput, calls=%fused_computation.53 | convolution fusion | flops 806387712 | bytes 8519680 | tf_op jit(solution)/shard_map/phrkn,pqhnj->qhrjk/dot_general | solution.py:172
  148.8 8.3 %reshape.1967 = f32[2,2,64,4096]{3,2,0,1:T(8,128)} reshape(f32[2,2,64,64,64]{4,3,2,0,1:T(8,128)} %fusion.34) | data formatting | bytes 8388608 | tf_op jit(solution)/shard_map/reshape | solution.py:173
  157.1 1.1 slice.310
  158.2 1.1 fusion.263
  159.3 4.6 %copy.109.spec_ref = f32[2,2,64,4096]{3,2,1,0:T(8,128)} copy(f32[2,2,64,4096]{3,2,0,1:T(8,128)} %reshape.1967) | data formatting | bytes 8388608 | tf_op jit(solution)/shard_map/reshape | solution.py:173
  165.0 0.5 fusion.162
  166.2 10.4 %shard_map.28 = f32[2,2,64,4096]{3,2,1,0:T(8,128)} custom-call(f32[2,2,64,4096]{3,2,1,0:T(8,128)} %copy.109.spec_ref, f32[2,64,4096]{2,1,0:T(8,128)} %copy.110.cos_ref, f32[2,64,4096]{2,1,0:T(8,128)} %copy.111.sin_ref, f32[2,2,64,1]{3,2,1,0:T(8,128)} %copy.112.row_ref, f32[2,2,1,4096]{3,2,1,0:T(1,128)} %broadcast_in_dim.23.column_ref), custom_call_target="tpu_custom_call" | custom-call | tf_op jit(solution)/shard_map/pallas_call | solution.py:116
  176.6 1.1 slice.335
  178.1 1.9 scatter.4
  180.0 7.9 %reshape.1941 = f32[2,2,64,64,64]{4,3,2,1,0:T(8,128)} reshape(f32[2,2,64,4096]{3,2,1,0:T(8,128)} %scatter.4) | data formatting | bytes 8388608 | tf_op jit(solution)/shard_map/reshape | solution.py:197
  187.9 9.5 %fusion.37 = f32[2,2,64,64,64]{4,3,2,0,1:T(8,128)S(1)} fusion(f32[2,2,64,64,64]{4,3,2,1,0:T(8,128)} %reshape.1941, f32[1,2,2,64,64]{3,4,1,2,0:T(8,128)S(1)} %get-tuple-element.65, f32[1,2,2,64,64]{3,4,1,2,0:T(8,128)S(1)} %get-tuple-element.64), kind=kOutput, calls=%fused_computation.54 | convolution fusion | flops 805339136 | bytes 8519680 | tf_op jit(solution)/shard_map/phrjk,pqhjv->qhrkv/dot_general | solution.py:201
  197.4 2.0 multiply_subtract_fusion
  199.4 3.9 fusion.43
  203.4 4.0 fusion.40
  207.3 3.4 reshape.1942
  210.8 4.8 %reshape.1943 = f32[128,8,512]{2,1,0:T(8,128)} reshape(f32[2,64,64,64]{3,2,1,0:T(8,128)} %fusion.43) | data formatting | bytes 4194304 | tf_op jit(solution)/shard_map/reshape | solution.py:207
  215.5 3.0 copy.124
  218.6 1.9 copy.121
  220.5 3.9 fusion.50
  224.4 0.3 pad_maximum_fusion.4
  224.7 2.3 copy.127
  227.0 4.7 %all-to-all-start.1 = ((f32[8,2,128,512]{2,3,1,0:T(8,128)}), f32[8,2,128,512]{2,3,1,0:T(8,128)}, u32[]{:S(2)}, u32[]{:S(2)}) async-start(f32[8,2,128,512]{2,3,1,0:T(8,128)} %copy.127), calls=%async_computation.1 | async-start | bytes 8388608 | tf_op jit(solution)/shard_map/all_to_all | solution.py:220
  231.7 16.8 %fusion.53 = (f32[1,1024,1024]{1,2,0:T(8,128)S(1)}, f32[1,1024,1024]{1,2,0:T(8,128)S(1)}, f32[1,1024,1024]{1,2,0:T(8,128)S(1)}) fusion(s32[1024]{0:T(1024)S(1)} %select_select_fusion.1), kind=kLoop, calls=%fused_computation.76 | loop fusion | flops 18874368 | bytes 12587008 | tf_op jit(solution)/shard_map/neg | solution.py:34
  248.5 6.7 %maximum_bitcast_fusion.1 = (f32[1,2,1024,1024]{2,3,0,1:T(8,128)}, f32[1,2,1024,1024]{2,3,0,1:T(8,128)}) fusion(f32[1,1024,1024]{1,2,0:T(8,128)S(1)} %get-tuple-element.80, f32[1,1024,1024]{1,2,0:T(8,128)S(1)} %get-tuple-element.78, f32[1,1024,1024]{1,2,0:T(8,128)S(1)} %get-tuple-element.79), kind=kLoop, calls=%fused_computation.7 | loop fusion | flops 4194304 | bytes 29360128 | tf_op jit(solution)/shard_map/stack | solution.py:34
  255.3 73.2 %all-to-all-done.1 = f32[8,2,128,512]{2,3,1,0:T(8,128)} async-done(((f32[8,2,128,512]{2,3,1,0:T(8,128)}), f32[8,2,128,512]{2,3,1,0:T(8,128)}, u32[]{:S(2)}, u32[]{:S(2)}) %all-to-all-start.1) | async-done | bytes 4194336 | tf_op jit(solution)/shard_map/all_to_all | solution.py:220
  328.5 5.4 %copy.128 = f32[2,8,128,512]{3,2,1,0:T(8,128)} copy(f32[2,8,128,512]{2,3,0,1:T(8,128)} %bitcast.83) | data formatting | bytes 8388608 | tf_op jit(solution)/shard_map/transpose | solution.py:221
  333.8 7.2 %fusion.54 = f32[2,256,512]{2,1,0:T(8,128)S(1)} fusion(f32[2,1024,512,1]{2,1,0,3:T(8,128)} %bitcast.265, f32[1,2,1024,1024]{2,3,0,1:T(8,128)} %get-tuple-element.38, f32[1,2,1024,1024]{2,3,0,1:T(8,128)} %get-tuple-element.39), kind=kOutput, calls=%fused_computation.80 | convolution fusion | flops 3222274048 | bytes 22020096 | tf_op jit(solution)/shard_map/prn,pqrm->qmn/dot_general | solution.py:230
  341.0 2.4 collective-permute-start
  343.4 16.1 %collective-permute-done = f32[2,256,512]{2,1,0:T(8,128)S(1)} collective-permute-done((f32[2,256,512]{2,1,0:T(8,128)S(1)}, f32[2,256,512]{2,1,0:T(8,128)S(1)}, u32[]{:S(2)}, u32[]{:S(2)}) %collective-permute-start) | collective-permute-done | bytes 1048608 | tf_op jit(solution)/shard_map/ppermute | solution.py:20
  359.5 3.5 fusion.64
  363.1 1.9 collective-permute-start.1
  365.0 3.5 fusion.55
  368.6 12.7 %collective-permute-done.1 = f32[2,256,512]{2,1,0:T(8,128)S(1)} collective-permute-done((f32[2,256,512]{2,1,0:T(8,128)S(1)}, f32[2,256,512]{2,1,0:T(8,128)S(1)}, u32[]{:S(2)}, u32[]{:S(2)}) %collective-permute-start.1) | collective-permute-done | bytes 1048608 | tf_op jit(solution)/shard_map/ppermute | solution.py:20
  381.5 1.9 collective-permute-start.2
  383.4 3.5 fusion.58
  387.0 12.7 %collective-permute-done.2 = f32[2,256,512]{2,1,0:T(8,128)S(1)} collective-permute-done((f32[2,256,512]{2,1,0:T(8,128)S(1)}, f32[2,256,512]{2,1,0:T(8,128)S(1)}, u32[]{:S(2)}, u32[]{:S(2)}) %collective-permute-start.2) | collective-permute-done | bytes 1048608 | tf_op jit(solution)/shard_map/ppermute | solution.py:20
  399.7 1.2 add_bitcast_fusion
  (79 shorter events, 4.3 us)
Async XLA Ops:
  0.0 6.2 %copy-start.3 = (f32[1,2,256,512]{3,2,1,0:T(8,128)S(1)}, f32[1,2,256,512]{3,2,1,0:T(8,128)}, u32[]{:S(2)}) copy-start(f32[1,2,256,512]{3,2,1,0:T(8,128)} %param.4) | copy-start | bytes 3145732
  17.4 13.1 %copy-start.2 = (f32[2,64,4096]{2,1,0:T(8,128)S(1)}, f32[2,64,4096]{2,1,0:T(8,128)}, u32[]{:S(2)}) copy-start(f32[2,64,4096]{2,1,0:T(8,128)} %param.5) | copy-start | bytes 6291460
  17.4 105.4 %all-to-all-start = ((f32[8,2,128,8,64]{2,4,3,1,0:T(8,128)}), f32[8,2,128,8,64]{2,4,3,1,0:T(8,128)}, u32[]{:S(2)}, u32[]{:S(2)}) async-start(f32[8,2,128,8,64]{2,4,3,1,0:T(8,128)} %copy.100), calls=%async_computation | async-start | bytes 8388608 | tf_op jit(solution)/shard_map/all_to_all | solution.py:164
  227.0 101.5 %all-to-all-start.1 = ((f32[8,2,128,512]{2,3,1,0:T(8,128)}), f32[8,2,128,512]{2,3,1,0:T(8,128)}, u32[]{:S(2)}, u32[]{:S(2)}) async-start(f32[8,2,128,512]{2,3,1,0:T(8,128)} %copy.127), calls=%async_computation.1 | async-start | bytes 8388608 | tf_op jit(solution)/shard_map/all_to_all | solution.py:220
  333.8 25.7 %slice-start = ((s8[8388608]{0:T(1024)(128)(4,1)}), s8[4194304]{0:T(1024)(128)(4,1)S(1)}, s32[]{:S(2)}) async-start(s8[8388608]{0:T(1024)(128)(4,1)} %bitcast.263), calls=%async_computation.2 | async-start | bytes 8388608
  333.8 25.7 %slice-start.1 = ((s8[8388608]{0:T(1024)(128)(4,1)}), s8[4194304]{0:T(1024)(128)(4,1)S(1)}, s32[]{:S(2)}) async-start(s8[8388608]{0:T(1024)(128)(4,1)} %bitcast.263), calls=%async_computation.3 | async-start | bytes 8388608
  333.8 25.7 %copy-start = (f32[1,2,1024,1024]{2,3,0,1:T(8,128)S(1)}, f32[1,2,1024,1024]{2,3,0,1:T(8,128)}, u32[]{:S(2)}) copy-start(f32[1,2,1024,1024]{2,3,0,1:T(8,128)} %get-tuple-element.39) | copy-start | bytes 25165828
  333.8 25.7 %copy-start.1 = (f32[2,8,128,512]{3,2,1,0:T(8,128)S(1)}, f32[2,8,128,512]{3,2,1,0:T(8,128)}, u32[]{:S(2)}) copy-start(f32[2,8,128,512]{3,2,1,0:T(8,128)} %copy.128) | copy-start | bytes 12582916
  341.0 18.5 %collective-permute-start = (f32[2,256,512]{2,1,0:T(8,128)S(1)}, f32[2,256,512]{2,1,0:T(8,128)S(1)}, u32[]{:S(2)}, u32[]{:S(2)}) collective-permute-start(f32[2,256,512]{2,1,0:T(8,128)S(1)} %fusion.54), channel_id=1, source_target_pairs={{0,8},{8,16},{16,24},{24,32},{32,40},{40,48},{48,56},{56,64},{64,7... | collective-permute-start | bytes 3145736 | tf_op jit(solution)/shard_map/ppermute | solution.py:20
  363.1 18.2 %collective-permute-start.1 = (f32[2,256,512]{2,1,0:T(8,128)S(1)}, f32[2,256,512]{2,1,0:T(8,128)S(1)}, u32[]{:S(2)}, u32[]{:S(2)}) collective-permute-start(f32[2,256,512]{2,1,0:T(8,128)S(1)} %fusion.64), channel_id=1, source_target_pairs={{0,8},{8,16},{16,24},{24,32},{32,40},{40,48},{48,56},{56,64},{64,7... | collective-permute-start | bytes 3145736 | tf_op jit(solution)/shard_map/ppermute | solution.py:20
  381.5 18.2 %collective-permute-start.2 = (f32[2,256,512]{2,1,0:T(8,128)S(1)}, f32[2,256,512]{2,1,0:T(8,128)S(1)}, u32[]{:S(2)}, u32[]{:S(2)}) collective-permute-start(f32[2,256,512]{2,1,0:T(8,128)S(1)} %add.702), channel_id=1, source_target_pairs={{0,8},{8,16},{16,24},{24,32},{32,40},{40,48},{48,56},{56,64},{64,7... | collective-permute-start | bytes 3145736 | tf_op jit(solution)/shard_map/ppermute | solution.py:20

commit v6 on v5

--- a/solution.py
+++ b/solution.py
@@ -109,23 +109,30 @@
 
 
 def middle(spectrum, phase_rows, row_turn, column_turn):
-    phase_block = pl.BlockSpec((2, TILE_ROWS, spectrum.shape[3]), lambda i: (0, i, 0))
-    rows = spectrum.shape[2]
-    columns = spectrum.shape[3]
-    spec_block = pl.BlockSpec((2, 2, TILE_ROWS, columns), lambda i: (0, 0, i, 0))
+    shape = spectrum.shape
+    tile = (TILE_ROWS,) + shape[3:]
+    spec_block = pl.BlockSpec((2, 2) + tile, lambda i: (0, 0, i, 0, 0))
+    phase_block = pl.BlockSpec((2,) + tile, lambda i: (0, i, 0, 0))
+    phase_rows = phase_rows.reshape((2,) + shape[2:])
     return pl.pallas_call(
         middle_kernel,
-        out_shape=jax.ShapeDtypeStruct(spectrum.shape, jnp.float32),
-        grid=(rows // TILE_ROWS,),
+        out_shape=jax.ShapeDtypeStruct(shape, jnp.float32),
+        grid=(shape[2] // TILE_ROWS,),
         in_specs=[
             spec_block,
             phase_block,
             phase_block,
-            pl.BlockSpec((2, 2, TILE_ROWS, 1), lambda i: (0, 0, i, 0)),
-            pl.BlockSpec((2, 2, 1, columns), lambda i: (0, 0, 0, 0)),
+            pl.BlockSpec((2, 2, TILE_ROWS, 1, 1), lambda i: (0, 0, i, 0, 0)),
+            pl.BlockSpec((2, 2, 1) + shape[3:], lambda i: (0, 0, 0, 0, 0)),
         ],
         out_specs=spec_block,
-    )(spectrum, jnp.cos(phase_rows), jnp.sin(phase_rows), row_turn, column_turn)
+    )(
+        spectrum,
+        jnp.cos(phase_rows),
+        jnp.sin(phase_rows),
+        row_turn[..., None],
+        column_turn.reshape((2, 2, 1) + shape[3:]),
+    )
 
 
 def per_device(voltage, chirp_phase):
@@ -170,14 +177,13 @@
     gathered = jnp.einsum("sphrun,pqhsuk->qhrkn", gathered, first_blocks, precision=HIGH)
     gathered = complex_mul(gathered, block_turn[:, :, None])
     spectrum = jnp.einsum("phrkn,pqhnj->qhrjk", gathered, real_table(section_two), precision=HIGH)
-    spectrum = spectrum.reshape(2, 2, half_count, columns)
     half_rows = jnp.stack([local_order[:half_count], local_order[half_count:]])
     row_turn = rotation(half_rows, 2 * total_bins)[..., None]
     stored_columns = jnp.stack([column_range, columns - 1 - column_range])
     column_turn = rotation(stored_columns, 2 * columns)[:, :, None, :]
     phase_rows = jnp.stack([chirp_phase[0], reverse_lanes(chirp_phase[1])])
     packed = middle(spectrum, phase_rows, row_turn, column_turn)
-    first_spec = spectrum[:, :, 0]
+    first_spec = spectrum[:, :, 0].reshape(2, 2, columns)
     first_turn = complex_mul(row_turn[:, :, 0], column_turn[:, :, 0])
     live = jnp.stack([column_range > 0, column_range >= 0])
     first_partner = jnp.stack(
@@ -193,8 +199,8 @@
         axis=1,
     )
     first_packed = pre_process(first_filtered, conjugate(first_partner), first_turn)
+    first_packed = first_packed.reshape(2, 2, second_len, B1)
     packed = packed.at[:, :, 0].set(jnp.where(is_first, first_packed, packed[:, :, 0]))
-    packed = packed.reshape(2, 2, half_count, second_len, B1)
     back_two = both_halves(second_range, second_range, second_len, True, False)
     back_turn = both_halves(first_range, second_range, columns, True, False)
     back_one = both_halves(first_range, first_range, B1, True, False)

time: 408 us -> 395 us (0.968)
  other arithmetic: 78.9 us -> 52.8 us
  waiting for transfers between devices: 164 us -> 177 us
  Pallas kernels: 10.4 us -> 17.4 us
  local copies, waits for them, and re-layouts: 69.7 us -> 63.3 us
    sin x1 -> x0, other arithmetic: 31.1 us -> none  [middle(): jnp.sin(phase_rows)]
    reshape x3 -> x0, local copies, waits for them, and re-layouts: 20.8 us -> none  [the longest x2 12.9 us: per_device(): spectrum = spectrum.reshape(2, 2, half_count, columns)]
    all_to_all x1, waiting for transfers between devices: 48.9 us -> 62.2 us  [per_device(): lax.all_to_all(spread, 'fft', split_axis=0, concat_axis=0, tiled=True)]
    sin x1, local copies, waits for them, and re-layouts: 2.54 us -> 15.9 us  [middle(): jnp.sin(phase_rows)]
    pallas_call x1, Pallas kernels: 10.4 us -> 17.4 us  [middle(): pl.pallas_call(middle_kernel, out_shape=jax.ShapeDtypeStruct(shape, jnp.f...]
    unnamed x17 -> x23, local copies, waits for them, and re-layouts: 1.63 us -> 8.24 us
    another operation x1 -> x8, local copies, waits for them, and re-layouts: 0.09 us -> 5.5 us  [the longest x4 4.39 us: per_device(): phase_rows = jnp.stack([chirp_phase[0], reverse_lanes(chirp_phase[1])])]
  transfers between devices with their start and end apart: 5 -> 5, of which waited for: 5 -> 5; matrix products, arithmetic and copies ran while one was open for 19% -> 17% of each run, Pallas kernels for 0% -> 0%
where the time goes in v6:
time: 395 us; the launch traced here: 388 us
  waiting for transfers between devices  177 us (45%)
  local copies, waits for them, and re-layouts  63.3 us (16%)
  matrix products  56.6 us (14%)
  other arithmetic  52.8 us (13%)
  starting transfers between devices  19.8 us (5%)
  Pallas kernels  17.4 us (4%)
    all_to_all x1, waiting for transfers between devices, per_device(): lax.all_to_all(packed, 'fft', split_axis=0, concat_axis=0, tiled=True)  73.2 us
    all_to_all x1, waiting for transfers between devices, per_device(): lax.all_to_all(spread, 'fft', split_axis=0, concat_axis=0, tiled=True)  62.2 us
    ppermute x3, waiting for transfers between devices, passed_along(): return lax.ppermute(shard, axis, pairs)  41.5 us
    dot_general x4, matrix products, sample_block(): return jnp.einsum('prn,pqrm->qmn', arrived, table, precision=HIGH)  17.8 us
    pallas_call x1, Pallas kernels, middle(): pl.pallas_call(middle_kernel, out_shape=jax.ShapeDtypeStruct(shape, jnp.f...  17.4 us
    neg x1, other arithmetic, real_table(): -pair[1]  16.8 us
    sin x1, local copies, waits for them, and re-layouts, middle(): jnp.sin(phase_rows)  15.9 us
    reshape x4, local copies, waits for them, and re-layouts, per_device(): jnp.einsum('phrkv,phku->hruv', packed, last_table[:, part], precision=HIGH)  13.1 us
  transfers between devices with their start and end apart: 5, of which 5 were waited for; matrix products, arithmetic and copies ran while one was open for 17% of the time, Pallas kernels for 0%

profile of v6, /device:TPU:16, one launch (start us, length us, event | category | flops | bytes accessed | tf_op | source)
XLA Modules:
  0.0 388.0 jit_solution(13266156806118813798)
XLA Ops:
  0.0 1.0 fusion.104
  1.1 5.0 %fusion.75 = (f32[1,1,256,8,128]{4,2,0,3,1:T(8,128)S(1)}, f32[1,1,256,8,128]{4,2,0,3,1:T(8,128)}, f32[1,1,256,8,128]{4,2,0,3,1:T(8,128)}) fusion(s32[8,128]{1,0:T(8,128)S(1)} %select_select_fusion), kind=kLoop, calls=%fused_computation.95 | loop fusion | flops 3932160 | bytes 3149824 | tf_op jit(solution)/shard_map/sin | solution.py:26
  6.2 1.3 copy.52
  7.5 0.2 multiply_subtract_fusion.7
  7.7 5.7 %fusion.47 = f32[8,2,128,8,64]{2,4,3,0,1:T(8,128)S(1)} fusion(f32[2,256,8,64,1,1]{1,3,2,0,5,4:T(8,128)} %bitcast.263, f32[1,1,256,8,128]{4,2,0,3,1:T(8,128)} %get-tuple-element.93, f32[1,1,256,8,128]{4,2,0,3,1:T(8,128)} %get-tuple-element.92, f32[1,1,256,8,128]{4,2,0,3,1:T(8,128)S(1)} %get-tuple-element.91), kind=kOutput, calls=%fused_computation.59 | convolution fusion | flops 3224371200 | bytes 8388608 | tf_op jit(solution)/shard_map/pmun,pqmdr->dqrun/dot_general | solution.py:166
  13.4 1.1 multiply_subtract_fusion.3
  14.6 0.6 pad_maximum_fusion.4
  15.2 2.3 copy.54
  17.5 8.7 %all-to-all-start = ((f32[8,2,128,8,64]{2,4,3,1,0:T(8,128)}), f32[8,2,128,8,64]{2,4,3,1,0:T(8,128)}, u32[]{:S(2)}, u32[]{:S(2)}) async-start(f32[8,2,128,8,64]{2,4,3,1,0:T(8,128)} %copy.54), calls=%async_computation | async-start | bytes 8388608 | tf_op jit(solution)/shard_map/all_to_all | solution.py:171
  26.2 1.7 slice_bitcast_fusion
  28.1 1.2 convolution_bitcast_fusion.1
  29.3 0.6 copy.60
  30.1 1.7 stack.341
  32.1 0.8 copy.61.row_ref
  32.9 2.2 stack.340
  35.7 0.4 fusion.212
  36.2 0.3 fusion.237
  36.5 0.7 pad_maximum_fusion.11.column_ref
  37.3 1.7 constant_dynamic-update-slice_fusion.1
  39.1 0.2 constant_dynamic-update-slice_fusion
  39.3 0.3 fusion.196
  39.6 0.3 fusion.200
  40.0 2.6 multiply_subtract_fusion.2
  42.6 0.8 fusion.261
  43.5 0.9 fusion.259
  44.4 15.9 %fusion.265 = (f32[2,64,64,64]{3,2,1,0:T(8,128)}, f32[2,64,64,64]{3,2,1,0:T(8,128)}) fusion(f32[2,64,64,64]{3,2,1,0:T(8,128)S(1)} %constant_dynamic-update-slice_fusion), kind=kLoop, calls=%fused_computation.421 | loop fusion | bytes 6291456 | tf_op jit(solution)/shard_map/sin | solution.py:132
  60.3 62.2 %all-to-all-done = f32[8,2,128,8,64]{2,4,3,1,0:T(8,128)} async-done(((f32[8,2,128,8,64]{2,4,3,1,0:T(8,128)}), f32[8,2,128,8,64]{2,4,3,1,0:T(8,128)}, u32[]{:S(2)}, u32[]{:S(2)}) %all-to-all-start) | async-done | bytes 4194336 | tf_op jit(solution)/shard_map/all_to_all | solution.py:171
  122.5 9.2 %copy.55 = f32[8,2,128,8,64]{4,3,0,1,2:T(8,128)} copy(f32[8,2,128,8,64]{2,4,3,1,0:T(8,128)} %all-to-all-done) | data formatting | bytes 8388608 | tf_op jit(solution)/shard_map/all_to_all | solution.py:171
  131.8 6.9 %convolution_bitcast_fusion = f32[2,2,64,64,64]{4,3,2,0,1:T(8,128)S(1)} fusion(f32[8,2,2,64,8,64,1]{5,4,0,1,3,6,2:T(8,128)} %bitcast.259, f32[1,2,2,8,8,64]{5,4,3,0,1,2:T(8,128)S(1)} %get-tuple-element.63, f32[1,1,1,8,8,64]{5,4,3,0,1,2:T(8,128)S(1)} %get-tuple-element.87, f32[1,1,1,8,8,64]{5,4,3,0,1,2:T(8,128)S(1)} %get-tuple-element.88, ...), kind=kOutput, calls=%fused_computation.55 | convolution fusion | flops 805437440 | bytes 8519680 | tf_op jit(solution)/shard_map/sphrun,pqhsuk->qhrkn/dot_general | solution.py:177
  138.6 2.0 multiply_subtract_fusion.1
  140.7 7.1 %fusion.38.spec_ref = f32[2,2,64,64,64]{4,3,2,1,0:T(8,128)S(1)} fusion(f32[1,2,64,64,64]{4,3,2,0,1:T(8,128)S(1)} %get-tuple-element.37, f32[1,2,64,64,64]{4,3,2,0,1:T(8,128)S(1)} %get-tuple-element.36, f32[1,2,2,64,64]{4,3,1,2,0:T(8,128)S(1)} %get-tuple-element.62, f32[1,2,2,64,64]{4,3,1,2,0:T(8,128)S(1)} %fusion.95), kind=kOutput, calls=%fused_computation.56 | convolution fusion | flops 806387712 | bytes 8519680 | tf_op jit(solution)/shard_map/phrkn,pqhnj->qhrjk/dot_general | solution.py:179
  147.8 3.2 copy-done.2
  152.0 1.0 multiply_subtract_fusion.5
  153.3 0.9 fusion.161
  155.2 0.3 fusion.158
  155.7 17.4 %shard_map.28 = f32[2,2,64,64,64]{4,3,2,1,0:T(8,128)} custom-call(f32[2,2,64,64,64]{4,3,2,1,0:T(8,128)} %copy-done.2, f32[2,64,64,64]{3,2,1,0:T(8,128)} %get-tuple-element.47.cos_ref, f32[2,64,64,64]{3,2,1,0:T(8,128)} %get-tuple-element.46.sin_ref, f32[2,2,64,1,1]{4,3,2,1,0:T(1,128)} %copy.61.row_ref, f32[2,2,1,64,64]{4,3,2,1,0:T(8,128)} %pad_maximum_fusion.11.column_ref), custom_call_target="tpu_custom_call" | custom-call | tf_op jit(solution)/shard_map/pallas_call | solution.py:117
  173.1 1.6 fusion.100
  174.7 9.4 %fusion.35 = f32[2,2,64,64,64]{4,3,2,0,1:T(8,128)S(1)} fusion(f32[2,2,64,64,64]{4,3,2,1,0:T(8,128)} %fusion.100, f32[1,2,2,64,64]{4,3,1,2,0:T(8,128)S(1)} %get-tuple-element.67, f32[1,2,2,64,64]{4,3,1,2,0:T(8,128)S(1)} %get-tuple-element.66), kind=kOutput, calls=%fused_computation.54 | convolution fusion | flops 805339136 | bytes 8519680 | tf_op jit(solution)/shard_map/phrjk,pqhjv->qhrkv/dot_general | solution.py:207
  184.1 2.0 multiply_subtract_fusion
  186.1 3.9 %fusion.44 = f32[2,64,64,64]{3,2,1,0:T(8,128)} fusion(f32[2,2,64,64,1]{3,2,1,0,4:T(8,128)S(1)} %get-tuple-element.50, f32[1,2,64,64,64]{4,3,2,0,1:T(8,128)S(1)} %get-tuple-element.35, f32[1,2,64,64,64]{4,3,2,0,1:T(8,128)S(1)} %get-tuple-element.34), kind=kOutput, calls=%fused_computation.58 | convolution fusion | flops 403701760 | bytes 6356992 | tf_op jit(solution)/shard_map/phrkv,phku->hruv/dot_general | solution.py:213
  190.0 4.0 %fusion.41 = f32[2,64,64,64]{3,2,1,0:T(8,128)} fusion(f32[2,2,64,64,1]{3,2,1,0,4:T(8,128)S(1)} %get-tuple-element.51, f32[1,2,64,64,64]{4,3,2,0,1:T(8,128)S(1)} %get-tuple-element.35, f32[1,2,64,64,64]{4,3,2,0,1:T(8,128)S(1)} %get-tuple-element.34), kind=kOutput, calls=%fused_computation.57 | convolution fusion | flops 403701760 | bytes 6356992 | tf_op jit(solution)/shard_map/phrkv,phku->hruv/dot_general | solution.py:213
  194.0 3.4 reshape.2051
  197.4 4.8 %reshape.2052 = f32[128,8,512]{2,1,0:T(8,128)} reshape(f32[2,64,64,64]{3,2,1,0:T(8,128)} %fusion.44) | data formatting | bytes 4194304 | tf_op jit(solution)/shard_map/reshape | solution.py:213
  202.2 3.0 copy.74
  205.2 1.9 copy.71
  207.1 3.9 %fusion.51 = (f32[8,1,128,512]{2,3,0,1:T(8,128)S(1)}, f32[8,1,128,512]{2,3,0,1:T(8,128)S(1)}) fusion(f32[128,8,512]{0,2,1:T(8,128)} %copy.74, f32[128,8,512]{0,2,1:T(8,128)} %copy.71, f32[128,8,512]{0,2,1:T(8,128)} %bitcast.261, f32[128,8,512]{0,2,1:T(8,128)} %bitcast.260), kind=kLoop, calls=%fused_computation.63 | loop fusion | flops 3145728 | bytes 12582912 | tf_op jit(solution)/shard_map/stack | solution.py:225
  211.0 0.3 pad_maximum_fusion.5
  211.3 2.3 copy.77
  213.6 4.8 %all-to-all-start.1 = ((f32[8,2,128,512]{2,3,1,0:T(8,128)}), f32[8,2,128,512]{2,3,1,0:T(8,128)}, u32[]{:S(2)}, u32[]{:S(2)}) async-start(f32[8,2,128,512]{2,3,1,0:T(8,128)} %copy.77), calls=%async_computation.1 | async-start | bytes 8388608 | tf_op jit(solution)/shard_map/all_to_all | solution.py:226
  218.4 16.8 %fusion.54 = (f32[1,1024,1024]{1,2,0:T(8,128)S(1)}, f32[1,1024,1024]{1,2,0:T(8,128)S(1)}, f32[1,1024,1024]{1,2,0:T(8,128)S(1)}) fusion(s32[1024]{0:T(1024)S(1)} %select_select_fusion.1), kind=kLoop, calls=%fused_computation.74 | loop fusion | flops 18874368 | bytes 12587008 | tf_op jit(solution)/shard_map/neg | solution.py:34
  235.2 6.7 %maximum_bitcast_fusion.1 = (f32[1,2,1024,1024]{2,3,0,1:T(8,128)}, f32[1,2,1024,1024]{2,3,0,1:T(8,128)}) fusion(f32[1,1024,1024]{1,2,0:T(8,128)S(1)} %get-tuple-element.84, f32[1,1024,1024]{1,2,0:T(8,128)S(1)} %get-tuple-element.82, f32[1,1024,1024]{1,2,0:T(8,128)S(1)} %get-tuple-element.83), kind=kLoop, calls=%fused_computation.7 | loop fusion | flops 4194304 | bytes 29360128 | tf_op jit(solution)/shard_map/stack | solution.py:34
  241.9 73.2 %all-to-all-done.1 = f32[8,2,128,512]{2,3,1,0:T(8,128)} async-done(((f32[8,2,128,512]{2,3,1,0:T(8,128)}), f32[8,2,128,512]{2,3,1,0:T(8,128)}, u32[]{:S(2)}, u32[]{:S(2)}) %all-to-all-start.1) | async-done | bytes 4194336 | tf_op jit(solution)/shard_map/all_to_all | solution.py:226
  315.1 5.4 %copy.78 = f32[2,8,128,512]{3,2,1,0:T(8,128)} copy(f32[2,8,128,512]{2,3,0,1:T(8,128)} %bitcast.76) | data formatting | bytes 8388608 | tf_op jit(solution)/shard_map/transpose | solution.py:227
  320.5 7.2 %fusion.55 = f32[2,256,512]{2,1,0:T(8,128)S(1)} fusion(f32[2,1024,512,1]{2,1,0,3:T(8,128)} %bitcast.255, f32[1,2,1024,1024]{2,3,0,1:T(8,128)} %get-tuple-element.44, f32[1,2,1024,1024]{2,3,0,1:T(8,128)} %get-tuple-element.45), kind=kOutput, calls=%fused_computation.78 | convolution fusion | flops 3222274048 | bytes 22020096 | tf_op jit(solution)/shard_map/prn,pqrm->qmn/dot_general | solution.py:236
  327.7 2.4 collective-permute-start
  330.1 16.0 %collective-permute-done = f32[2,256,512]{2,1,0:T(8,128)S(1)} collective-permute-done((f32[2,256,512]{2,1,0:T(8,128)S(1)}, f32[2,256,512]{2,1,0:T(8,128)S(1)}, u32[]{:S(2)}, u32[]{:S(2)}) %collective-permute-start) | collective-permute-done | bytes 1048608 | tf_op jit(solution)/shard_map/ppermute | solution.py:20
  346.2 3.5 fusion.65
  349.8 1.9 collective-permute-start.1
  351.7 3.5 fusion.56
  355.2 12.7 %collective-permute-done.1 = f32[2,256,512]{2,1,0:T(8,128)S(1)} collective-permute-done((f32[2,256,512]{2,1,0:T(8,128)S(1)}, f32[2,256,512]{2,1,0:T(8,128)S(1)}, u32[]{:S(2)}, u32[]{:S(2)}) %collective-permute-start.1) | collective-permute-done | bytes 1048608 | tf_op jit(solution)/shard_map/ppermute | solution.py:20
  368.2 1.9 collective-permute-start.2
  370.1 3.5 fusion.59
  373.7 12.7 %collective-permute-done.2 = f32[2,256,512]{2,1,0:T(8,128)S(1)} collective-permute-done((f32[2,256,512]{2,1,0:T(8,128)S(1)}, f32[2,256,512]{2,1,0:T(8,128)S(1)}, u32[]{:S(2)}, u32[]{:S(2)}) %collective-permute-start.2) | collective-permute-done | bytes 1048608 | tf_op jit(solution)/shard_map/ppermute | solution.py:20
  386.4 1.2 add_bitcast_fusion
  (79 shorter events, 4.0 us)
Async XLA Ops:
  0.0 6.2 %copy-start.4 = (f32[1,2,256,512]{3,2,1,0:T(8,128)S(1)}, f32[1,2,256,512]{3,2,1,0:T(8,128)}, u32[]{:S(2)}) copy-start(f32[1,2,256,512]{3,2,1,0:T(8,128)} %param.4) | copy-start | bytes 3145732
  17.5 105.1 %all-to-all-start = ((f32[8,2,128,8,64]{2,4,3,1,0:T(8,128)}), f32[8,2,128,8,64]{2,4,3,1,0:T(8,128)}, u32[]{:S(2)}, u32[]{:S(2)}) async-start(f32[8,2,128,8,64]{2,4,3,1,0:T(8,128)} %copy.54), calls=%async_computation | async-start | bytes 8388608 | tf_op jit(solution)/shard_map/all_to_all | solution.py:171
  35.2 3.9 %copy-start.3 = (f32[1,64,64,64]{3,2,1,0:T(8,128)S(1)}, f32[1,64,64,64]{3,2,1,0:T(8,128)}, u32[]{:S(2)}) copy-start(f32[1,64,64,64]{3,2,1,0:T(8,128)} %stack.341) | copy-start | bytes 3145732
  147.8 3.3 copy-start.2
  213.6 101.5 %all-to-all-start.1 = ((f32[8,2,128,512]{2,3,1,0:T(8,128)}), f32[8,2,128,512]{2,3,1,0:T(8,128)}, u32[]{:S(2)}, u32[]{:S(2)}) async-start(f32[8,2,128,512]{2,3,1,0:T(8,128)} %copy.77), calls=%async_computation.1 | async-start | bytes 8388608 | tf_op jit(solution)/shard_map/all_to_all | solution.py:226
  320.5 25.7 %slice-start = ((s8[8388608]{0:T(1024)(128)(4,1)}), s8[4194304]{0:T(1024)(128)(4,1)S(1)}, s32[]{:S(2)}) async-start(s8[8388608]{0:T(1024)(128)(4,1)} %bitcast.253), calls=%async_computation.2 | async-start | bytes 8388608
  320.5 25.7 %slice-start.1 = ((s8[8388608]{0:T(1024)(128)(4,1)}), s8[4194304]{0:T(1024)(128)(4,1)S(1)}, s32[]{:S(2)}) async-start(s8[8388608]{0:T(1024)(128)(4,1)} %bitcast.253), calls=%async_computation.3 | async-start | bytes 8388608
  320.5 25.7 %copy-start = (f32[1,2,1024,1024]{2,3,0,1:T(8,128)S(1)}, f32[1,2,1024,1024]{2,3,0,1:T(8,128)}, u32[]{:S(2)}) copy-start(f32[1,2,1024,1024]{2,3,0,1:T(8,128)} %get-tuple-element.45) | copy-start | bytes 25165828
  320.5 25.7 %copy-start.1 = (f32[2,8,128,512]{3,2,1,0:T(8,128)S(1)}, f32[2,8,128,512]{3,2,1,0:T(8,128)}, u32[]{:S(2)}) copy-start(f32[2,8,128,512]{3,2,1,0:T(8,128)} %copy.78) | copy-start | bytes 12582916
  327.7 18.5 %collective-permute-start = (f32[2,256,512]{2,1,0:T(8,128)S(1)}, f32[2,256,512]{2,1,0:T(8,128)S(1)}, u32[]{:S(2)}, u32[]{:S(2)}) collective-permute-start(f32[2,256,512]{2,1,0:T(8,128)S(1)} %fusion.55), channel_id=1, source_target_pairs={{0,8},{8,16},{16,24},{24,32},{32,40},{40,48},{48,56},{56,64},{64,7... | collective-permute-start | bytes 3145736 | tf_op jit(solution)/shard_map/ppermute | solution.py:20
  349.8 18.2 %collective-permute-start.1 = (f32[2,256,512]{2,1,0:T(8,128)S(1)}, f32[2,256,512]{2,1,0:T(8,128)S(1)}, u32[]{:S(2)}, u32[]{:S(2)}) collective-permute-start(f32[2,256,512]{2,1,0:T(8,128)S(1)} %fusion.65), channel_id=1, source_target_pairs={{0,8},{8,16},{16,24},{24,32},{32,40},{40,48},{48,56},{56,64},{64,7... | collective-permute-start | bytes 3145736 | tf_op jit(solution)/shard_map/ppermute | solution.py:20
  368.2 18.2 %collective-permute-start.2 = (f32[2,256,512]{2,1,0:T(8,128)S(1)}, f32[2,256,512]{2,1,0:T(8,128)S(1)}, u32[]{:S(2)}, u32[]{:S(2)}) collective-permute-start(f32[2,256,512]{2,1,0:T(8,128)S(1)} %add.742), channel_id=1, source_target_pairs={{0,8},{8,16},{16,24},{24,32},{32,40},{40,48},{48,56},{56,64},{64,7... | collective-permute-start | bytes 3145736 | tf_op jit(solution)/shard_map/ppermute | solution.py:20

commit v7 on v6

--- a/solution.py
+++ b/solution.py
@@ -7,7 +7,7 @@
 from jax.sharding import PartitionSpec as P
 
 B1 = 64
-TILE_ROWS = 8
+TILE_ROWS = 16
 
 
 HIGHEST = lax.Precision.HIGHEST

time: 395 us -> 396 us (level)
  no operation moved by 1% of the time
where the time goes in v7:
time: 396 us; the launch traced here: 389 us
  waiting for transfers between devices  177 us (45%)
  local copies, waits for them, and re-layouts  63.3 us (16%)
  matrix products  56.3 us (14%)
  other arithmetic  52.8 us (13%)
  starting transfers between devices  19.9 us (5%)
  Pallas kernels  18.9 us (5%)
    all_to_all x1, waiting for transfers between devices, per_device(): lax.all_to_all(packed, 'fft', split_axis=0, concat_axis=0, tiled=True)  73.2 us
    all_to_all x1, waiting for transfers between devices, per_device(): lax.all_to_all(spread, 'fft', split_axis=0, concat_axis=0, tiled=True)  62.2 us
    ppermute x3, waiting for transfers between devices, passed_along(): return lax.ppermute(shard, axis, pairs)  41.6 us
    pallas_call x1, Pallas kernels, middle(): pl.pallas_call(middle_kernel, out_shape=jax.ShapeDtypeStruct(shape, jnp.f...  18.9 us
    dot_general x4, matrix products, sample_block(): return jnp.einsum('prn,pqrm->qmn', arrived, table, precision=HIGH)  17.8 us
    neg x1, other arithmetic, real_table(): -pair[1]  16.8 us
    sin x1, local copies, waits for them, and re-layouts, middle(): jnp.sin(phase_rows)  15.9 us
    reshape x4, local copies, waits for them, and re-layouts, per_device(): jnp.einsum('phrkv,phku->hruv', packed, last_table[:, part], precision=HIGH)  13.1 us
  transfers between devices with their start and end apart: 5, of which 5 were waited for; matrix products, arithmetic and copies ran while one was open for 17% of the time, Pallas kernels for 0%

profile of v7, /device:TPU:16, one launch (start us, length us, event | category | flops | bytes accessed | tf_op | source)
XLA Modules:
  0.0 389.3 jit_solution(2477219093566017181)
XLA Ops:
  0.0 1.0 fusion.104
  1.1 5.0 %fusion.75 = (f32[1,1,256,8,128]{4,2,0,3,1:T(8,128)S(1)}, f32[1,1,256,8,128]{4,2,0,3,1:T(8,128)}, f32[1,1,256,8,128]{4,2,0,3,1:T(8,128)}) fusion(s32[8,128]{1,0:T(8,128)S(1)} %select_select_fusion), kind=kLoop, calls=%fused_computation.95 | loop fusion | flops 3932160 | bytes 3149824 | tf_op jit(solution)/shard_map/sin | solution.py:26
  6.2 1.3 copy.52
  7.5 0.2 multiply_subtract_fusion.7
  7.7 5.7 %fusion.47 = f32[8,2,128,8,64]{2,4,3,0,1:T(8,128)S(1)} fusion(f32[2,256,8,64,1,1]{1,3,2,0,5,4:T(8,128)} %bitcast.263, f32[1,1,256,8,128]{4,2,0,3,1:T(8,128)} %get-tuple-element.93, f32[1,1,256,8,128]{4,2,0,3,1:T(8,128)} %get-tuple-element.92, f32[1,1,256,8,128]{4,2,0,3,1:T(8,128)S(1)} %get-tuple-element.91), kind=kOutput, calls=%fused_computation.59 | convolution fusion | flops 3224371200 | bytes 8388608 | tf_op jit(solution)/shard_map/pmun,pqmdr->dqrun/dot_general | solution.py:166
  13.4 1.1 multiply_subtract_fusion.3
  14.6 0.6 pad_maximum_fusion.4
  15.2 2.3 copy.54
  17.5 9.0 %all-to-all-start = ((f32[8,2,128,8,64]{2,4,3,1,0:T(8,128)}), f32[8,2,128,8,64]{2,4,3,1,0:T(8,128)}, u32[]{:S(2)}, u32[]{:S(2)}) async-start(f32[8,2,128,8,64]{2,4,3,1,0:T(8,128)} %copy.54), calls=%async_computation | async-start | bytes 8388608 | tf_op jit(solution)/shard_map/all_to_all | solution.py:171
  26.4 1.7 slice_bitcast_fusion
  28.3 1.2 convolution_bitcast_fusion.1
  29.6 0.6 copy.60
  30.4 1.7 stack.341
  32.4 0.8 copy.61.row_ref
  33.2 2.2 stack.340
  36.0 0.4 fusion.212
  36.4 0.3 fusion.237
  36.7 0.7 pad_maximum_fusion.11.column_ref
  37.6 1.7 constant_dynamic-update-slice_fusion.1
  39.3 0.2 constant_dynamic-update-slice_fusion
  39.6 0.3 fusion.196
  39.9 0.3 fusion.200
  40.2 2.6 multiply_subtract_fusion.2
  42.9 0.8 fusion.261
  43.7 0.9 fusion.259
  44.7 15.9 %fusion.265 = (f32[2,64,64,64]{3,2,1,0:T(8,128)}, f32[2,64,64,64]{3,2,1,0:T(8,128)}) fusion(f32[2,64,64,64]{3,2,1,0:T(8,128)S(1)} %constant_dynamic-update-slice_fusion), kind=kLoop, calls=%fused_computation.421 | loop fusion | bytes 6291456 | tf_op jit(solution)/shard_map/sin | solution.py:132
  60.5 62.2 %all-to-all-done = f32[8,2,128,8,64]{2,4,3,1,0:T(8,128)} async-done(((f32[8,2,128,8,64]{2,4,3,1,0:T(8,128)}), f32[8,2,128,8,64]{2,4,3,1,0:T(8,128)}, u32[]{:S(2)}, u32[]{:S(2)}) %all-to-all-start) | async-done | bytes 4194336 | tf_op jit(solution)/shard_map/all_to_all | solution.py:171
  122.8 9.2 %copy.55 = f32[8,2,128,8,64]{4,3,0,1,2:T(8,128)} copy(f32[8,2,128,8,64]{2,4,3,1,0:T(8,128)} %all-to-all-done) | data formatting | bytes 8388608 | tf_op jit(solution)/shard_map/all_to_all | solution.py:171
  132.0 6.6 %convolution_bitcast_fusion = f32[2,2,64,64,64]{4,3,2,0,1:T(8,128)S(1)} fusion(f32[8,2,2,64,8,64,1]{5,4,0,1,3,6,2:T(8,128)} %bitcast.259, f32[1,2,2,8,8,64]{5,4,3,0,1,2:T(8,128)S(1)} %get-tuple-element.63, f32[1,1,1,8,8,64]{5,4,3,0,1,2:T(8,128)S(1)} %get-tuple-element.87, f32[1,1,1,8,8,64]{5,4,3,0,1,2:T(8,128)S(1)} %get-tuple-element.88, ...), kind=kOutput, calls=%fused_computation.55 | convolution fusion | flops 805437440 | bytes 8519680 | tf_op jit(solution)/shard_map/sphrun,pqhsuk->qhrkn/dot_general | solution.py:177
  138.6 2.0 multiply_subtract_fusion.1
  140.6 7.1 %fusion.38.spec_ref = f32[2,2,64,64,64]{4,3,2,1,0:T(8,128)S(1)} fusion(f32[1,2,64,64,64]{4,3,2,0,1:T(8,128)S(1)} %get-tuple-element.37, f32[1,2,64,64,64]{4,3,2,0,1:T(8,128)S(1)} %get-tuple-element.36, f32[1,2,2,64,64]{4,3,1,2,0:T(8,128)S(1)} %get-tuple-element.62, f32[1,2,2,64,64]{4,3,1,2,0:T(8,128)S(1)} %fusion.95), kind=kOutput, calls=%fused_computation.56 | convolution fusion | flops 806387712 | bytes 8519680 | tf_op jit(solution)/shard_map/phrkn,pqhnj->qhrjk/dot_general | solution.py:179
  147.7 3.2 copy-done.2
  152.0 1.0 multiply_subtract_fusion.5
  153.2 0.9 fusion.161
  155.1 0.3 fusion.158
  155.6 18.9 %shard_map.28 = f32[2,2,64,64,64]{4,3,2,1,0:T(8,128)} custom-call(f32[2,2,64,64,64]{4,3,2,1,0:T(8,128)} %copy-done.2, f32[2,64,64,64]{3,2,1,0:T(8,128)} %get-tuple-element.47.cos_ref, f32[2,64,64,64]{3,2,1,0:T(8,128)} %get-tuple-element.46.sin_ref, f32[2,2,64,1,1]{4,3,2,1,0:T(1,128)} %copy.61.row_ref, f32[2,2,1,64,64]{4,3,2,1,0:T(8,128)} %pad_maximum_fusion.11.column_ref), custom_call_target="tpu_custom_call" | custom-call | tf_op jit(solution)/shard_map/pallas_call | solution.py:117
  174.6 1.6 fusion.100
  176.2 9.4 %fusion.35 = f32[2,2,64,64,64]{4,3,2,0,1:T(8,128)S(1)} fusion(f32[2,2,64,64,64]{4,3,2,1,0:T(8,128)} %fusion.100, f32[1,2,2,64,64]{4,3,1,2,0:T(8,128)S(1)} %get-tuple-element.67, f32[1,2,2,64,64]{4,3,1,2,0:T(8,128)S(1)} %get-tuple-element.66), kind=kOutput, calls=%fused_computation.54 | convolution fusion | flops 805339136 | bytes 8519680 | tf_op jit(solution)/shard_map/phrjk,pqhjv->qhrkv/dot_general | solution.py:207
  185.5 2.0 multiply_subtract_fusion
  187.6 3.9 %fusion.44 = f32[2,64,64,64]{3,2,1,0:T(8,128)} fusion(f32[2,2,64,64,1]{3,2,1,0,4:T(8,128)S(1)} %get-tuple-element.50, f32[1,2,64,64,64]{4,3,2,0,1:T(8,128)S(1)} %get-tuple-element.35, f32[1,2,64,64,64]{4,3,2,0,1:T(8,128)S(1)} %get-tuple-element.34), kind=kOutput, calls=%fused_computation.58 | convolution fusion | flops 403701760 | bytes 6356992 | tf_op jit(solution)/shard_map/phrkv,phku->hruv/dot_general | solution.py:213
  191.5 4.0 %fusion.41 = f32[2,64,64,64]{3,2,1,0:T(8,128)} fusion(f32[2,2,64,64,1]{3,2,1,0,4:T(8,128)S(1)} %get-tuple-element.51, f32[1,2,64,64,64]{4,3,2,0,1:T(8,128)S(1)} %get-tuple-element.35, f32[1,2,64,64,64]{4,3,2,0,1:T(8,128)S(1)} %get-tuple-element.34), kind=kOutput, calls=%fused_computation.57 | convolution fusion | flops 403701760 | bytes 6356992 | tf_op jit(solution)/shard_map/phrkv,phku->hruv/dot_general | solution.py:213
  195.5 3.4 reshape.2051
  198.9 4.8 %reshape.2052 = f32[128,8,512]{2,1,0:T(8,128)} reshape(f32[2,64,64,64]{3,2,1,0:T(8,128)} %fusion.44) | data formatting | bytes 4194304 | tf_op jit(solution)/shard_map/reshape | solution.py:213
  203.7 3.0 copy.74
  206.7 1.9 copy.71
  208.6 3.9 %fusion.51 = (f32[8,1,128,512]{2,3,0,1:T(8,128)S(1)}, f32[8,1,128,512]{2,3,0,1:T(8,128)S(1)}) fusion(f32[128,8,512]{0,2,1:T(8,128)} %copy.74, f32[128,8,512]{0,2,1:T(8,128)} %copy.71, f32[128,8,512]{0,2,1:T(8,128)} %bitcast.261, f32[128,8,512]{0,2,1:T(8,128)} %bitcast.260), kind=kLoop, calls=%fused_computation.63 | loop fusion | flops 3145728 | bytes 12582912 | tf_op jit(solution)/shard_map/stack | solution.py:225
  212.5 0.3 pad_maximum_fusion.5
  212.8 2.3 copy.77
  215.1 4.7 %all-to-all-start.1 = ((f32[8,2,128,512]{2,3,1,0:T(8,128)}), f32[8,2,128,512]{2,3,1,0:T(8,128)}, u32[]{:S(2)}, u32[]{:S(2)}) async-start(f32[8,2,128,512]{2,3,1,0:T(8,128)} %copy.77), calls=%async_computation.1 | async-start | bytes 8388608 | tf_op jit(solution)/shard_map/all_to_all | solution.py:226
  219.8 16.8 %fusion.54 = (f32[1,1024,1024]{1,2,0:T(8,128)S(1)}, f32[1,1024,1024]{1,2,0:T(8,128)S(1)}, f32[1,1024,1024]{1,2,0:T(8,128)S(1)}) fusion(s32[1024]{0:T(1024)S(1)} %select_select_fusion.1), kind=kLoop, calls=%fused_computation.74 | loop fusion | flops 18874368 | bytes 12587008 | tf_op jit(solution)/shard_map/neg | solution.py:34
  236.6 6.7 %maximum_bitcast_fusion.1 = (f32[1,2,1024,1024]{2,3,0,1:T(8,128)}, f32[1,2,1024,1024]{2,3,0,1:T(8,128)}) fusion(f32[1,1024,1024]{1,2,0:T(8,128)S(1)} %get-tuple-element.84, f32[1,1024,1024]{1,2,0:T(8,128)S(1)} %get-tuple-element.82, f32[1,1024,1024]{1,2,0:T(8,128)S(1)} %get-tuple-element.83), kind=kLoop, calls=%fused_computation.7 | loop fusion | flops 4194304 | bytes 29360128 | tf_op jit(solution)/shard_map/stack | solution.py:34
  243.4 73.2 %all-to-all-done.1 = f32[8,2,128,512]{2,3,1,0:T(8,128)} async-done(((f32[8,2,128,512]{2,3,1,0:T(8,128)}), f32[8,2,128,512]{2,3,1,0:T(8,128)}, u32[]{:S(2)}, u32[]{:S(2)}) %all-to-all-start.1) | async-done | bytes 4194336 | tf_op jit(solution)/shard_map/all_to_all | solution.py:226
  316.6 5.4 %copy.78 = f32[2,8,128,512]{3,2,1,0:T(8,128)} copy(f32[2,8,128,512]{2,3,0,1:T(8,128)} %bitcast.76) | data formatting | bytes 8388608 | tf_op jit(solution)/shard_map/transpose | solution.py:227
  321.9 7.2 %fusion.55 = f32[2,256,512]{2,1,0:T(8,128)S(1)} fusion(f32[2,1024,512,1]{2,1,0,3:T(8,128)} %bitcast.255, f32[1,2,1024,1024]{2,3,0,1:T(8,128)} %get-tuple-element.44, f32[1,2,1024,1024]{2,3,0,1:T(8,128)} %get-tuple-element.45), kind=kOutput, calls=%fused_computation.78 | convolution fusion | flops 3222274048 | bytes 22020096 | tf_op jit(solution)/shard_map/prn,pqrm->qmn/dot_general | solution.py:236
  329.1 2.4 collective-permute-start
  331.5 16.1 %collective-permute-done = f32[2,256,512]{2,1,0:T(8,128)S(1)} collective-permute-done((f32[2,256,512]{2,1,0:T(8,128)S(1)}, f32[2,256,512]{2,1,0:T(8,128)S(1)}, u32[]{:S(2)}, u32[]{:S(2)}) %collective-permute-start) | collective-permute-done | bytes 1048608 | tf_op jit(solution)/shard_map/ppermute | solution.py:20
  347.6 3.5 fusion.65
  351.2 1.9 collective-permute-start.1
  353.1 3.5 fusion.56
  356.7 12.7 %collective-permute-done.1 = f32[2,256,512]{2,1,0:T(8,128)S(1)} collective-permute-done((f32[2,256,512]{2,1,0:T(8,128)S(1)}, f32[2,256,512]{2,1,0:T(8,128)S(1)}, u32[]{:S(2)}, u32[]{:S(2)}) %collective-permute-start.1) | collective-permute-done | bytes 1048608 | tf_op jit(solution)/shard_map/ppermute | solution.py:20
  369.6 1.9 collective-permute-start.2
  371.6 3.5 fusion.59
  375.1 12.7 %collective-permute-done.2 = f32[2,256,512]{2,1,0:T(8,128)S(1)} collective-permute-done((f32[2,256,512]{2,1,0:T(8,128)S(1)}, f32[2,256,512]{2,1,0:T(8,128)S(1)}, u32[]{:S(2)}, u32[]{:S(2)}) %collective-permute-start.2) | collective-permute-done | bytes 1048608 | tf_op jit(solution)/shard_map/ppermute | solution.py:20
  387.9 1.2 add_bitcast_fusion
  (79 shorter events, 4.0 us)
Async XLA Ops:
  0.0 6.2 %copy-start.4 = (f32[1,2,256,512]{3,2,1,0:T(8,128)S(1)}, f32[1,2,256,512]{3,2,1,0:T(8,128)}, u32[]{:S(2)}) copy-start(f32[1,2,256,512]{3,2,1,0:T(8,128)} %param.4) | copy-start | bytes 3145732
  17.5 105.3 %all-to-all-start = ((f32[8,2,128,8,64]{2,4,3,1,0:T(8,128)}), f32[8,2,128,8,64]{2,4,3,1,0:T(8,128)}, u32[]{:S(2)}, u32[]{:S(2)}) async-start(f32[8,2,128,8,64]{2,4,3,1,0:T(8,128)} %copy.54), calls=%async_computation | async-start | bytes 8388608 | tf_op jit(solution)/shard_map/all_to_all | solution.py:171
  35.4 3.9 %copy-start.3 = (f32[1,64,64,64]{3,2,1,0:T(8,128)S(1)}, f32[1,64,64,64]{3,2,1,0:T(8,128)}, u32[]{:S(2)}) copy-start(f32[1,64,64,64]{3,2,1,0:T(8,128)} %stack.341) | copy-start | bytes 3145732
  147.7 3.3 copy-start.2
  215.1 101.5 %all-to-all-start.1 = ((f32[8,2,128,512]{2,3,1,0:T(8,128)}), f32[8,2,128,512]{2,3,1,0:T(8,128)}, u32[]{:S(2)}, u32[]{:S(2)}) async-start(f32[8,2,128,512]{2,3,1,0:T(8,128)} %copy.77), calls=%async_computation.1 | async-start | bytes 8388608 | tf_op jit(solution)/shard_map/all_to_all | solution.py:226
  321.9 25.7 %slice-start = ((s8[8388608]{0:T(1024)(128)(4,1)}), s8[4194304]{0:T(1024)(128)(4,1)S(1)}, s32[]{:S(2)}) async-start(s8[8388608]{0:T(1024)(128)(4,1)} %bitcast.253), calls=%async_computation.2 | async-start | bytes 8388608
  321.9 25.7 %slice-start.1 = ((s8[8388608]{0:T(1024)(128)(4,1)}), s8[4194304]{0:T(1024)(128)(4,1)S(1)}, s32[]{:S(2)}) async-start(s8[8388608]{0:T(1024)(128)(4,1)} %bitcast.253), calls=%async_computation.3 | async-start | bytes 8388608
  321.9 25.7 %copy-start = (f32[1,2,1024,1024]{2,3,0,1:T(8,128)S(1)}, f32[1,2,1024,1024]{2,3,0,1:T(8,128)}, u32[]{:S(2)}) copy-start(f32[1,2,1024,1024]{2,3,0,1:T(8,128)} %get-tuple-element.45) | copy-start | bytes 25165828
  321.9 25.7 %copy-start.1 = (f32[2,8,128,512]{3,2,1,0:T(8,128)S(1)}, f32[2,8,128,512]{3,2,1,0:T(8,128)}, u32[]{:S(2)}) copy-start(f32[2,8,128,512]{3,2,1,0:T(8,128)} %copy.78) | copy-start | bytes 12582916
  329.1 18.5 %collective-permute-start = (f32[2,256,512]{2,1,0:T(8,128)S(1)}, f32[2,256,512]{2,1,0:T(8,128)S(1)}, u32[]{:S(2)}, u32[]{:S(2)}) collective-permute-start(f32[2,256,512]{2,1,0:T(8,128)S(1)} %fusion.55), channel_id=1, source_target_pairs={{0,8},{8,16},{16,24},{24,32},{32,40},{40,48},{48,56},{56,64},{64,7... | collective-permute-start | bytes 3145736 | tf_op jit(solution)/shard_map/ppermute | solution.py:20
  351.2 18.2 %collective-permute-start.1 = (f32[2,256,512]{2,1,0:T(8,128)S(1)}, f32[2,256,512]{2,1,0:T(8,128)S(1)}, u32[]{:S(2)}, u32[]{:S(2)}) collective-permute-start(f32[2,256,512]{2,1,0:T(8,128)S(1)} %fusion.65), channel_id=1, source_target_pairs={{0,8},{8,16},{16,24},{24,32},{32,40},{40,48},{48,56},{56,64},{64,7... | collective-permute-start | bytes 3145736 | tf_op jit(solution)/shard_map/ppermute | solution.py:20
  369.6 18.2 %collective-permute-start.2 = (f32[2,256,512]{2,1,0:T(8,128)S(1)}, f32[2,256,512]{2,1,0:T(8,128)S(1)}, u32[]{:S(2)}, u32[]{:S(2)}) collective-permute-start(f32[2,256,512]{2,1,0:T(8,128)S(1)} %add.742), channel_id=1, source_target_pairs={{0,8},{8,16},{16,24},{24,32},{32,40},{40,48},{48,56},{56,64},{64,7... | collective-permute-start | bytes 3145736 | tf_op jit(solution)/shard_map/ppermute | solution.py:20

commit v8 on v6

--- a/solution.py
+++ b/solution.py
@@ -153,7 +153,11 @@
     second_range = jnp.arange(second_len, dtype=jnp.int32)
     column_range = jnp.arange(columns, dtype=jnp.int32)
     sample_rows = jnp.arange(quarter, dtype=jnp.int32)
-    entry_table = real_table(rotation(sample_rows[:, None] * row_order[None, :], row_count))
+    sixteen = jnp.arange(16, dtype=jnp.int32)
+    entry_hi = rotation((16 * sixteen)[:, None] * row_order[None, :], row_count)
+    entry_lo = rotation(sixteen[:, None] * row_order[None, :], row_count)
+    entry_turn = complex_mul(entry_hi[:, :, None, :], entry_lo[:, None, :, :]).reshape(2, quarter, row_count)
+    entry_table = real_table(entry_turn)
     samples_in = voltage[0].reshape(2, quarter, B1 // groups, second_len)
     entry_blocks = entry_table.reshape(2, 2, quarter, groups, local_rows)
     device_turn = rotation(row_order * (device * local_width), total_bins)

time: 395 us -> 390 us (0.987)
    sin x4 -> x3, other arithmetic: 5.41 us -> 0.36 us  [rotation(): return jnp.stack([jnp.cos(angles), jnp.sin(angles)])]
where the time goes in v8:
time: 390 us; the launch traced here: 383 us
  waiting for transfers between devices  177 us (45%)
  local copies, waits for them, and re-layouts  64.1 us (16%)
  matrix products  54.5 us (14%)
  other arithmetic  48.9 us (13%)
  starting transfers between devices  19.8 us (5%)
  Pallas kernels  17.4 us (4%)
    all_to_all x1, waiting for transfers between devices, per_device(): lax.all_to_all(packed, 'fft', split_axis=0, concat_axis=0, tiled=True)  73.2 us
    all_to_all x1, waiting for transfers between devices, per_device(): lax.all_to_all(spread, 'fft', split_axis=0, concat_axis=0, tiled=True)  62.2 us
    ppermute x3, waiting for transfers between devices, passed_along(): return lax.ppermute(shard, axis, pairs)  41.5 us
    dot_general x4, matrix products, sample_block(): return jnp.einsum('prn,pqrm->qmn', arrived, table, precision=HIGH)  17.8 us
    pallas_call x1, Pallas kernels, middle(): pl.pallas_call(middle_kernel, out_shape=jax.ShapeDtypeStruct(shape, jnp.f...  17.4 us
    neg x1, other arithmetic, real_table(): -pair[1]  16.8 us
    sin x1, local copies, waits for them, and re-layouts, middle(): jnp.sin(phase_rows)  15.9 us
    reshape x4, local copies, waits for them, and re-layouts, per_device(): jnp.einsum('phrkv,phku->hruv', packed, last_table[:, part], precision=HIGH)  13.1 us
  transfers between devices with their start and end apart: 5, of which 5 were waited for; matrix products, arithmetic and copies ran while one was open for 17% of the time, Pallas kernels for 0%

profile of v8, /device:TPU:16, one launch (start us, length us, event | category | flops | bytes accessed | tf_op | source)
XLA Modules:
  0.0 382.9 jit_solution(8399193043119544554)
XLA Ops:
  0.1 1.0 fusion.95
  1.1 1.6 copy.60
  2.7 0.6 fusion.174
  3.3 0.3 multiply_add_fusion.5
  4.2 0.3 fusion.270
  4.7 3.6 fusion.47
  8.3 1.1 multiply_subtract_fusion.3
  9.4 0.6 pad_maximum_fusion.4
  10.0 2.3 copy.62
  12.3 8.7 %all-to-all-start = ((f32[8,2,128,8,64]{2,4,3,1,0:T(8,128)}), f32[8,2,128,8,64]{2,4,3,1,0:T(8,128)}, u32[]{:S(2)}, u32[]{:S(2)}) async-start(f32[8,2,128,8,64]{2,4,3,1,0:T(8,128)} %copy.62), calls=%async_computation | async-start | bytes 8388608 | tf_op jit(solution)/shard_map/all_to_all | solution.py:175
  21.1 1.7 slice_bitcast_fusion
  23.0 1.2 convolution_bitcast_fusion.1
  24.2 0.6 copy.68
  25.0 1.7 stack.348
  27.0 0.8 copy.69.row_ref
  27.8 2.2 stack.347
  30.6 0.4 fusion.216
  31.0 0.3 fusion.241
  31.3 0.7 pad_maximum_fusion.11.column_ref
  32.2 1.7 constant_dynamic-update-slice_fusion.1
  34.2 0.3 fusion.200
  34.5 0.3 fusion.204
  34.8 2.6 multiply_subtract_fusion.2
  37.5 0.8 fusion.265
  38.3 0.9 fusion.263
  39.3 15.9 %fusion.269 = (f32[2,64,64,64]{3,2,1,0:T(8,128)}, f32[2,64,64,64]{3,2,1,0:T(8,128)}) fusion(f32[2,64,64,64]{3,2,1,0:T(8,128)S(1)} %constant_dynamic-update-slice_fusion), kind=kLoop, calls=%fused_computation.434 | loop fusion | bytes 6291456 | tf_op jit(solution)/shard_map/sin | solution.py:132
  55.1 62.2 %all-to-all-done = f32[8,2,128,8,64]{2,4,3,1,0:T(8,128)} async-done(((f32[8,2,128,8,64]{2,4,3,1,0:T(8,128)}), f32[8,2,128,8,64]{2,4,3,1,0:T(8,128)}, u32[]{:S(2)}, u32[]{:S(2)}) %all-to-all-start) | async-done | bytes 4194336 | tf_op jit(solution)/shard_map/all_to_all | solution.py:175
  117.4 9.2 %copy.63 = f32[8,2,128,8,64]{4,3,0,1,2:T(8,128)} copy(f32[8,2,128,8,64]{2,4,3,1,0:T(8,128)} %all-to-all-done) | data formatting | bytes 8388608 | tf_op jit(solution)/shard_map/all_to_all | solution.py:175
  126.6 6.9 %convolution_bitcast_fusion = f32[2,2,64,64,64]{4,3,2,0,1:T(8,128)S(1)} fusion(f32[8,2,2,64,8,64,1]{5,4,0,1,3,6,2:T(8,128)} %bitcast.267, f32[1,2,2,8,8,64]{5,4,3,0,1,2:T(8,128)S(1)} %get-tuple-element.67, f32[1,1,1,8,8,64]{5,4,3,0,1,2:T(8,128)S(1)} %get-tuple-element.93, f32[1,1,1,8,8,64]{5,4,3,0,1,2:T(8,128)S(1)} %get-tuple-element.94, ...), kind=kOutput, calls=%fused_computation.55 | convolution fusion | flops 805437440 | bytes 8519680 | tf_op jit(solution)/shard_map/sphrun,pqhsuk->qhrkn/dot_general | solution.py:181
  133.5 2.0 multiply_subtract_fusion.1
  135.5 7.1 %fusion.38.spec_ref = f32[2,2,64,64,64]{4,3,2,1,0:T(8,128)S(1)} fusion(f32[1,2,64,64,64]{4,3,2,0,1:T(8,128)S(1)} %get-tuple-element.37, f32[1,2,64,64,64]{4,3,2,0,1:T(8,128)S(1)} %get-tuple-element.36, f32[1,2,2,64,64]{4,3,1,2,0:T(8,128)S(1)} %get-tuple-element.66, f32[1,2,2,64,64]{4,3,1,2,0:T(8,128)S(1)} %fusion.86), kind=kOutput, calls=%fused_computation.56 | convolution fusion | flops 806387712 | bytes 8519680 | tf_op jit(solution)/shard_map/phrkn,pqhnj->qhrjk/dot_general | solution.py:183
  142.6 3.2 copy-done.2
  146.9 1.0 multiply_subtract_fusion.6
  148.1 0.9 fusion.161
  150.0 0.3 fusion.158
  150.5 17.4 %shard_map.28 = f32[2,2,64,64,64]{4,3,2,1,0:T(8,128)} custom-call(f32[2,2,64,64,64]{4,3,2,1,0:T(8,128)} %copy-done.2, f32[2,64,64,64]{3,2,1,0:T(8,128)} %get-tuple-element.47.cos_ref, f32[2,64,64,64]{3,2,1,0:T(8,128)} %get-tuple-element.46.sin_ref, f32[2,2,64,1,1]{4,3,2,1,0:T(1,128)} %copy.69.row_ref, f32[2,2,1,64,64]{4,3,2,1,0:T(8,128)} %pad_maximum_fusion.11.column_ref), custom_call_target="tpu_custom_call" | custom-call | tf_op jit(solution)/shard_map/pallas_call | solution.py:117
  168.0 1.6 fusion.91
  169.5 9.4 %fusion.35 = f32[2,2,64,64,64]{4,3,2,0,1:T(8,128)S(1)} fusion(f32[2,2,64,64,64]{4,3,2,1,0:T(8,128)} %fusion.91, f32[1,2,2,64,64]{4,3,1,2,0:T(8,128)S(1)} %get-tuple-element.71, f32[1,2,2,64,64]{4,3,1,2,0:T(8,128)S(1)} %get-tuple-element.70), kind=kOutput, calls=%fused_computation.54 | convolution fusion | flops 805339136 | bytes 8519680 | tf_op jit(solution)/shard_map/phrjk,pqhjv->qhrkv/dot_general | solution.py:211
  178.9 2.0 multiply_subtract_fusion
  180.9 3.9 %fusion.44 = f32[2,64,64,64]{3,2,1,0:T(8,128)} fusion(f32[2,2,64,64,1]{3,2,1,0,4:T(8,128)S(1)} %get-tuple-element.52, f32[1,2,64,64,64]{4,3,2,0,1:T(8,128)S(1)} %get-tuple-element.35, f32[1,2,64,64,64]{4,3,2,0,1:T(8,128)S(1)} %get-tuple-element.34), kind=kOutput, calls=%fused_computation.58 | convolution fusion | flops 403701760 | bytes 6356992 | tf_op jit(solution)/shard_map/phrkv,phku->hruv/dot_general | solution.py:217
  184.9 4.0 %fusion.41 = f32[2,64,64,64]{3,2,1,0:T(8,128)} fusion(f32[2,2,64,64,1]{3,2,1,0,4:T(8,128)S(1)} %get-tuple-element.53, f32[1,2,64,64,64]{4,3,2,0,1:T(8,128)S(1)} %get-tuple-element.35, f32[1,2,64,64,64]{4,3,2,0,1:T(8,128)S(1)} %get-tuple-element.34), kind=kOutput, calls=%fused_computation.57 | convolution fusion | flops 403701760 | bytes 6356992 | tf_op jit(solution)/shard_map/phrkv,phku->hruv/dot_general | solution.py:217
  188.8 3.4 reshape.2203
  192.3 4.8 %reshape.2204 = f32[128,8,512]{2,1,0:T(8,128)} reshape(f32[2,64,64,64]{3,2,1,0:T(8,128)} %fusion.44) | data formatting | bytes 4194304 | tf_op jit(solution)/shard_map/reshape | solution.py:217
  197.1 3.0 copy.82
  200.0 1.9 copy.79
  201.9 3.9 %fusion.51 = (f32[8,1,128,512]{2,3,0,1:T(8,128)S(1)}, f32[8,1,128,512]{2,3,0,1:T(8,128)S(1)}) fusion(f32[128,8,512]{0,2,1:T(8,128)} %copy.82, f32[128,8,512]{0,2,1:T(8,128)} %copy.79, f32[128,8,512]{0,2,1:T(8,128)} %bitcast.269, f32[128,8,512]{0,2,1:T(8,128)} %bitcast.268), kind=kLoop, calls=%fused_computation.63 | loop fusion | flops 3145728 | bytes 12582912 | tf_op jit(solution)/shard_map/stack | solution.py:229
  205.9 0.3 pad_maximum_fusion.5
  206.2 2.3 copy.85
  208.5 4.8 %all-to-all-start.1 = ((f32[8,2,128,512]{2,3,1,0:T(8,128)}), f32[8,2,128,512]{2,3,1,0:T(8,128)}, u32[]{:S(2)}, u32[]{:S(2)}) async-start(f32[8,2,128,512]{2,3,1,0:T(8,128)} %copy.85), calls=%async_computation.1 | async-start | bytes 8388608 | tf_op jit(solution)/shard_map/all_to_all | solution.py:230
  213.2 16.8 %fusion.54 = (f32[1,1024,1024]{1,2,0:T(8,128)S(1)}, f32[1,1024,1024]{1,2,0:T(8,128)S(1)}, f32[1,1024,1024]{1,2,0:T(8,128)S(1)}) fusion(s32[1024]{0:T(1024)S(1)} %select_select_fusion.1), kind=kLoop, calls=%fused_computation.74 | loop fusion | flops 18874368 | bytes 12587008 | tf_op jit(solution)/shard_map/neg | solution.py:34
  230.0 6.7 %maximum_bitcast_fusion.1 = (f32[1,2,1024,1024]{2,3,0,1:T(8,128)}, f32[1,2,1024,1024]{2,3,0,1:T(8,128)}) fusion(f32[1,1024,1024]{1,2,0:T(8,128)S(1)} %get-tuple-element.90, f32[1,1024,1024]{1,2,0:T(8,128)S(1)} %get-tuple-element.88, f32[1,1024,1024]{1,2,0:T(8,128)S(1)} %get-tuple-element.89), kind=kLoop, calls=%fused_computation.7 | loop fusion | flops 4194304 | bytes 29360128 | tf_op jit(solution)/shard_map/stack | solution.py:34
  236.8 73.2 %all-to-all-done.1 = f32[8,2,128,512]{2,3,1,0:T(8,128)} async-done(((f32[8,2,128,512]{2,3,1,0:T(8,128)}), f32[8,2,128,512]{2,3,1,0:T(8,128)}, u32[]{:S(2)}, u32[]{:S(2)}) %all-to-all-start.1) | async-done | bytes 4194336 | tf_op jit(solution)/shard_map/all_to_all | solution.py:230
  309.9 5.4 %copy.86 = f32[2,8,128,512]{3,2,1,0:T(8,128)} copy(f32[2,8,128,512]{2,3,0,1:T(8,128)} %bitcast.76) | data formatting | bytes 8388608 | tf_op jit(solution)/shard_map/transpose | solution.py:231
  315.3 7.2 %fusion.55 = f32[2,256,512]{2,1,0:T(8,128)S(1)} fusion(f32[2,1024,512,1]{2,1,0,3:T(8,128)} %bitcast.263, f32[1,2,1024,1024]{2,3,0,1:T(8,128)} %get-tuple-element.44, f32[1,2,1024,1024]{2,3,0,1:T(8,128)} %get-tuple-element.45), kind=kOutput, calls=%fused_computation.75 | convolution fusion | flops 3222274048 | bytes 22020096 | tf_op jit(solution)/shard_map/prn,pqrm->qmn/dot_general | solution.py:240
  322.5 2.4 collective-permute-start
  324.9 16.0 %collective-permute-done = f32[2,256,512]{2,1,0:T(8,128)S(1)} collective-permute-done((f32[2,256,512]{2,1,0:T(8,128)S(1)}, f32[2,256,512]{2,1,0:T(8,128)S(1)}, u32[]{:S(2)}, u32[]{:S(2)}) %collective-permute-start) | collective-permute-done | bytes 1048608 | tf_op jit(solution)/shard_map/ppermute | solution.py:20
  341.0 3.5 fusion.65
  344.6 1.9 collective-permute-start.1
  346.5 3.5 fusion.56
  350.0 12.7 %collective-permute-done.1 = f32[2,256,512]{2,1,0:T(8,128)S(1)} collective-permute-done((f32[2,256,512]{2,1,0:T(8,128)S(1)}, f32[2,256,512]{2,1,0:T(8,128)S(1)}, u32[]{:S(2)}, u32[]{:S(2)}) %collective-permute-start.1) | collective-permute-done | bytes 1048608 | tf_op jit(solution)/shard_map/ppermute | solution.py:20
  363.0 1.9 collective-permute-start.2
  364.9 3.5 fusion.59
  368.5 12.7 %collective-permute-done.2 = f32[2,256,512]{2,1,0:T(8,128)S(1)} collective-permute-done((f32[2,256,512]{2,1,0:T(8,128)S(1)}, f32[2,256,512]{2,1,0:T(8,128)S(1)}, u32[]{:S(2)}, u32[]{:S(2)}) %collective-permute-start.2) | collective-permute-done | bytes 1048608 | tf_op jit(solution)/shard_map/ppermute | solution.py:20
  381.2 1.2 add_bitcast_fusion
  (83 shorter events, 5.0 us)
Async XLA Ops:
  12.3 105.1 %all-to-all-start = ((f32[8,2,128,8,64]{2,4,3,1,0:T(8,128)}), f32[8,2,128,8,64]{2,4,3,1,0:T(8,128)}, u32[]{:S(2)}, u32[]{:S(2)}) async-start(f32[8,2,128,8,64]{2,4,3,1,0:T(8,128)} %copy.62), calls=%async_computation | async-start | bytes 8388608 | tf_op jit(solution)/shard_map/all_to_all | solution.py:175
  30.0 3.9 %copy-start.3 = (f32[1,64,64,64]{3,2,1,0:T(8,128)S(1)}, f32[1,64,64,64]{3,2,1,0:T(8,128)}, u32[]{:S(2)}) copy-start(f32[1,64,64,64]{3,2,1,0:T(8,128)} %stack.348) | copy-start | bytes 3145732
  142.6 3.3 copy-start.2
  208.5 101.5 %all-to-all-start.1 = ((f32[8,2,128,512]{2,3,1,0:T(8,128)}), f32[8,2,128,512]{2,3,1,0:T(8,128)}, u32[]{:S(2)}, u32[]{:S(2)}) async-start(f32[8,2,128,512]{2,3,1,0:T(8,128)} %copy.85), calls=%async_computation.1 | async-start | bytes 8388608 | tf_op jit(solution)/shard_map/all_to_all | solution.py:230
  315.3 25.7 %slice-start = ((s8[8388608]{0:T(1024)(128)(4,1)}), s8[4194304]{0:T(1024)(128)(4,1)S(1)}, s32[]{:S(2)}) async-start(s8[8388608]{0:T(1024)(128)(4,1)} %bitcast.261), calls=%async_computation.2 | async-start | bytes 8388608
  315.3 25.7 %slice-start.1 = ((s8[8388608]{0:T(1024)(128)(4,1)}), s8[4194304]{0:T(1024)(128)(4,1)S(1)}, s32[]{:S(2)}) async-start(s8[8388608]{0:T(1024)(128)(4,1)} %bitcast.261), calls=%async_computation.3 | async-start | bytes 8388608
  315.3 25.7 %copy-start = (f32[1,2,1024,1024]{2,3,0,1:T(8,128)S(1)}, f32[1,2,1024,1024]{2,3,0,1:T(8,128)}, u32[]{:S(2)}) copy-start(f32[1,2,1024,1024]{2,3,0,1:T(8,128)} %get-tuple-element.45) | copy-start | bytes 25165828
  315.3 25.7 %copy-start.1 = (f32[2,8,128,512]{3,2,1,0:T(8,128)S(1)}, f32[2,8,128,512]{3,2,1,0:T(8,128)}, u32[]{:S(2)}) copy-start(f32[2,8,128,512]{3,2,1,0:T(8,128)} %copy.86) | copy-start | bytes 12582916
  322.5 18.5 %collective-permute-start = (f32[2,256,512]{2,1,0:T(8,128)S(1)}, f32[2,256,512]{2,1,0:T(8,128)S(1)}, u32[]{:S(2)}, u32[]{:S(2)}) collective-permute-start(f32[2,256,512]{2,1,0:T(8,128)S(1)} %fusion.55), channel_id=1, source_target_pairs={{0,8},{8,16},{16,24},{24,32},{32,40},{40,48},{48,56},{56,64},{64,7... | collective-permute-start | bytes 3145736 | tf_op jit(solution)/shard_map/ppermute | solution.py:20
  344.6 18.2 %collective-permute-start.1 = (f32[2,256,512]{2,1,0:T(8,128)S(1)}, f32[2,256,512]{2,1,0:T(8,128)S(1)}, u32[]{:S(2)}, u32[]{:S(2)}) collective-permute-start(f32[2,256,512]{2,1,0:T(8,128)S(1)} %fusion.65), channel_id=1, source_target_pairs={{0,8},{8,16},{16,24},{24,32},{32,40},{40,48},{48,56},{56,64},{64,7... | collective-permute-start | bytes 3145736 | tf_op jit(solution)/shard_map/ppermute | solution.py:20
  363.0 18.2 %collective-permute-start.2 = (f32[2,256,512]{2,1,0:T(8,128)S(1)}, f32[2,256,512]{2,1,0:T(8,128)S(1)}, u32[]{:S(2)}, u32[]{:S(2)}) collective-permute-start(f32[2,256,512]{2,1,0:T(8,128)S(1)} %add.774), channel_id=1, source_target_pairs={{0,8},{8,16},{16,24},{24,32},{32,40},{40,48},{48,56},{56,64},{64,7... | collective-permute-start | bytes 3145736 | tf_op jit(solution)/shard_map/ppermute | solution.py:20

commit v9 on v8

--- a/solution.py
+++ b/solution.py
@@ -160,19 +160,21 @@
     entry_table = real_table(entry_turn)
     samples_in = voltage[0].reshape(2, quarter, B1 // groups, second_len)
     entry_blocks = entry_table.reshape(2, 2, quarter, groups, local_rows)
-    device_turn = rotation(row_order * (device * local_width), total_bins)
+    spread = jnp.einsum("pmun,pqmdr->dqrun", samples_in, entry_blocks, precision=HIGH)
+    gathered = lax.all_to_all(spread, "fft", split_axis=0, concat_axis=0, tiled=True)
+    source_range = jnp.arange(groups, dtype=jnp.int32)
     block_range = jnp.arange(B1 // groups, dtype=jnp.int32)
-    within_turn = rotation(row_order[:, None] * (second_len * block_range)[None, :], total_bins)
-    inner_turn = rotation(row_order[:, None] * second_range[None, :], total_bins)
-    outer_turn = complex_mul(device_turn[:, :, None], within_turn)
-    turn = complex_mul(outer_turn[..., None], inner_turn[:, :, None, :])
-    turn = turn.reshape(2, groups, local_rows, B1 // groups, second_len)
-    spread = jnp.einsum("pmun,pqmdr->dqrun", samples_in, entry_blocks, precision=HIGH)
-    spread = jnp.stack([
-        spread[:, 0] * turn[0] - spread[:, 1] * turn[1],
-        spread[:, 0] * turn[1] + spread[:, 1] * turn[0],
+    source_turn = rotation((local_width * source_range)[:, None] * local_order[None, :], total_bins)
+    within_turn = rotation(local_order[:, None] * (second_len * block_range)[None, :], total_bins)
+    inner_turn = rotation(local_order[:, None] * second_range[None, :], total_bins)
+    turn = complex_mul(
+        complex_mul(source_turn[..., None, None], within_turn[:, None, :, :, None]),
+        inner_turn[:, None, :, None, :],
+    )
+    gathered = jnp.stack([
+        gathered[:, 0] * turn[0] - gathered[:, 1] * turn[1],
+        gathered[:, 0] * turn[1] + gathered[:, 1] * turn[0],
     ], axis=1)
-    gathered = lax.all_to_all(spread, "fft", split_axis=0, concat_axis=0, tiled=True)
     gathered = gathered.reshape(groups, 2, 2, half_count, B1 // groups, second_len)
     section_one = both_halves(first_range, first_range, B1, False, True)
     block_turn = both_halves(first_range, second_range, columns, True, False)

time: 390 us -> 391 us (level)
  other arithmetic: 48.9 us -> 55.3 us
  waiting for transfers between devices: 177 us -> 172 us
    all_to_all x1 -> x0, local copies, waits for them, and re-layouts: 9.21 us -> none  [per_device(): lax.all_to_all(spread, 'fft', split_axis=0, concat_axis=0, tiled=True)]
    sub x0 -> x1, local copies, waits for them, and re-layouts: none -> 5.59 us  [per_device(): gathered[:, 0] * turn[0] - gathered[:, 1] * turn[1]]
    all_to_all x1, waiting for transfers between devices: 62.2 us -> 56.9 us  [per_device(): lax.all_to_all(spread, 'fft', split_axis=0, concat_axis=0, tiled=True)]
    add x0 -> x1, local copies, waits for them, and re-layouts: none -> 4.58 us  [per_device(): gathered[:, 0] * turn[1] + gathered[:, 1] * turn[0]]
    unnamed x23 -> x61, local copies, waits for them, and re-layouts: 8.88 us -> 9.02 us
  transfers between devices with their start and end apart: 5 -> 5, of which waited for: 5 -> 5; matrix products, arithmetic and copies ran while one was open for 17% -> 18% of each run, Pallas kernels for 0% -> 0%
where the time goes in v9:
time: 391 us; the launch traced here: 386 us
  waiting for transfers between devices  172 us (44%)
  local copies, waits for them, and re-layouts  65.8 us (17%)
  other arithmetic  55.3 us (14%)
  matrix products  54.4 us (14%)
  starting transfers between devices  19.9 us (5%)
  Pallas kernels  17.4 us (4%)
    all_to_all x1, waiting for transfers between devices, per_device(): lax.all_to_all(packed, 'fft', split_axis=0, concat_axis=0, tiled=True)  73.1 us
    all_to_all x1, waiting for transfers between devices, per_device(): lax.all_to_all(spread, 'fft', split_axis=0, concat_axis=0, tiled=True)  56.9 us
    ppermute x3, waiting for transfers between devices, passed_along(): return lax.ppermute(shard, axis, pairs)  41.5 us
    dot_general x4, matrix products, sample_block(): return jnp.einsum('prn,pqrm->qmn', arrived, table, precision=HIGH)  17.8 us
    pallas_call x1, Pallas kernels, middle(): pl.pallas_call(middle_kernel, out_shape=jax.ShapeDtypeStruct(shape, jnp.f...  17.4 us
    neg x1, other arithmetic, real_table(): -pair[1]  16.8 us
    sin x1, local copies, waits for them, and re-layouts, middle(): jnp.sin(phase_rows)  15.9 us
    reshape x4, local copies, waits for them, and re-layouts, per_device(): jnp.einsum('phrkv,phku->hruv', packed, last_table[:, part], precision=HIGH)  13.1 us
  transfers between devices with their start and end apart: 5, of which 5 were waited for; matrix products, arithmetic and copies ran while one was open for 18% of the time, Pallas kernels for 0%

profile of v9, /device:TPU:16, one launch (start us, length us, event | category | flops | bytes accessed | tf_op | source)
XLA Modules:
  0.0 385.7 jit_solution(11184508179502383089)
XLA Ops:
  0.0 1.6 copy.66
  1.6 0.6 fusion.167
  3.3 3.6 fusion.51
  6.9 2.3 copy.68
  9.2 8.7 %all-to-all-start = ((f32[8,2,128,8,64]{2,4,3,1,0:T(8,128)}), f32[8,2,128,8,64]{2,4,3,1,0:T(8,128)}, u32[]{:S(2)}, u32[]{:S(2)}) async-start(f32[8,2,128,8,64]{2,4,3,1,0:T(8,128)} %copy.68), calls=%async_computation | async-start | bytes 8388608 | tf_op jit(solution)/shard_map/all_to_all | solution.py:164
  17.9 1.7 slice_bitcast_fusion
  19.8 1.2 convolution_bitcast_fusion
  21.1 0.6 copy.75
  21.9 1.7 stack.351
  23.8 0.8 copy.76.row_ref
  24.6 2.3 stack.350
  27.0 0.7 slice_reduce_fusion.1
  28.0 0.4 fusion.207
  28.7 0.7 pad_maximum_fusion.10.column_ref
  29.4 0.7 fusion.84
  30.1 0.7 fusion.93
  30.8 0.7 negate_bitcast_fusion
  31.5 0.7 fusion.88
  32.2 1.7 constant_dynamic-update-slice_fusion.1
  34.5 0.6 multiply_subtract_fusion.8
  35.1 0.3 fusion.193
  35.4 1.0 fusion.195
  36.4 2.7 multiply_subtract_fusion.2
  39.1 1.5 fusion.252
  40.5 0.9 fusion.250
  41.5 15.9 %fusion.256 = (f32[2,64,64,64]{3,2,1,0:T(8,128)}, f32[2,64,64,64]{3,2,1,0:T(8,128)}) fusion(f32[2,64,64,64]{3,2,1,0:T(8,128)S(1)} %constant_dynamic-update-slice_fusion), kind=kLoop, calls=%fused_computation.412 | loop fusion | bytes 6291456 | tf_op jit(solution)/shard_map/sin | solution.py:132
  57.4 56.9 %all-to-all-done = f32[8,2,128,8,64]{2,4,3,1,0:T(8,128)} async-done(((f32[8,2,128,8,64]{2,4,3,1,0:T(8,128)}), f32[8,2,128,8,64]{2,4,3,1,0:T(8,128)}, u32[]{:S(2)}, u32[]{:S(2)}) %all-to-all-start) | async-done | bytes 4194336 | tf_op jit(solution)/shard_map/all_to_all | solution.py:164
  114.3 4.5 %multiply_subtract_fusion.3 = (f32[8,1,128,8,64]{2,4,3,1,0:T(8,128)}, f32[8,1,128,8,64]{2,4,3,1,0:T(8,128)S(1)}) fusion(f32[8,2,128,8,64]{2,4,3,1,0:T(8,128)} %all-to-all-done, f32[128,64]{0,1:T(8,128)S(1)} %get-tuple-element.105, f32[8,128,8]{1,2,0:T(8,128)S(1)} %copy-done.12, f32[128,64]{0,1:T(8,128)S(1)} %get-tuple-element.106, f32[8,128,8]{1,2,0:T(8,128)S(1)} %copy-done.11), kind=kLoop, calls=%fused_computation.74 | loop fusion | flops 6291456 | bytes 8519680 | tf_op jit(solution)/shard_map/sub | solution.py:175
  118.8 5.6 %copy.69 = f32[8,1,128,8,64]{4,3,0,2,1:T(8,128)} copy(f32[8,1,128,8,64]{2,4,3,1,0:T(8,128)} %get-tuple-element.42) | data formatting | bytes 4194304 | tf_op jit(solution)/shard_map/sub | solution.py:175
  124.4 4.6 %copy.70 = f32[8,1,128,8,64]{4,3,0,2,1:T(8,128)} copy(f32[8,1,128,8,64]{2,4,3,1,0:T(8,128)S(1)} %get-tuple-element.43) | data formatting | bytes 4194304 | tf_op jit(solution)/shard_map/add | solution.py:176
  129.0 6.8 %fusion.41 = f32[2,2,64,64,64]{4,3,2,0,1:T(8,128)S(1)} fusion(f32[8,1,2,64,8,64]{5,4,0,1,3,2:T(8,128)} %bitcast.271, f32[8,1,2,64,8,64]{5,4,0,1,3,2:T(8,128)} %bitcast.270, f32[1,2,2,8,8,64]{5,4,3,0,1,2:T(8,128)S(1)} %copy-done.5, f32[1,1,1,8,8,64]{5,4,3,0,1,2:T(8,128)S(1)} %copy-done.17, f32[1,1,1,8,8,64]{5,4,3,0,1,2:T(8,128)S(1)} %copy-done.18, ...), kind=kOutput, calls=%fused_computation.58 | convolution fusion | flops 806486016 | bytes 8519680 | tf_op jit(solution)/shard_map/sphrun,pqhsuk->qhrkn/dot_general | solution.py:183
  135.9 2.0 multiply_subtract_fusion.1
  138.0 7.1 %fusion.42.spec_ref = f32[2,2,64,64,64]{4,3,2,1,0:T(8,128)S(1)} fusion(f32[1,2,64,64,64]{4,3,2,0,1:T(8,128)S(1)} %get-tuple-element.37, f32[1,2,64,64,64]{4,3,2,0,1:T(8,128)S(1)} %get-tuple-element.36, f32[1,2,2,64,64]{4,3,1,2,0:T(8,128)S(1)} %copy-done.4, f32[1,2,2,64,64]{4,3,1,2,0:T(8,128)S(1)} %copy-done.6), kind=kOutput, calls=%fused_computation.59 | convolution fusion | flops 806387712 | bytes 8519680 | tf_op jit(solution)/shard_map/phrkn,pqhnj->qhrjk/dot_general | solution.py:185
  145.1 3.3 copy-done.2
  149.4 1.0 multiply_subtract_fusion.6
  150.7 0.9 fusion.154
  153.1 17.4 %shard_map.28 = f32[2,2,64,64,64]{4,3,2,1,0:T(8,128)} custom-call(f32[2,2,64,64,64]{4,3,2,1,0:T(8,128)} %copy-done.2, f32[2,64,64,64]{3,2,1,0:T(8,128)} %get-tuple-element.47.cos_ref, f32[2,64,64,64]{3,2,1,0:T(8,128)} %get-tuple-element.46.sin_ref, f32[2,2,64,1,1]{4,3,2,1,0:T(1,128)} %copy.76.row_ref, f32[2,2,1,64,64]{4,3,2,1,0:T(8,128)} %pad_maximum_fusion.10.column_ref), custom_call_target="tpu_custom_call" | custom-call | tf_op jit(solution)/shard_map/pallas_call | solution.py:117
  170.5 1.6 fusion.89
  172.0 9.4 %fusion.38 = f32[2,2,64,64,64]{4,3,2,0,1:T(8,128)S(1)} fusion(f32[2,2,64,64,64]{4,3,2,1,0:T(8,128)} %fusion.89, f32[1,2,2,64,64]{4,3,1,2,0:T(8,128)S(1)} %get-tuple-element.71, f32[1,2,2,64,64]{4,3,1,2,0:T(8,128)S(1)} %get-tuple-element.70), kind=kOutput, calls=%fused_computation.57 | convolution fusion | flops 805339136 | bytes 8519680 | tf_op jit(solution)/shard_map/phrjk,pqhjv->qhrkv/dot_general | solution.py:213
  181.5 2.1 multiply_subtract_fusion
  183.6 3.9 %fusion.48 = f32[2,64,64,64]{3,2,1,0:T(8,128)} fusion(f32[2,2,64,64,1]{3,2,1,0,4:T(8,128)S(1)} %copy-done.8, f32[1,2,64,64,64]{4,3,2,0,1:T(8,128)S(1)} %get-tuple-element.35, f32[1,2,64,64,64]{4,3,2,0,1:T(8,128)S(1)} %get-tuple-element.34), kind=kOutput, calls=%fused_computation.61 | convolution fusion | flops 403701760 | bytes 6356992 | tf_op jit(solution)/shard_map/phrkv,phku->hruv/dot_general | solution.py:219
  187.5 4.0 %fusion.45 = f32[2,64,64,64]{3,2,1,0:T(8,128)} fusion(f32[2,2,64,64,1]{3,2,1,0,4:T(8,128)S(1)} %copy-done.7, f32[1,2,64,64,64]{4,3,2,0,1:T(8,128)S(1)} %get-tuple-element.35, f32[1,2,64,64,64]{4,3,2,0,1:T(8,128)S(1)} %get-tuple-element.34), kind=kOutput, calls=%fused_computation.60 | convolution fusion | flops 403701760 | bytes 6356992 | tf_op jit(solution)/shard_map/phrkv,phku->hruv/dot_general | solution.py:219
  191.5 3.4 reshape.2135
  194.9 4.8 %reshape.2136 = f32[128,8,512]{2,1,0:T(8,128)} reshape(f32[2,64,64,64]{3,2,1,0:T(8,128)} %fusion.48) | data formatting | bytes 4194304 | tf_op jit(solution)/shard_map/reshape | solution.py:219
  199.7 2.9 copy.89
  202.6 1.9 copy.86
  204.5 3.9 %fusion.55 = (f32[8,1,128,512]{2,3,0,1:T(8,128)S(1)}, f32[8,1,128,512]{2,3,0,1:T(8,128)S(1)}) fusion(f32[128,8,512]{0,2,1:T(8,128)} %copy.89, f32[128,8,512]{0,2,1:T(8,128)} %copy.86, f32[128,8,512]{0,2,1:T(8,128)} %bitcast.273, f32[128,8,512]{0,2,1:T(8,128)} %bitcast.272), kind=kLoop, calls=%fused_computation.66 | loop fusion | flops 3145728 | bytes 12582912 | tf_op jit(solution)/shard_map/stack | solution.py:231
  208.8 2.3 copy.92
  211.1 4.9 %all-to-all-start.1 = ((f32[8,2,128,512]{2,3,1,0:T(8,128)}), f32[8,2,128,512]{2,3,1,0:T(8,128)}, u32[]{:S(2)}, u32[]{:S(2)}) async-start(f32[8,2,128,512]{2,3,1,0:T(8,128)} %copy.92), calls=%async_computation.1 | async-start | bytes 8388608 | tf_op jit(solution)/shard_map/all_to_all | solution.py:232
  216.0 16.8 %fusion.58 = (f32[1,1024,1024]{1,2,0:T(8,128)S(1)}, f32[1,1024,1024]{1,2,0:T(8,128)S(1)}, f32[1,1024,1024]{1,2,0:T(8,128)S(1)}) fusion(s32[1024]{0:T(1024)S(1)} %copy-done.20), kind=kLoop, calls=%fused_computation.77 | loop fusion | flops 18874368 | bytes 12587008 | tf_op jit(solution)/shard_map/neg | solution.py:34
  232.8 6.8 %maximum_bitcast_fusion.1 = (f32[1,2,1024,1024]{2,3,0,1:T(8,128)}, f32[1,2,1024,1024]{2,3,0,1:T(8,128)}) fusion(f32[1,1024,1024]{1,2,0:T(8,128)S(1)} %get-tuple-element.90, f32[1,1024,1024]{1,2,0:T(8,128)S(1)} %get-tuple-element.88, f32[1,1024,1024]{1,2,0:T(8,128)S(1)} %get-tuple-element.89), kind=kLoop, calls=%fused_computation.7 | loop fusion | flops 4194304 | bytes 29360128 | tf_op jit(solution)/shard_map/stack | solution.py:34
  239.6 73.1 %all-to-all-done.1 = f32[8,2,128,512]{2,3,1,0:T(8,128)} async-done(((f32[8,2,128,512]{2,3,1,0:T(8,128)}), f32[8,2,128,512]{2,3,1,0:T(8,128)}, u32[]{:S(2)}, u32[]{:S(2)}) %all-to-all-start.1) | async-done | bytes 4194336 | tf_op jit(solution)/shard_map/all_to_all | solution.py:232
  312.7 5.4 %copy.93 = f32[2,8,128,512]{3,2,1,0:T(8,128)} copy(f32[2,8,128,512]{2,3,0,1:T(8,128)} %bitcast.76) | data formatting | bytes 8388608 | tf_op jit(solution)/shard_map/transpose | solution.py:233
  318.1 7.2 %fusion.59 = f32[2,256,512]{2,1,0:T(8,128)S(1)} fusion(f32[2,1024,512,1]{2,1,0,3:T(8,128)} %bitcast.266, f32[1,2,1024,1024]{2,3,0,1:T(8,128)} %get-tuple-element.44, f32[1,2,1024,1024]{2,3,0,1:T(8,128)} %get-tuple-element.45), kind=kOutput, calls=%fused_computation.78 | convolution fusion | flops 3222274048 | bytes 22020096 | tf_op jit(solution)/shard_map/prn,pqrm->qmn/dot_general | solution.py:242
  325.3 2.4 collective-permute-start
  327.8 16.0 %collective-permute-done = f32[2,256,512]{2,1,0:T(8,128)S(1)} collective-permute-done((f32[2,256,512]{2,1,0:T(8,128)S(1)}, f32[2,256,512]{2,1,0:T(8,128)S(1)}, u32[]{:S(2)}, u32[]{:S(2)}) %collective-permute-start) | collective-permute-done | bytes 1048608 | tf_op jit(solution)/shard_map/ppermute | solution.py:20
  343.8 3.5 fusion.69
  347.4 1.9 collective-permute-start.1
  349.3 3.5 fusion.60
  352.9 12.7 %collective-permute-done.1 = f32[2,256,512]{2,1,0:T(8,128)S(1)} collective-permute-done((f32[2,256,512]{2,1,0:T(8,128)S(1)}, f32[2,256,512]{2,1,0:T(8,128)S(1)}, u32[]{:S(2)}, u32[]{:S(2)}) %collective-permute-start.1) | collective-permute-done | bytes 1048608 | tf_op jit(solution)/shard_map/ppermute | solution.py:20
  365.8 1.9 collective-permute-start.2
  367.8 3.5 fusion.63
  371.3 12.7 %collective-permute-done.2 = f32[2,256,512]{2,1,0:T(8,128)S(1)} collective-permute-done((f32[2,256,512]{2,1,0:T(8,128)S(1)}, f32[2,256,512]{2,1,0:T(8,128)S(1)}, u32[]{:S(2)}, u32[]{:S(2)}) %collective-permute-start.2) | collective-permute-done | bytes 1048608 | tf_op jit(solution)/shard_map/ppermute | solution.py:20
  384.1 1.2 add_bitcast_fusion
  (121 shorter events, 6.2 us)
Async XLA Ops:
  0.0 23.5 %copy-start.19 = (s32[1024]{0:T(1024)}, s32[1024]{0:T(1024)S(1)}, u32[]{:S(2)}) copy-start(s32[1024]{0:T(1024)S(1)} %select_select_fusion) | copy-start | bytes 12292
  9.2 105.1 %all-to-all-start = ((f32[8,2,128,8,64]{2,4,3,1,0:T(8,128)}), f32[8,2,128,8,64]{2,4,3,1,0:T(8,128)}, u32[]{:S(2)}, u32[]{:S(2)}) async-start(f32[8,2,128,8,64]{2,4,3,1,0:T(8,128)} %copy.68), calls=%async_computation | async-start | bytes 8388608 | tf_op jit(solution)/shard_map/all_to_all | solution.py:164
  26.9 7.1 %copy-start.3 = (f32[1,64,64,64]{3,2,1,0:T(8,128)S(1)}, f32[1,64,64,64]{3,2,1,0:T(8,128)}, u32[]{:S(2)}) copy-start(f32[1,64,64,64]{3,2,1,0:T(8,128)} %stack.351) | copy-start | bytes 3145732
  41.5 72.8 %copy-start.11 = (f32[8,128,8]{1,2,0:T(8,128)S(1)}, f32[8,128,8]{1,2,0:T(8,128)}, u32[]{:S(2)}) copy-start(f32[8,128,8]{1,2,0:T(8,128)} %get-tuple-element.82) | copy-start | bytes 98308
  41.5 72.8 %copy-start.12 = (f32[8,128,8]{1,2,0:T(8,128)S(1)}, f32[8,128,8]{1,2,0:T(8,128)}, u32[]{:S(2)}) copy-start(f32[8,128,8]{1,2,0:T(8,128)} %get-tuple-element.83) | copy-start | bytes 98308
  124.4 4.6 %copy-start.5 = (f32[1,2,2,8,8,64]{5,4,3,0,1,2:T(8,128)S(1)}, f32[1,2,2,8,8,64]{5,4,3,0,1,2:T(8,128)}, u32[]{:S(2)}) copy-start(f32[1,2,2,8,8,64]{5,4,3,0,1,2:T(8,128)} %get-tuple-element.67) | copy-start | bytes 196612
  124.4 4.6 %copy-start.15 = (f32[1,1,1,8,8,64]{5,4,3,0,1,2:T(8,128)S(1)}, f32[1,1,1,8,8,64]{5,4,3,0,1,2:T(8,128)}, u32[]{:S(2)}) copy-start(f32[1,1,1,8,8,64]{5,4,3,0,1,2:T(8,128)} %get-tuple-element.91) | copy-start | bytes 49156
  124.4 4.6 %copy-start.16 = (f32[1,1,1,8,8,64]{5,4,3,0,1,2:T(8,128)S(1)}, f32[1,1,1,8,8,64]{5,4,3,0,1,2:T(8,128)}, u32[]{:S(2)}) copy-start(f32[1,1,1,8,8,64]{5,4,3,0,1,2:T(8,128)} %get-tuple-element.92) | copy-start | bytes 49156
  124.4 4.6 %copy-start.17 = (f32[1,1,1,8,8,64]{5,4,3,0,1,2:T(8,128)S(1)}, f32[1,1,1,8,8,64]{5,4,3,0,1,2:T(8,128)}, u32[]{:S(2)}) copy-start(f32[1,1,1,8,8,64]{5,4,3,0,1,2:T(8,128)} %get-tuple-element.93) | copy-start | bytes 49156
  124.4 4.6 %copy-start.18 = (f32[1,1,1,8,8,64]{5,4,3,0,1,2:T(8,128)S(1)}, f32[1,1,1,8,8,64]{5,4,3,0,1,2:T(8,128)}, u32[]{:S(2)}) copy-start(f32[1,1,1,8,8,64]{5,4,3,0,1,2:T(8,128)} %get-tuple-element.94) | copy-start | bytes 49156
  129.0 6.8 %copy-start.10 = (f32[2,64,64]{2,1,0:T(8,128)S(1)}, f32[2,64,64]{2,1,0:T(8,128)}, u32[]{:S(2)}) copy-start(f32[2,64,64]{2,1,0:T(8,128)} %get-tuple-element.59) | copy-start | bytes 98308
  135.8 2.1 copy-start.4
  135.8 2.1 copy-start.6
  137.9 11.4 %copy-start.21 = (f32[2]{0:T(128)S(1)}, f32[2]{0:T(128)}, u32[]{:S(2)}) copy-start(f32[2]{0:T(128)} %get-tuple-element.19) | copy-start | bytes 28
  137.9 11.4 %copy-start.22 = (f32[2]{0:T(128)S(1)}, f32[2]{0:T(128)}, u32[]{:S(2)}) copy-start(f32[2]{0:T(128)} %get-tuple-element.20) | copy-start | bytes 28
  137.9 12.7 %copy-start.13 = (f32[2,1,4096]{2,1,0:T(1,128)S(1)}, f32[2,1,4096]{2,1,0:T(1,128)}, u32[]{:S(2)}) copy-start(f32[2,1,4096]{2,1,0:T(1,128)} %get-tuple-element.30) | copy-start | bytes 98308
  138.0 12.7 %copy-start.14 = (f32[2,1,4096]{2,1,0:T(1,128)S(1)}, f32[2,1,4096]{2,1,0:T(1,128)}, u32[]{:S(2)}) copy-start(f32[2,1,4096]{2,1,0:T(1,128)} %get-tuple-element.31) | copy-start | bytes 98308
  145.0 3.3 copy-start.2
  172.0 9.4 %copy-start.9 = (f32[2,64,64]{2,1,0:T(8,128)S(1)}, f32[2,64,64]{2,1,0:T(8,128)}, u32[]{:S(2)}) copy-start(f32[2,64,64]{2,1,0:T(8,128)} %get-tuple-element.58) | copy-start | bytes 98308
  181.5 2.1 copy-start.8
  183.5 4.0 %copy-start.7 = (f32[2,2,64,64,1]{3,2,1,0,4:T(8,128)S(1)}, f32[2,2,64,64,1]{3,2,1,0,4:T(8,128)}, u32[]{:S(2)}) copy-start(f32[2,2,64,64,1]{3,2,1,0,4:T(8,128)} %get-tuple-element.53) | copy-start | bytes 196612
  211.1 4.9 %copy-start.20 = (s32[1024]{0:T(1024)S(1)}, s32[1024]{0:T(1024)}, u32[]{:S(2)}) copy-start(s32[1024]{0:T(1024)} %copy-done.19) | copy-start | bytes 12292
  211.1 101.6 %all-to-all-start.1 = ((f32[8,2,128,512]{2,3,1,0:T(8,128)}), f32[8,2,128,512]{2,3,1,0:T(8,128)}, u32[]{:S(2)}, u32[]{:S(2)}) async-start(f32[8,2,128,512]{2,3,1,0:T(8,128)} %copy.92), calls=%async_computation.1 | async-start | bytes 8388608 | tf_op jit(solution)/shard_map/all_to_all | solution.py:232
  318.1 25.7 %slice-start = ((s8[8388608]{0:T(1024)(128)(4,1)}), s8[4194304]{0:T(1024)(128)(4,1)S(1)}, s32[]{:S(2)}) async-start(s8[8388608]{0:T(1024)(128)(4,1)} %bitcast.264), calls=%async_computation.2 | async-start | bytes 8388608
  318.1 25.7 %slice-start.1 = ((s8[8388608]{0:T(1024)(128)(4,1)}), s8[4194304]{0:T(1024)(128)(4,1)S(1)}, s32[]{:S(2)}) async-start(s8[8388608]{0:T(1024)(128)(4,1)} %bitcast.264), calls=%async_computation.3 | async-start | bytes 8388608
  318.1 25.7 %copy-start = (f32[1,2,1024,1024]{2,3,0,1:T(8,128)S(1)}, f32[1,2,1024,1024]{2,3,0,1:T(8,128)}, u32[]{:S(2)}) copy-start(f32[1,2,1024,1024]{2,3,0,1:T(8,128)} %get-tuple-element.45) | copy-start | bytes 25165828
  318.1 25.7 %copy-start.1 = (f32[2,8,128,512]{3,2,1,0:T(8,128)S(1)}, f32[2,8,128,512]{3,2,1,0:T(8,128)}, u32[]{:S(2)}) copy-start(f32[2,8,128,512]{3,2,1,0:T(8,128)} %copy.93) | copy-start | bytes 12582916
  325.3 18.5 %collective-permute-start = (f32[2,256,512]{2,1,0:T(8,128)S(1)}, f32[2,256,512]{2,1,0:T(8,128)S(1)}, u32[]{:S(2)}, u32[]{:S(2)}) collective-permute-start(f32[2,256,512]{2,1,0:T(8,128)S(1)} %fusion.59), channel_id=1, source_target_pairs={{0,8},{8,16},{16,24},{24,32},{32,40},{40,48},{48,56},{56,64},{64,7... | collective-permute-start | bytes 3145736 | tf_op jit(solution)/shard_map/ppermute | solution.py:20
  347.4 18.2 %collective-permute-start.1 = (f32[2,256,512]{2,1,0:T(8,128)S(1)}, f32[2,256,512]{2,1,0:T(8,128)S(1)}, u32[]{:S(2)}, u32[]{:S(2)}) collective-permute-start(f32[2,256,512]{2,1,0:T(8,128)S(1)} %fusion.69), channel_id=1, source_target_pairs={{0,8},{8,16},{16,24},{24,32},{32,40},{40,48},{48,56},{56,64},{64,7... | collective-permute-start | bytes 3145736 | tf_op jit(solution)/shard_map/ppermute | solution.py:20
  365.8 18.2 %collective-permute-start.2 = (f32[2,256,512]{2,1,0:T(8,128)S(1)}, f32[2,256,512]{2,1,0:T(8,128)S(1)}, u32[]{:S(2)}, u32[]{:S(2)}) collective-permute-start(f32[2,256,512]{2,1,0:T(8,128)S(1)} %add.648), channel_id=1, source_target_pairs={{0,8},{8,16},{16,24},{24,32},{32,40},{40,48},{48,56},{56,64},{64,7... | collective-permute-start | bytes 3145736 | tf_op jit(solution)/shard_map/ppermute | solution.py:20
